TPU v7x, 32 devices: a whole 2x2x4 slice. The times are simulated.
32 devices in a mesh: row: 8 (over y, x, core), col: 4 (over z).
Axes of the slice: x: 2, y: 2, z: 4, core: 2. Of those that a mesh axis runs over, the one named last changes fastest.
Arguments:
- features: bfloat16 [65536, 256], P(('row', 'col')), may hold values from -6 to 6
- w_self: bfloat16 [256, 256], replicated, may hold values from -0.375 to 0.375
- w_neigh: bfloat16 [256, 256], replicated, may hold values from -1.5 to 1.5
- bias: float32 [256], replicated, may hold values from -3 to 3
- hub_ids: int32 [6], replicated, may hold values from 0 to 7
- hub_adj: bfloat16 [32, 6, 2048, 256], P(('row', 'col')), may hold values from 0 to 2, as said below
- send_tile: int32 [32, 4, 2], P(('row', 'col')), may hold values from 0 to 15
- recv_count: int32 [32, 4], P(('row', 'col')), may hold values from 0 to 2, as said below
- recv_dst: int32 [32, 4, 2], P(('row', 'col')), may hold values from 0 to 15
- recv_adj: bfloat16 [32, 4, 2, 128, 128], P(('row', 'col')), may hold values from 0 to 2, as said below
- cotangent: bfloat16 [65536, 256], P(('row', 'col')), may hold values from -6 to 6
Outputs:
- output: bfloat16 [65536, 256], P(('row', 'col'))
- feature_grad: bfloat16 [65536, 256], P(('row', 'col'))
Inputs may be any that keep to these rules, and one draw needn't show every extreme that they name: `recv_count`: every device uses all 2 slots from at least one device of its row group. `hub_adj`: nonnegative edge weights. `recv_adj`: nonnegative edge weights.
All inputs are finite; a program needn't handle non-finite values.
Results may differ from a plain program's by a relative error of at most 0.0055.
Values may be sent and summed in bfloat16 or wider, within the bound.
No kernel may reach another device: no remote copies, remote signals or barrier semaphores. Data moves between devices by JAX's collectives and lax.ppermute only.
A program may use at most 64 MiB of HBM per device.

v0:
```python
import jax
import jax.numpy as jnp
from jax import lax
from jax.sharding import PartitionSpec as P


def shards(
    features,
    w_self,
    w_neigh,
    bias,
    hub_ids,
    hub_adj,
    send_tile,
    recv_count,
    recv_dst,
    recv_adj,
    cotangent,
):
    f32 = jnp.float32
    bf16 = jnp.bfloat16
    nodes, width = features.shape
    sections = hub_ids.shape[0]
    hub_rows = hub_adj.shape[3]
    peers, slots, tile = (recv_adj.shape[1], recv_adj.shape[2], recv_adj.shape[3])
    total = peers * slots
    count_tiles = nodes // tile
    row_pos = lax.axis_index("row")
    adjacency = hub_adj[0]
    own_hub = features[:hub_rows]
    every_hub = lax.all_gather(own_hub, "row", axis=0, tiled=True)
    hub_sum = jnp.zeros((nodes, width), f32)
    for section in range(sections):
        owner = hub_ids[section]
        block = lax.dynamic_slice_in_dim(every_hub, owner * hub_rows, hub_rows, 0)
        hub_sum = hub_sum + jnp.dot(adjacency[section], block, preferred_element_type=f32)
    offered = send_tile[0].reshape(total)
    outgoing = features.reshape(count_tiles, tile, width)[offered].reshape(
        peers, slots, tile, width
    )
    incoming = lax.all_to_all(outgoing, "col", split_axis=0, concat_axis=0, tiled=True)
    live = (
        (jnp.arange(slots, dtype=jnp.int32)[None, :] < recv_count[0][:, None])
        .astype(f32)
        .reshape(total)
    )
    landing = recv_dst[0].reshape(total)
    select = (landing[:, None] == jnp.arange(count_tiles, dtype=jnp.int32)[None, :]).astype(
        f32
    ) * live[:, None]
    weights = recv_adj[0].reshape(total, tile, tile)
    contrib = jnp.einsum(
        "sij,sjd->sid", weights, incoming.reshape(total, tile, width), preferred_element_type=f32
    )
    tile_sum = jnp.einsum("sn,sid->nid", select, contrib, precision=lax.Precision.HIGHEST).reshape(
        nodes, width
    )
    row_weight = jnp.sum(weights.astype(f32), axis=2)
    tile_deg = jnp.einsum("sn,si->ni", select, row_weight, precision=lax.Precision.HIGHEST).reshape(
        nodes
    )
    degree = 1.0 + jnp.sum(adjacency.astype(f32), axis=(0, 2)) + tile_deg
    agg = ((tile_sum + hub_sum) / degree[:, None]).astype(bf16)
    pre = (
        jnp.dot(features, w_self, preferred_element_type=f32)
        + jnp.dot(agg, w_neigh, preferred_element_type=f32)
        + bias
    )
    sig = jax.nn.sigmoid(pre)
    output = (pre * sig).astype(bf16)
    grad = (cotangent.astype(f32) * sig * (1.0 + pre * (1.0 - sig))).astype(bf16)
    contract = (((1,), (1,)), ((), ()))
    self_grad = lax.dot_general(grad, w_self, contract, preferred_element_type=f32)
    agg_grad = (
        lax.dot_general(grad, w_neigh, contract, preferred_element_type=f32) / degree[:, None]
    ).astype(bf16)
    hub_back = jnp.zeros((hub_rows, width), f32)
    for section in range(sections):
        partial_grad = lax.dot_general(
            adjacency[section], agg_grad, (((0,), (0,)), ((), ())), preferred_element_type=f32
        )
        summed_section = lax.psum(partial_grad, "row")
        hub_back = hub_back + jnp.where(row_pos == hub_ids[section], summed_section, 0.0)
    dest_rows = agg_grad.reshape(count_tiles, tile, width)[landing]
    slot_grad = (
        jnp.einsum("sij,sid->sjd", weights, dest_rows, preferred_element_type=f32)
        * live[:, None, None]
    ).astype(bf16)
    returned = lax.all_to_all(
        slot_grad.reshape(peers, slots, tile, width), "col", split_axis=0, concat_axis=0, tiled=True
    )
    owned = (offered[:, None] == jnp.arange(count_tiles, dtype=jnp.int32)[None, :]).astype(f32)
    tile_back = jnp.einsum(
        "sn,sid->nid",
        owned,
        returned.reshape(total, tile, width).astype(f32),
        precision=lax.Precision.HIGHEST,
    ).reshape(nodes, width)
    hub_padded = jnp.concatenate([hub_back, jnp.zeros((nodes - hub_rows, width), f32)], axis=0)
    feature_grad = (self_grad + tile_back + hub_padded).astype(bf16)
    return (output, feature_grad)


def solution(mesh):
    placed = (
        P(("row", "col"), None),
        P(),
        P(),
        P(),
        P(),
        P(("row", "col"), None, None, None),
        P(("row", "col"), None, None),
        P(("row", "col"), None),
        P(("row", "col"), None, None),
        P(("row", "col"), None, None, None, None),
        P(("row", "col"), None),
    )
    return jax.shard_map(
        shards,
        mesh=mesh,
        in_specs=placed,
        out_specs=(P(("row", "col"), None), P(("row", "col"), None)),
        check_vma=False,
    )
```

profile of v0, /device:TPU:0, one launch (start us, length us, event | category | flops | bytes accessed | tf_op | source)
XLA Modules:
  0.0 147.1 jit_solution(16033478632111042276)
XLA Ops:
  7.2 0.0 all-gather.2.cloned.1.call-start
  7.2 1.6 %slice.57 = bf16[256,256]{1,0:T(8,128)(2,1)} slice(bf16[2048,256]{1,0:T(8,128)(2,1)} %param.11), slice={[0:256], [0:256]} | slice | bytes 262144 | tf_op jit(solution)/shard_map/slice | solution.py:30
  8.8 0.0 all-gather.2.cloned.1.call-update
  8.8 0.8 copy.25
  9.6 0.1 reshape_squeeze.11
  9.7 0.8 copy.26
  10.4 0.1 reshape_squeeze.9
  10.6 2.6 %gather_fusion = bf16[8,128,256]{2,1,0:T(8,128)(2,1)} fusion(bf16[16,128,256]{2,1,0:T(8,128)(2,1)} %bitcast.113, s32[1024]{0:T(1024)S(1)} %pad_clamp_fusion.1), kind=kCustom, calls=%fused_computation | custom fusion | bytes 1048608 | tf_op jit(solution)/shard_map/gather | solution.py:38
  13.1 6.3 %all-to-all-start = ((bf16[4,2,128,256]{3,2,1,0:T(8,128)(2,1)}), bf16[4,2,128,256]{3,2,1,0:T(8,128)(2,1)S(1)}, u32[]{:S(2)}, u32[]{:S(2)}) async-start(bf16[4,2,128,256]{3,2,1,0:T(8,128)(2,1)} %bitcast.4), calls=%async_computation | async-start | bytes 1048576 | tf_op jit(solution)/shard_map/all_to_all | solution.py:41
  19.5 0.1 fusion.58
  19.6 3.9 %convert_reduce_fusion = f32[2048]{0:T(1024)S(1)} fusion(bf16[1,6,2048,256]{3,2,1,0:T(8,128)(2,1)} %param.16), kind=kLoop, calls=%fused_computation.2 | loop fusion | flops 6289408 | bytes 6299648 | tf_op jit(solution)/shard_map/reduce_sum | solution.py:62
  23.5 0.7 fusion.70
  27.9 0.1 eq.48
  28.0 0.1 reshape.153
  28.1 0.1 convert_reduce_fusion.1
  28.2 0.9 fusion.9
  29.1 1.8 %fusion.75 = f32[2048,256]{1,0:T(8,128)} fusion(bf16[2048,256]{1,0:T(8,128)(2,1)S(1)} %copy-done.1, bf16[256,256]{1,0:T(8,128)(2,1)S(1)} %copy-done.4), kind=kOutput, calls=%fused_computation.98 | convolution fusion | flops 268435456 | bytes 3276800 | tf_op jit(solution)/shard_map/dot_general | solution.py:65
  30.9 3.1 %all-to-all-done = bf16[4,2,128,256]{3,2,1,0:T(8,128)(2,1)S(1)} async-done(((bf16[4,2,128,256]{3,2,1,0:T(8,128)(2,1)}), bf16[4,2,128,256]{3,2,1,0:T(8,128)(2,1)S(1)}, u32[]{:S(2)}, u32[]{:S(2)}) %all-to-all-start) | async-done | bytes 524320 | tf_op jit(solution)/shard_map/all_to_all | solution.py:41
  34.0 0.3 fusion.76
  34.3 0.5 copy.39
  34.8 1.9 %fusion.24 = f32[16,128,256]{2,0,1:T(8,128)S(1)} fusion(f32[8,256,128]{1,0,2:T(8,128)S(1)} %copy.39, f32[8]{0:T(128)S(1)} %reshape.153, s32[8]{0:T(128)S(1)} %eq.48), kind=kOutput, calls=%fused_computation.45 | convolution fusion | flops 50331904 | bytes 3145792 | tf_op jit(solution)/shard_map/sn,sid->nid/dot_general | solution.py:55
  36.7 2.5 %copy.27 = f32[16,128,256]{2,1,0:T(8,128)} copy(f32[16,128,256]{2,0,1:T(8,128)S(1)} %fusion.24) | data formatting | bytes 4194304 | tf_op jit(solution)/shard_map/sn,sid->nid/dot_general | solution.py:55
  39.3 1.7 %fusion.22 = f32[256,2048]{0,1:T(8,128)S(1)} fusion(bf16[1,6,2048,256]{3,2,1,0:T(8,128)(2,1)} %param.16, bf16[2048,256]{1,0:T(8,128)(2,1)} %all-gather.2.cloned.1.call-done, s32[]{:T(128)S(6)} %select_n.77), kind=kOutput, calls=%fused_computation.43 | convolution fusion | flops 268435456 | bytes 3276804 | tf_op jit(solution)/shard_map/dot_general | solution.py:36
  41.1 1.7 %convolution_add_fusion.4 = f32[256,2048]{0,1:T(8,128)S(1)} fusion(f32[256,2048]{0,1:T(8,128)S(1)} %fusion.22, bf16[1,6,2048,256]{3,2,1,0:T(8,128)(2,1)} %param.16, bf16[2048,256]{1,0:T(8,128)(2,1)S(1)} %copy-done.6, s32[]{:T(128)S(6)} %select_n.78), kind=kOutput, calls=%fused_computation.9 | convolution fusion | flops 268959744 | bytes 5373956 | tf_op jit(solution)/shard_map/dot_general | solution.py:36
  42.7 1.7 %convolution_add_fusion.3 = f32[256,2048]{0,1:T(8,128)S(1)} fusion(f32[256,2048]{0,1:T(8,128)S(1)} %convolution_add_fusion.4, bf16[1,6,2048,256]{3,2,1,0:T(8,128)(2,1)} %param.16, bf16[2048,256]{1,0:T(8,128)(2,1)S(1)} %copy-done.6, s32[]{:T(128)S(6)} %select_n.79), kind=kOutput, calls=%fused_computation.8 | convolution fusion | flops 268959744 | bytes 5373956 | tf_op jit(solution)/shard_map/dot_general | solution.py:36
  44.4 1.7 %convolution_add_fusion.2 = f32[256,2048]{0,1:T(8,128)S(1)} fusion(f32[256,2048]{0,1:T(8,128)S(1)} %convolution_add_fusion.3, bf16[1,6,2048,256]{3,2,1,0:T(8,128)(2,1)} %param.16, bf16[2048,256]{1,0:T(8,128)(2,1)S(1)} %copy-done.6, s32[]{:T(128)S(6)} %select_n.80), kind=kOutput, calls=%fused_computation.7 | convolution fusion | flops 268959744 | bytes 5373956 | tf_op jit(solution)/shard_map/dot_general | solution.py:36
  46.1 3.1 %convolution_add_fusion.1 = f32[256,2048]{0,1:T(8,128)} fusion(f32[256,2048]{0,1:T(8,128)S(1)} %convolution_add_fusion.2, bf16[1,6,2048,256]{3,2,1,0:T(8,128)(2,1)} %param.16, bf16[2048,256]{1,0:T(8,128)(2,1)S(1)} %copy-done.6, s32[]{:T(128)S(6)} %select_n.81), kind=kOutput, calls=%fused_computation.6 | convolution fusion | flops 268959744 | bytes 5373956 | tf_op jit(solution)/shard_map/dot_general | solution.py:36
  49.3 5.3 %multiply_convert_fusion = (bf16[2048,256]{1,0:T(8,128)(2,1)S(1)}, bf16[2048,256]{1,0:T(8,128)(2,1)}) fusion(bf16[2048,256]{1,0:T(8,128)(2,1)} %param.21, f32[256]{0:T(256)S(1)} %copy-done.9, f32[2048,256]{1,0:T(8,128)S(1)} %copy-done.3, bf16[256,256]{1,0:T(8,128)(2,1)S(1)} %copy-done, f32[2048,256]{1,0:T(8,128)} %bitcast.117, ...), kind=kOutput, calls=%fused_computation.19 | convolution fusion | flops 546308096 | bytes 10757124 | tf_op jit(solution)/shard_map/dot_general | solution.py:66
  54.6 1.2 fusion.5
  55.8 2.5 %convolution_bitcast_fusion = f32[256,256]{1,0:T(8,128)} fusion(bf16[2048,256]{1,0:T(8,128)(2,1)S(1)} %fusion.5, bf16[1,6,2048,256]{3,2,1,0:T(8,128)(2,1)} %param.16), kind=kOutput, calls=%fused_computation.24 | convolution fusion | flops 268435456 | bytes 2359296 | tf_op jit(solution)/shard_map/dot_general | solution.py:79
  58.2 2.5 %convolution_bitcast_fusion.1 = f32[256,256]{1,0:T(8,128)} fusion(bf16[2048,256]{1,0:T(8,128)(2,1)S(1)} %fusion.5, bf16[1,6,2048,256]{3,2,1,0:T(8,128)(2,1)} %param.16), kind=kOutput, calls=%fused_computation.25 | convolution fusion | flops 268435456 | bytes 2359296 | tf_op jit(solution)/shard_map/dot_general | solution.py:79
  60.7 2.5 %convolution_bitcast_fusion.2 = f32[256,256]{1,0:T(8,128)} fusion(bf16[2048,256]{1,0:T(8,128)(2,1)S(1)} %fusion.5, bf16[1,6,2048,256]{3,2,1,0:T(8,128)(2,1)} %param.16), kind=kOutput, calls=%fused_computation.26 | convolution fusion | flops 268435456 | bytes 2359296 | tf_op jit(solution)/shard_map/dot_general | solution.py:79
  63.2 2.5 %convolution_bitcast_fusion.3 = f32[256,256]{1,0:T(8,128)} fusion(bf16[2048,256]{1,0:T(8,128)(2,1)S(1)} %fusion.5, bf16[1,6,2048,256]{3,2,1,0:T(8,128)(2,1)} %param.16), kind=kOutput, calls=%fused_computation.27 | convolution fusion | flops 268435456 | bytes 2359296 | tf_op jit(solution)/shard_map/dot_general | solution.py:79
  65.7 0.6 gather_fusion.1
  66.2 1.1 fusion.8
  67.4 3.5 %all-to-all-start.1 = ((bf16[4,2,128,256]{2,3,1,0:T(8,128)(2,1)}), bf16[4,2,128,256]{2,3,1,0:T(8,128)(2,1)S(1)}, u32[]{:S(2)}, u32[]{:S(2)}) async-start(bf16[4,2,128,256]{2,3,1,0:T(8,128)(2,1)} %bitcast.28), calls=%async_computation.1 | async-start | bytes 1048576 | tf_op jit(solution)/shard_map/all_to_all | solution.py:89
  70.9 0.2 all-reduce.4.cloned.1.call-start
  71.1 2.5 %convolution_bitcast_fusion.4 = f32[256,256]{1,0:T(8,128)} fusion(bf16[2048,256]{1,0:T(8,128)(2,1)S(1)} %fusion.5, bf16[1,6,2048,256]{3,2,1,0:T(8,128)(2,1)} %param.16), kind=kOutput, calls=%fused_computation.28 | convolution fusion | flops 268435456 | bytes 2359296 | tf_op jit(solution)/shard_map/dot_general | solution.py:79
  73.6 2.5 %convolution_bitcast_fusion.5 = f32[256,256]{1,0:T(8,128)} fusion(bf16[2048,256]{1,0:T(8,128)(2,1)S(1)} %fusion.5, bf16[1,6,2048,256]{3,2,1,0:T(8,128)(2,1)} %param.16), kind=kOutput, calls=%fused_computation.29 | convolution fusion | flops 268435456 | bytes 2359296 | tf_op jit(solution)/shard_map/dot_general | solution.py:79
  76.0 0.0 all-reduce.4.cloned.1.call-update
  79.8 0.1 eq.52
  79.9 5.0 %all-to-all-done.1 = bf16[4,2,128,256]{2,3,1,0:T(8,128)(2,1)S(1)} async-done(((bf16[4,2,128,256]{2,3,1,0:T(8,128)(2,1)}), bf16[4,2,128,256]{2,3,1,0:T(8,128)(2,1)S(1)}, u32[]{:S(2)}, u32[]{:S(2)}) %all-to-all-start.1) | async-done | bytes 524320 | tf_op jit(solution)/shard_map/all_to_all | solution.py:89
  84.9 0.4 copy.47
  85.3 0.5 fusion.49
  85.8 1.2 copy.32
  87.1 50.6 %all-reduce.4.cloned.1.call-done = (f32[256,256]{1,0:T(8,128)}, f32[256,256]{1,0:T(8,128)}, f32[256,256]{1,0:T(8,128)}, f32[256,256]{1,0:T(8,128)}, f32[256,256]{1,0:T(8,128)}, /*index=5*/f32[256,256]{1,0:T(8,128)}) async-done(((f32[256,256]{1,0:T(8,128)}, f32[256,256]{1,0:T(8,128)}, f32[256,256]{1,0:T(8,128)}, f32[256,256]{1,0:T(8,128)}, f32[256,256]{1,0:T(8,128)}, /*index=5*/f32[256,256]{1,0:T(8,128)}), ...) | async-done | bytes 1572880 | tf_op jit(solution)/shard_map/psum | solution.py:82
  137.6 1.1 select_add_fusion
  138.8 1.4 fusion.4
  (24 shorter events, 0.1 us)
Async XLA Ops:
  7.2 42.1 %copy-start = (bf16[256,256]{1,0:T(8,128)(2,1)S(1)}, bf16[256,256]{1,0:T(8,128)(2,1)}, u32[]{:S(2)}) copy-start(bf16[256,256]{1,0:T(8,128)(2,1)} %param.13) | copy-start | bytes 393220
  7.2 12.3 %copy-start.8 = (s32[1,4]{1,0:T(1,128)S(1)}, s32[1,4]{1,0:T(1,128)}, u32[]{:S(2)}) copy-start(s32[1,4]{1,0:T(1,128)} %param.18) | copy-start | bytes 52
  7.2 32.1 %all-gather.2.cloned.1.call-start = ((), (), s32[]{:S(2)}) async-start(), calls=%async_computation.2 | async-start | bytes 1179648 | tf_op jit(solution)/shard_map/all_gather | solution.py:31
  13.1 20.8 %all-to-all-start = ((bf16[4,2,128,256]{3,2,1,0:T(8,128)(2,1)}), bf16[4,2,128,256]{3,2,1,0:T(8,128)(2,1)S(1)}, u32[]{:S(2)}, u32[]{:S(2)}) async-start(bf16[4,2,128,256]{3,2,1,0:T(8,128)(2,1)} %bitcast.4), calls=%async_computation | async-start | bytes 1048576 | tf_op jit(solution)/shard_map/all_to_all | solution.py:41
  19.6 3.9 %copy-start.7 = (s32[6]{0:T(128)S(1)}, s32[6]{0:T(128)}, u32[]{:S(2)}) copy-start(s32[6]{0:T(128)} %param.15) | copy-start | bytes 76
  19.6 8.5 %copy-start.2 = (bf16[1,4,2,128,128]{4,3,2,1,0:T(8,128)(2,1)S(1)}, bf16[1,4,2,128,128]{4,3,2,1,0:T(8,128)(2,1)}, u32[]{:S(2)}) copy-start(bf16[1,4,2,128,128]{4,3,2,1,0:T(8,128)(2,1)} %param.20) | copy-start | bytes 786436
  19.6 9.5 %copy-start.1 = (bf16[2048,256]{1,0:T(8,128)(2,1)S(1)}, bf16[2048,256]{1,0:T(8,128)(2,1)}, u32[]{:S(2)}) copy-start(bf16[2048,256]{1,0:T(8,128)(2,1)} %param.11) | copy-start | bytes 3145732
  19.6 9.5 %copy-start.4 = (bf16[256,256]{1,0:T(8,128)(2,1)S(1)}, bf16[256,256]{1,0:T(8,128)(2,1)}, u32[]{:S(2)}) copy-start(bf16[256,256]{1,0:T(8,128)(2,1)} %param.12) | copy-start | bytes 393220
  39.3 1.8 %copy-start.6 = (bf16[2048,256]{1,0:T(8,128)(2,1)S(1)}, bf16[2048,256]{1,0:T(8,128)(2,1)}, u32[]{:S(2)}) copy-start(bf16[2048,256]{1,0:T(8,128)(2,1)} %all-gather.2.cloned.1.call-done) | copy-start | bytes 3145732
  46.1 3.2 %copy-start.3 = (f32[2048,256]{1,0:T(8,128)S(1)}, f32[2048,256]{1,0:T(8,128)}, u32[]{:S(2)}) copy-start(f32[2048,256]{1,0:T(8,128)} %fusion.75) | copy-start | bytes 6291460
  46.1 3.2 %copy-start.9 = (f32[256]{0:T(256)S(1)}, f32[256]{0:T(256)}, u32[]{:S(2)}) copy-start(f32[256]{0:T(256)} %param.14) | copy-start | bytes 3076
  67.4 17.5 %all-to-all-start.1 = ((bf16[4,2,128,256]{2,3,1,0:T(8,128)(2,1)}), bf16[4,2,128,256]{2,3,1,0:T(8,128)(2,1)S(1)}, u32[]{:S(2)}, u32[]{:S(2)}) async-start(bf16[4,2,128,256]{2,3,1,0:T(8,128)(2,1)} %bitcast.28), calls=%async_computation.1 | async-start | bytes 1048576 | tf_op jit(solution)/shard_map/all_to_all | solution.py:89
  70.9 66.8 %all-reduce.4.cloned.1.call-start = ((), (), s32[]{:S(2)}) async-start(), calls=%async_computation.3 | async-start | bytes 3145728 | tf_op jit(solution)/shard_map/psum | solution.py:82
  85.8 52.9 %copy-start.5 = (bf16[256,256]{1,0:T(8,128)(2,1)S(1)}, bf16[256,256]{1,0:T(8,128)(2,1)}, u32[]{:S(2)}) copy-start(bf16[256,256]{1,0:T(8,128)(2,1)} %param.12) | copy-start | bytes 393220
Sparse Core Ops, SparseCore 0:
  10.5 26.0 all-gather.1
  76.2 61.3 all-reduce.3
where the time goes:
time: 148 us; the launch traced here: 147 us
  waiting for transfers between devices  58.7 us (40%)
  matrix products  39.3 us (27%)
  between operations  21.7 us (15%)
  local copies, waits for them, and re-layouts  12.1 us (8%)
  starting transfers between devices  10.1 us (7%)
  other arithmetic  5.25 us (4%)
    psum x1, waiting for transfers between devices, shards(): summed_section = lax.psum(partial_grad, 'row')  50.6 us
    dot_general x6, matrix products, shards(): lax.dot_general(adjacency[section], agg_grad, (((0,), (0,)), ((), ())), p...  14.8 us
    dot_general x5, matrix products, shards(): jnp.dot(adjacency[section], block, preferred_element_type=f32)  9.91 us
    all_to_all x1, starting transfers between devices, shards(): lax.all_to_all(outgoing, 'col', split_axis=0, concat_axis=0, tiled=True)  6.35 us
    dot_general x1, matrix products, shards(): jnp.dot(agg, w_neigh, preferred_element_type=f32)  5.32 us
    all_to_all x1, waiting for transfers between devices, shards(): lax.all_to_all(slot_grad.reshape(peers, slots, tile, width), 'col', split...  4.98 us
    reduce_sum x1, other arithmetic, shards(): degree = 1.0 + jnp.sum(adjacency.astype(f32), axis=(0, 2)) + tile_deg  3.87 us
    all_to_all x1, starting transfers between devices, shards(): lax.all_to_all(slot_grad.reshape(peers, slots, tile, width), 'col', split...  3.47 us
  transfers between devices with their start and end apart: 4, of which 3 were waited for; matrix products, arithmetic and copies ran while one was open for 17% of the time, Pallas kernels for 0%

commit v1 on v0

v1 whole, which is shorter than its diff:
```python
import functools

import jax
import jax.numpy as jnp
from jax import lax
from jax.experimental import pallas as pl
from jax.experimental.pallas import tpu as pltpu
from jax.sharding import PartitionSpec as P

F32 = jnp.float32
BF16 = jnp.bfloat16
BY_LAST = (((1,), (1,)), ((), ()))
BY_FIRST = (((0,), (0,)), ((), ()))
SMEM = pl.BlockSpec(memory_space=pltpu.SMEM)
ANY = pl.BlockSpec(memory_space=pl.ANY)
HBM = pl.BlockSpec(memory_space=pltpu.HBM)
VMEM = pl.BlockSpec(memory_space=pltpu.VMEM)


def rows_at(index, size):
    return pl.ds(pl.multiple_of(index * size, size), size)


def pick_kernel(send, feats, hub, *rest, tile):
    outs, sems = rest[:-1], rest[-1]
    col = lax.axis_index("col")
    slots = outs[0].shape[0]
    copies = []
    for d, out in enumerate(outs):
        for k in range(slots):
            at = rows_at(send[k, col ^ d], tile)
            copies.append(pltpu.make_async_copy(feats.at[at], out.at[k], sems.at[d * slots + k]))
    copies.append(pltpu.make_async_copy(feats.at[pl.ds(0, hub.shape[0])], hub, sems.at[len(copies)]))
    for copy in copies:
        copy.start()
    for copy in copies:
        copy.wait()


def tile_order(count, dst, order, place, *, peers, slots, tiles):
    landed = jnp.int32(0)
    for p in range(peers):
        for k in range(slots):
            landed = landed | jnp.where(k < count[0, p], jnp.int32(1) << dst[k, p], 0)
    front, back = jnp.int32(0), jnp.int32(tiles - 1)
    for t in range(tiles):
        bit = (landed >> t) & 1
        at = jnp.where(bit == 1, front, back)
        order[at] = jnp.int32(t)
        place[t] = at
        front = front + bit
        back = back - (1 - bit)


def load_kernel(adj, kept, deg, sems, *, chunk):
    sections, nodes, _ = kept.shape
    copies = []
    for i, start in enumerate(range(0, nodes, chunk)):
        at = pl.ds(start, chunk)
        copies.append(pltpu.make_async_copy(adj.at[:, at, :], kept.at[:, at, :], sems.at[i]))
        copies[-1].start()
    for i, copy in enumerate(copies):
        copy.wait()
        at = pl.ds(i * chunk, chunk)
        wide = jnp.concatenate([kept[s, at, :] for s in range(sections)], axis=1).astype(F32)
        lanes = wide[:, 0:128]
        for c in range(128, wide.shape[1], 128):
            lanes = lanes + wide[:, c : c + 128]
        deg[at, :] = jnp.broadcast_to(1.0 + jnp.sum(lanes, axis=1, keepdims=True), (chunk, 128))


def hub_forward_kernel(hub_ids, adj, same, other, raw, blocks, *, chunk):
    row = lax.axis_index("row")
    sections, nodes, hub_rows = adj.shape
    for s in range(sections):
        away = hub_ids[s] ^ row
        at = pl.ds(s * hub_rows, hub_rows)

        @pl.when(away & 1 == 0)
        def _(away=away, at=at):
            blocks[at, :] = same[away >> 1]

        @pl.when(away & 1 == 1)
        def _(away=away, at=at):
            blocks[at, :] = other[away >> 1]

    for start in range(0, nodes, chunk):
        at = pl.ds(start, chunk)
        weights = jnp.concatenate([adj[s, at, :] for s in range(sections)], axis=1)
        raw[at, :] = jnp.dot(weights, blocks[...], preferred_element_type=F32)


def dense(raw, deg, feats, cot, w_self, w_neigh, bias):
    inverse = 1.0 / deg
    inverse = jnp.concatenate([inverse] * (raw.shape[1] // inverse.shape[1]), axis=1)
    agg = (raw * inverse).astype(BF16)
    pre = (
        jnp.dot(feats, w_self[...], preferred_element_type=F32)
        + jnp.dot(agg, w_neigh[...], preferred_element_type=F32)
        + bias[...]
    )
    sig = 0.5 * jnp.tanh(0.5 * pre) + 0.5
    out = (pre * sig).astype(BF16)
    grad = (cot.astype(F32) * sig * (1.0 + pre * (1.0 - sig))).astype(BF16)
    agg_grad = (lax.dot_general(grad, w_neigh[...], BY_LAST, preferred_element_type=F32) * inverse).astype(BF16)
    return out, grad, agg_grad


def landed_kernel(count, dst, raw_in, deg_in, feats, cot, adj, w_self, w_neigh, bias, *rest, peers, slots, tile, group):
    inc = rest[:peers]
    out, grad, agg_grad = rest[peers : peers + 3]
    back = rest[peers + 3 : 2 * peers + 3]
    raw, deg, order, place = rest[2 * peers + 3 :]
    col = lax.axis_index("col")
    tile_order(count, dst, order, place, peers=peers, slots=slots, tiles=raw_in.shape[0] // tile)
    first = raw.shape[0] // tile
    for i in range(first):
        at = rows_at(order[i], tile)
        raw[pl.ds(i * tile, tile), :] = raw_in[at, :]
        deg[pl.ds(i * tile, tile), :] = deg_in[at, :]
    for d in range(peers):
        p = col ^ d
        for k in range(slots):

            @pl.when(k < count[0, p])
            def _(d=d, k=k, p=p):
                at = rows_at(place[dst[k, p]], tile)
                weights = adj[p, k]
                raw[at, :] += jnp.dot(weights, inc[d][k], preferred_element_type=F32)
                deg[at, :] += jnp.sum(weights.astype(F32), axis=1, keepdims=True)

    for start in range(0, first, group):
        here = pl.ds(start * tile, group * tile)
        there = [rows_at(order[i], tile) for i in range(start, start + group)]
        o, g, a = dense(
            raw[here, :],
            deg[here, :],
            jnp.concatenate([feats[at, :] for at in there]),
            jnp.concatenate([cot[at, :] for at in there]),
            w_self,
            w_neigh,
            bias,
        )
        out[here, :] = o
        grad[here, :] = g
        agg_grad[here, :] = a
    for d in range(peers):
        p = col ^ d
        for k in range(slots):
            alive = k < count[0, p]
            at = rows_at(jnp.where(alive, place[dst[k, p]], 0), tile)
            part = lax.dot_general(adj[p, k], agg_grad[at, :], BY_FIRST, preferred_element_type=F32)
            back[d][k] = (part * jnp.where(alive, 1.0, 0.0).astype(F32)).astype(BF16)


def others_kernel(
    count, dst, raw, deg, feats, cot, w_self, w_neigh, bias, out, grad, agg_grad, order, place, *, peers, slots, tile, group
):
    tiles = raw.shape[0] // tile
    first = tiles - out.shape[0] // tile
    tile_order(count, dst, order, place, peers=peers, slots=slots, tiles=tiles)
    for start in range(first, tiles, group):
        here = pl.ds((start - first) * tile, group * tile)
        there = [rows_at(order[i], tile) for i in range(start, start + group)]
        o, g, a = dense(
            *[jnp.concatenate([x[at, :] for at in there]) for x in (raw, deg, feats, cot)], w_self, w_neigh, bias
        )
        out[here, :] = o
        grad[here, :] = g
        agg_grad[here, :] = a


def hub_backward_kernel(count, dst, hub_ids, adj, *rest, peers, slots, tile):
    pieces, (even, odd, agg_grad, order, place) = rest[:-5], rest[-5:]
    row = lax.axis_index("row")
    sections = adj.shape[0]
    tiles = agg_grad.shape[0] // tile
    tile_order(count, dst, order, place, peers=peers, slots=slots, tiles=tiles)
    i = 0
    for piece in pieces:
        for j in range(piece.shape[0] // tile):
            agg_grad[rows_at(order[i], tile), :] = piece[pl.ds(j * tile, tile), :]
            i += 1
    turned = agg_grad[...].T
    owner = [hub_ids[s] ^ row for s in range(sections)]
    for ref in (even, odd):
        ref[...] = jnp.zeros_like(ref)
    parts = [jnp.dot(turned, adj[s], preferred_element_type=F32) for s in range(sections)]
    for s in range(sections):
        total = parts[s]
        for other in range(sections):
            if other != s:
                total = total + parts[other] * jnp.where(owner[other] == owner[s], 1.0, 0.0).astype(F32)

        @pl.when(owner[s] & 1 == 0)
        def _(s=s, total=total):
            even[owner[s] >> 1] = total.astype(BF16)

        @pl.when(owner[s] & 1 == 1)
        def _(s=s, total=total):
            odd[owner[s] >> 1] = total.astype(BF16)


def self_kernel(count, dst, w_self, *rest, peers, slots, tile):
    pieces, (out, self_grad, order, place, sems) = rest[:-5], rest[-5:]
    tiles = self_grad.shape[0] // tile
    tile_order(count, dst, order, place, peers=peers, slots=slots, tiles=tiles)
    copies = []
    i = 0
    for outs, grads in zip(pieces[: len(pieces) // 2], pieces[len(pieces) // 2 :]):
        for j in range(outs.shape[0] // tile):
            copies.append(
                pltpu.make_async_copy(outs.at[pl.ds(j * tile, tile)], out.at[rows_at(order[i], tile)], sems.at[i])
            )
            copies[-1].start()
            i += 1
    i = 0
    for grads in pieces[len(pieces) // 2 :]:
        through = lax.dot_general(grads[...], w_self[...], BY_LAST, preferred_element_type=F32)
        for j in range(grads.shape[0] // tile):
            self_grad[rows_at(order[i], tile), :] = through[j * tile : (j + 1) * tile]
            i += 1
    for copy in copies:
        copy.wait()


def pair_add_kernel(even, came, *outs):
    for e, out in enumerate(outs):
        out[...] = (even[e].astype(F32) + came[e].astype(F32)).astype(BF16)


def final_kernel(send, self_grad, *rest, peers, slots, tile, chunk):
    back, hub, (out, total, done, sems) = rest[:peers], rest[peers:-4], rest[-4:]
    col = lax.axis_index("col")
    total[...] = self_grad[...]
    for d in range(peers):
        for k in range(slots):
            total[rows_at(send[k, col ^ d], tile), :] += back[d][k].astype(F32)
    come = hub[0][...].astype(F32)
    for h in hub[1:]:
        come = come + h[...].astype(F32)
    total[0 : come.shape[1], :] += come.T
    copies = []
    for i, start in enumerate(range(0, total.shape[0], chunk)):
        at = pl.ds(start, chunk)
        done[at, :] = total[at, :].astype(BF16)
        copies.append(pltpu.make_async_copy(done.at[at], out.at[at], sems.at[i]))
        copies[-1].start()
    for copy in copies:
        copy.wait()


def shards(
    features, w_self, w_neigh, bias, hub_ids, hub_adj, send_tile, recv_count, recv_dst, recv_adj, cotangent, *, n_row, n_col
):
    nodes, width = features.shape
    sections, hub_rows = hub_ids.shape[0], hub_adj.shape[3]
    peers, slots, tile = recv_adj.shape[1], recv_adj.shape[2], recv_adj.shape[3]
    out_width = w_self.shape[1]
    tiles = nodes // tile
    first = min(peers * slots, tiles)
    group = 4
    send, count, dst = send_tile.swapaxes(1, 2)[0], recv_count, recv_dst.swapaxes(1, 2)[0]
    adj, weights, bias = hub_adj[0], recv_adj[0], bias.reshape(1, -1)
    params = pltpu.CompilerParams(vmem_limit_bytes=24 * 1024 * 1024)
    shape = jax.ShapeDtypeStruct
    sizes = dict(peers=peers, slots=slots, tile=tile)

    def cost(flops):
        return pl.CostEstimate(flops=flops, transcendentals=0, bytes_accessed=8 * nodes * width)

    def across(x, axis, size, d):
        return lax.ppermute(x, axis, [(i, i ^ d) for i in range(size)])

    order = exchange_order(n_col)
    pair = shape((slots, tile, width), BF16)
    own_hub, *picked = pl.pallas_call(
        functools.partial(pick_kernel, tile=tile),
        in_specs=[SMEM, HBM],
        out_specs=[VMEM] * (peers + 1),
        scratch_shapes=[pltpu.SemaphoreType.DMA((peers * slots + 1,))],
        out_shape=[shape((hub_rows, width), BF16)] + [pair] * peers,
        compiler_params=params,
        name="pick",
    )(pltpu.with_memory_space_constraint(send, pltpu.HBM), pltpu.with_memory_space_constraint(features, pltpu.HBM))
    incoming = [picked[0]] + [None] * (peers - 1)
    for d in order:
        incoming[d] = across(picked[d], "col", n_col, d)
    same = jnp.stack([own_hub] + [across(own_hub, "row", n_row, d) for d in range(2, n_row, 2)])
    other = across(same, "row", n_row, 1)

    adj, deg = pl.pallas_call(
        functools.partial(load_kernel, chunk=nodes // 8),
        in_specs=[HBM],
        out_specs=[VMEM, VMEM],
        scratch_shapes=[pltpu.SemaphoreType.DMA((8,))],
        out_shape=[shape(adj.shape, BF16), shape((nodes, 128), F32)],
        compiler_params=params,
        name="load",
    )(pltpu.with_memory_space_constraint(adj, pltpu.HBM))
    raw = pl.pallas_call(
        functools.partial(hub_forward_kernel, chunk=256),
        in_specs=[SMEM, VMEM, VMEM, VMEM],
        out_specs=VMEM,
        scratch_shapes=[pltpu.VMEM((sections * hub_rows, width), BF16)],
        out_shape=shape((nodes, width), F32),
        compiler_params=params,
        cost_estimate=cost(2 * sections * nodes * hub_rows * width),
        name="hub_forward",
    )(hub_ids, adj, same, other)

    tables = [pltpu.SMEM((tiles,), jnp.int32), pltpu.SMEM((tiles,), jnp.int32)]

    def results(number):
        return [shape((number * tile, n), BF16) for n in (out_width, out_width, width)]

    others = []
    if first < tiles:
        others = pl.pallas_call(
            functools.partial(others_kernel, group=group, **sizes),
            in_specs=[SMEM, SMEM] + [VMEM] * 7,
            out_specs=[VMEM] * 3,
            scratch_shapes=tables,
            out_shape=results(tiles - first),
            compiler_params=params,
            name="others",
        )(count, dst, raw, deg, features, cotangent, w_self, w_neigh, bias)
    landed = pl.pallas_call(
        functools.partial(landed_kernel, group=group, **sizes),
        in_specs=[SMEM, SMEM] + [VMEM] * (8 + peers),
        out_specs=[VMEM] * (3 + peers),
        scratch_shapes=[pltpu.VMEM((first * tile, width), F32), pltpu.VMEM((first * tile, 128), F32)] + tables,
        out_shape=results(first) + [pair] * peers,
        compiler_params=params,
        name="landed",
    )(count, dst, raw, deg, features, cotangent, weights, w_self, w_neigh, bias, *incoming)
    outs, grads, agg_grads = zip(*([landed[:3]] + ([others] if others else [])))
    going = landed[3:]
    returned = [going[0]] + [None] * (peers - 1)
    for d in order:
        returned[d] = across(going[d], "col", n_col, d)

    half = shape((n_row // 2, width, hub_rows), BF16)
    even, odd = pl.pallas_call(
        functools.partial(hub_backward_kernel, **sizes),
        in_specs=[SMEM] * 3 + [VMEM] * (1 + len(agg_grads)),
        out_specs=[VMEM] * 2,
        scratch_shapes=[pltpu.VMEM((nodes, width), BF16)] + tables,
        out_shape=[half, half],
        compiler_params=params,
        cost_estimate=cost(2 * sections * nodes * hub_rows * width),
        name="hub_backward",
    )(count, dst, hub_ids, adj, *agg_grads)
    came = across(odd, "row", n_row, 1)
    output, self_grad = pl.pallas_call(
        functools.partial(self_kernel, **sizes),
        in_specs=[SMEM] * 2 + [VMEM] * (1 + 2 * len(outs)),
        out_specs=[HBM, VMEM],
        scratch_shapes=tables + [pltpu.SemaphoreType.DMA((tiles,))],
        out_shape=[shape((nodes, out_width), BF16), shape((nodes, width), F32)],
        compiler_params=params,
        name="self",
    )(count, dst, w_self, *outs, *grads)
    block = shape((width, hub_rows), BF16)
    sums = pl.pallas_call(
        pair_add_kernel,
        out_shape=[block] * (n_row // 2),
        compiler_params=params,
        name="pair_add",
    )(even, came)
    hubs = [sums[0]] + [across(sums[d // 2], "row", n_row, d) for d in range(2, n_row, 2)]

    feature_grad = pl.pallas_call(
        functools.partial(final_kernel, chunk=nodes // 4, **sizes),
        in_specs=[SMEM] + [VMEM] * (1 + peers + len(hubs)),
        out_specs=ANY,
        scratch_shapes=[
            pltpu.VMEM((nodes, width), F32),
            pltpu.VMEM((nodes, width), BF16),
            pltpu.SemaphoreType.DMA((4,)),
        ],
        out_shape=shape((nodes, width), BF16),
        compiler_params=params,
        name="final",
    )(send, self_grad, *returned, *hubs)
    return (output, feature_grad)


def exchange_order(n_col):
    return sorted(range(1, n_col), key=lambda d: (d != n_col // 2, -d))


def solution(mesh):
    blocks = ("row", "col")
    placed = (
        P(blocks, None),
        P(),
        P(),
        P(),
        P(),
        P(blocks, None, None, None),
        P(blocks, None, None),
        P(blocks, None),
        P(blocks, None, None),
        P(blocks, None, None, None, None),
        P(blocks, None),
    )
    n_row, n_col = mesh.shape["row"], mesh.shape["col"]

    def body(*args):
        return shards(*args, n_row=n_row, n_col=n_col)

    return jax.shard_map(
        body, mesh=mesh, in_specs=placed, out_specs=(P(blocks, None), P(blocks, None)), check_vma=False
    )
```

time: 148 us -> 52.1 us (0.35)
  waiting for transfers between devices: 58.7 us -> 12.9 us
  matrix products: 39.3 us -> 0 us
  between operations: 21.7 us -> 0.89 us
  Pallas kernels: 0 us -> 19.8 us
  local copies, waits for them, and re-layouts: 12.1 us -> 0.06 us
  starting transfers between devices: 10.1 us -> 18.2 us
  other arithmetic: 5.25 us -> 0.07 us
    psum x1 -> x0, waiting for transfers between devices: 50.6 us -> none  [shards(): summed_section = lax.psum(partial_grad, 'row')]
    dot_general x20 -> x0, matrix products: 39.3 us -> none  [the longest x6 14.8 us: shards(): lax.dot_general(adjacency[section], agg_grad, (((0,), (0,)), ((), ())), p...]
    pallas_call x0 -> x9, Pallas kernels: none -> 19.8 us  [the longest x1 3.39 us: shards(): pl.pallas_call(functools.partial(hub_backward_kernel, **sizes), in_specs=...]
    ppermute x0 -> x14, starting transfers between devices: none -> 18.2 us  [across(): return lax.ppermute(x, axis, [(i, i ^ d) for i in range(size)])]
    ppermute x0 -> x14, waiting for transfers between devices: none -> 12.9 us  [across(): return lax.ppermute(x, axis, [(i, i ^ d) for i in range(size)])]
    all_to_all x2 -> x0, starting transfers between devices: 9.82 us -> none  [the longest x1 6.35 us: shards(): lax.all_to_all(outgoing, 'col', split_axis=0, concat_axis=0, tiled=True)]
    all_to_all x2 -> x0, waiting for transfers between devices: 8.08 us -> none  [the longest x1 4.98 us: shards(): lax.all_to_all(slot_grad.reshape(peers, slots, tile, width), 'col', split...]
    dot_general x3 -> x0, local copies, waits for them, and re-layouts: 4.24 us -> none  [the longest x1 2.55 us: shards(): jnp.einsum('sn,sid->nid', select, contrib, precision=lax.Precision.HIGHEST)]
  transfers between devices with their start and end apart: 4 -> 14, of which waited for: 3 -> 6; matrix products, arithmetic and copies ran while one was open for 17% -> 0% of each run, Pallas kernels for 0% -> 18%
where the time goes in v1:
time: 52.1 us; the launch traced here: 51.9 us
  Pallas kernels  19.8 us (38%)
  starting transfers between devices  18.2 us (35%)
  waiting for transfers between devices  12.9 us (25%)
  between operations  0.89 us (2%)
    ppermute x14, starting transfers between devices, across(): return lax.ppermute(x, axis, [(i, i ^ d) for i in range(size)])  18.2 us
    ppermute x14, waiting for transfers between devices, across(): return lax.ppermute(x, axis, [(i, i ^ d) for i in range(size)])  12.9 us
    pallas_call x1, Pallas kernels, shards(): pl.pallas_call(functools.partial(hub_backward_kernel, **sizes), in_specs=...  3.39 us
    pallas_call x1, Pallas kernels, shards(): pl.pallas_call(functools.partial(landed_kernel, group=group, **sizes), in...  3.11 us
    pallas_call x1, Pallas kernels, shards(): pl.pallas_call(functools.partial(load_kernel, chunk=nodes // 8), in_specs...  3.04 us
    pallas_call x1, Pallas kernels, shards(): pl.pallas_call(functools.partial(hub_forward_kernel, chunk=256), in_specs...  2.47 us
    pallas_call x1, Pallas kernels, shards(): pl.pallas_call(functools.partial(pick_kernel, tile=tile), in_specs=[SMEM,...  2.08 us
    pallas_call x1, Pallas kernels, shards(): pl.pallas_call(functools.partial(self_kernel, **sizes), in_specs=[SMEM] *...  1.99 us
  transfers between devices with their start and end apart: 14, of which 6 were waited for; matrix products, arithmetic and copies ran while one was open for 0% of the time, Pallas kernels for 18%

profile of v1, /device:TPU:0, one launch (start us, length us, event | category | flops | bytes accessed | tf_op | source)
XLA Modules:
  0.0 51.9 jit_solution(11929090262406639166)
XLA Ops:
  0.6 2.1 %pick.1 = (bf16[256,256]{1,0:T(8,128)(2,1)S(1)}, bf16[2,128,256]{2,1,0:T(8,128)(2,1)S(1)}, bf16[2,128,256]{2,1,0:T(8,128)(2,1)S(1)}, bf16[2,128,256]{2,1,0:T(8,128)(2,1)S(1)}, bf16[2,128,256]{2,1,0:T(8,128)(2,1)S(1)}) custom-call(s32[2,4]{1,0:T(2,128)} %bitcast.19, bf16[2048,256]{1,0:T(8,128)(2,1)} %feats.5), custom_call_target="tpu_custom_call" | custom-call | tf_op jit(solution)/shard_map/pick/pallas_call | solution.py:277
  2.7 4.0 %collective-permute-start.2 = (bf16[256,256]{1,0:T(8,128)(2,1)S(1)}, bf16[256,256]{1,0:T(8,128)(2,1)S(1)}, u32[]{:S(2)}, u32[]{:S(2)}) collective-permute-start(bf16[256,256]{1,0:T(8,128)(2,1)S(1)} %get-tuple-element.28), channel_id=1, source_target_pairs={{0,24},{4,28},{8,16},{12,20},{16,8},{20,12},{24,0},{28,4},{1,25},{... | collective-permute-start | bytes 393224 | tf_op jit(solution)/shard_map/ppermute | solution.py:273
  6.7 0.5 collective-permute-start.1
  7.2 0.1 collective-permute-start
  7.4 3.2 %collective-permute-done.2 = bf16[256,256]{1,0:T(8,128)(2,1)S(1)} collective-permute-done((bf16[256,256]{1,0:T(8,128)(2,1)S(1)}, bf16[256,256]{1,0:T(8,128)(2,1)S(1)}, u32[]{:S(2)}, u32[]{:S(2)}) %collective-permute-start.2) | collective-permute-done | bytes 131104 | tf_op jit(solution)/shard_map/ppermute | solution.py:273
  10.6 2.4 %collective-permute-done.1 = bf16[256,256]{1,0:T(8,128)(2,1)S(1)} collective-permute-done((bf16[256,256]{1,0:T(8,128)(2,1)S(1)}, bf16[256,256]{1,0:T(8,128)(2,1)S(1)}, u32[]{:S(2)}, u32[]{:S(2)}) %collective-permute-start.1) | collective-permute-done | bytes 131104 | tf_op jit(solution)/shard_map/ppermute | solution.py:273
  13.0 0.3 collective-permute-done
  13.3 0.1 pad_maximum_fusion.same
  13.3 0.1 collective-permute-start.3
  13.4 1.6 %collective-permute-start.4 = (bf16[2,128,256]{2,1,0:T(8,128)(2,1)S(1)}, bf16[2,128,256]{2,1,0:T(8,128)(2,1)S(1)}, u32[]{:S(2)}, u32[]{:S(2)}) collective-permute-start(bf16[2,128,256]{2,1,0:T(8,128)(2,1)S(1)} %get-tuple-element.31), channel_id=1, source_target_pairs={{0,1},{1,0},{2,3},{3,2},{4,5},{5,4},{6,7},{7,6},{8,9},{9,8},{10,11... | collective-permute-start | bytes 393224 | tf_op jit(solution)/shard_map/ppermute | solution.py:273
  15.1 2.6 %collective-permute-start.5 = (bf16[2,128,256]{2,1,0:T(8,128)(2,1)S(1)}, bf16[2,128,256]{2,1,0:T(8,128)(2,1)S(1)}, u32[]{:S(2)}, u32[]{:S(2)}) collective-permute-start(bf16[2,128,256]{2,1,0:T(8,128)(2,1)S(1)} %get-tuple-element.32), channel_id=1, source_target_pairs={{0,2},{1,3},{2,0},{3,1},{4,6},{5,7},{6,4},{7,5},{8,10},{9,11},{10,... | collective-permute-start | bytes 393224 | tf_op jit(solution)/shard_map/ppermute | solution.py:273
  17.7 0.2 collective-permute-start.6
  17.9 3.0 %load.1 = (bf16[6,2048,256]{2,1,0:T(8,128)(2,1)S(1)}, f32[2048,128]{1,0:T(8,128)S(1)}) custom-call(bf16[6,2048,256]{2,1,0:T(8,128)(2,1)} %bitcast.23), custom_call_target="tpu_custom_call" | custom-call | tf_op jit(solution)/shard_map/load/pallas_call | solution.py:292
  20.9 0.0 copy-start
  20.9 0.0 copy-start.1
  20.9 0.0 copy-start.2
  21.0 0.0 copy-start.3
  21.0 0.0 copy-start.5
  21.0 0.0 copy-start.6
  21.0 0.0 copy-start.8
  21.0 0.0 collective-permute-done.3.other
  21.0 0.0 copy-start.4
  21.0 2.5 %hub_forward.1.raw_in.raw = f32[2048,256]{1,0:T(8,128)S(1)} custom-call(s32[6]{0:T(128)S(1)} %copy-done.9, bf16[6,2048,256]{2,1,0:T(8,128)(2,1)S(1)} %get-tuple-element.27.adj, bf16[4,256,256]{2,1,0:T(8,128)(2,1)S(1)} %pad_maximum_fusion.same, bf16[4,256,256]{2,1,0:T(8,128)(2,1)S(1)} %collective-permute-done.3.other), custom_call_target="tpu_custom_call" | custom-call | flops 1610612736 | bytes 4194304 | tf_op jit(solution)/shard_map/hub_forward/pallas_call | solution.py:301
  23.6 1.7 %others.1 = (bf16[1024,256]{1,0:T(8,128)(2,1)S(1)}, bf16[1024,256]{1,0:T(8,128)(2,1)S(1)}, bf16[1024,256]{1,0:T(8,128)(2,1)S(1)}) custom-call(s32[1,4]{1,0:T(1,128)S(1)} %copy-done.6, s32[2,4]{1,0:T(2,128)S(1)} %bitcast.15, f32[2048,256]{1,0:T(8,128)S(1)} %hub_forward.1.raw_in.raw, f32[2048,128]{1,0:T(8,128)S(1)} %get-tuple-element.29.deg_in.deg, ...), custom_call_target="tpu_custom_call" | custom-call | tf_op jit(solution)/shard_map/others/pallas_call | solution.py:319
  25.3 0.0 collective-permute-done.4.rest_1_
  25.3 2.7 %collective-permute-done.5.rest_2_ = bf16[2,128,256]{2,1,0:T(8,128)(2,1)S(1)} collective-permute-done((bf16[2,128,256]{2,1,0:T(8,128)(2,1)S(1)}, bf16[2,128,256]{2,1,0:T(8,128)(2,1)S(1)}, u32[]{:S(2)}, u32[]{:S(2)}) %collective-permute-start.5) | collective-permute-done | bytes 131104 | tf_op jit(solution)/shard_map/ppermute | solution.py:273
  28.0 0.0 collective-permute-done.6.rest_3_
  28.0 0.0 copy-done.4
  28.0 3.1 %landed.1 = (bf16[1024,256]{1,0:T(8,128)(2,1)S(1)}, bf16[1024,256]{1,0:T(8,128)(2,1)S(1)}, bf16[1024,256]{1,0:T(8,128)(2,1)S(1)}, bf16[2,128,256]{2,1,0:T(8,128)...) custom-call(s32[1,4]{1,0:T(1,128)S(1)} %copy-done.6, ...), custom_call_target="tpu_custom_call" | custom-call | tf_op jit(solution)/shard_map/landed/pallas_call | solution.py:328
  31.1 0.0 copy-start.7
  31.1 3.4 %hub_backward.1 = (bf16[4,256,256]{2,1,0:T(8,128)(2,1)S(1)}, bf16[4,256,256]{2,1,0:T(8,128)(2,1)S(1)}) custom-call(s32[1,4]{1,0:T(1,128)S(1)} %copy-done.6, s32[2,4]{1,0:T(2,128)S(1)} %bitcast.17, s32[6]{0:T(128)S(1)} %copy-done.9, bf16[6,2048,256]{2,1,0:T(8,128)(2,1)S(1)} %get-tuple-element.27.adj, bf16[1024,256]{1,0:T(8,128)(2,1)S(1)} %get-tuple-element.44.rest_0_, ...), custom_call_target="tpu_custom_call" | custom-call | flops 1610612736 | bytes 4194304 | tf_op jit(solution)/shard_map/hub_backward/pallas_call | solution.py:344
  34.5 0.1 collective-permute-start.10
  34.6 2.5 %collective-permute-start.7 = (bf16[2,128,256]{2,1,0:T(8,128)(2,1)S(1)}, bf16[2,128,256]{2,1,0:T(8,128)(2,1)S(1)}, u32[]{:S(2)}, u32[]{:S(2)}) collective-permute-start(bf16[2,128,256]{2,1,0:T(8,128)(2,1)S(1)} %get-tuple-element.41), channel_id=1, source_target_pairs={{0,1},{1,0},{2,3},{3,2},{4,5},{5,4},{6,7},{7,6},{8,9},{9,8},{10,11... | collective-permute-start | bytes 393224 | tf_op jit(solution)/shard_map/ppermute | solution.py:273
  37.1 0.8 %collective-permute-start.8 = (bf16[2,128,256]{2,1,0:T(8,128)(2,1)S(1)}, bf16[2,128,256]{2,1,0:T(8,128)(2,1)S(1)}, u32[]{:S(2)}, u32[]{:S(2)}) collective-permute-start(bf16[2,128,256]{2,1,0:T(8,128)(2,1)S(1)} %get-tuple-element.42), channel_id=1, source_target_pairs={{0,2},{1,3},{2,0},{3,1},{4,6},{5,7},{6,4},{7,5},{8,10},{9,11},{10,... | collective-permute-start | bytes 393224 | tf_op jit(solution)/shard_map/ppermute | solution.py:273
  37.9 1.6 %collective-permute-start.9 = (bf16[2,128,256]{2,1,0:T(8,128)(2,1)S(1)}, bf16[2,128,256]{2,1,0:T(8,128)(2,1)S(1)}, u32[]{:S(2)}, u32[]{:S(2)}) collective-permute-start(bf16[2,128,256]{2,1,0:T(8,128)(2,1)S(1)} %get-tuple-element.43), channel_id=1, source_target_pairs={{0,3},{1,2},{2,1},{3,0},{4,7},{5,6},{6,5},{7,4},{8,11},{9,10},{10,... | collective-permute-start | bytes 393224 | tf_op jit(solution)/shard_map/ppermute | solution.py:273
  39.5 0.0 collective-permute-done.10.came
  39.5 0.1 pair_add.1
  39.7 1.8 %collective-permute-start.11 = (bf16[256,256]{1,0:T(8,128)(2,1)S(1)}, bf16[256,256]{1,0:T(8,128)(2,1)S(1)}, u32[]{:S(2)}, u32[]{:S(2)}) collective-permute-start(bf16[256,256]{1,0:T(8,128)(2,1)S(1)} %get-tuple-element.49), channel_id=1, source_target_pairs={{0,8},{4,12},{8,0},{12,4},{16,24},{20,28},{24,16},{28,20},{1,9},{5... | collective-permute-start | bytes 393224 | tf_op jit(solution)/shard_map/ppermute | solution.py:273
  41.5 0.5 %collective-permute-start.12 = (bf16[256,256]{1,0:T(8,128)(2,1)S(1)}, bf16[256,256]{1,0:T(8,128)(2,1)S(1)}, u32[]{:S(2)}, u32[]{:S(2)}) collective-permute-start(bf16[256,256]{1,0:T(8,128)(2,1)S(1)} %get-tuple-element.50), channel_id=1, source_target_pairs={{0,16},{4,20},{8,24},{12,28},{16,0},{20,4},{24,8},{28,12},{1,17},{... | collective-permute-start | bytes 393224 | tf_op jit(solution)/shard_map/ppermute | solution.py:273
  42.0 1.2 %collective-permute-done.7.rest_1_ = bf16[2,128,256]{2,1,0:T(8,128)(2,1)S(1)} collective-permute-done((bf16[2,128,256]{2,1,0:T(8,128)(2,1)S(1)}, bf16[2,128,256]{2,1,0:T(8,128)(2,1)S(1)}, u32[]{:S(2)}, u32[]{:S(2)}) %collective-permute-start.7) | collective-permute-done | bytes 131104 | tf_op jit(solution)/shard_map/ppermute | solution.py:273
  43.2 1.7 %collective-permute-start.13 = (bf16[256,256]{1,0:T(8,128)(2,1)S(1)}, bf16[256,256]{1,0:T(8,128)(2,1)S(1)}, u32[]{:S(2)}, u32[]{:S(2)}) collective-permute-start(bf16[256,256]{1,0:T(8,128)(2,1)S(1)} %get-tuple-element.51), channel_id=1, source_target_pairs={{0,24},{4,28},{8,16},{12,20},{16,8},{20,12},{24,0},{28,4},{1,25},{... | collective-permute-start | bytes 393224 | tf_op jit(solution)/shard_map/ppermute | solution.py:273
  45.0 2.0 %self.1 = (bf16[2048,256]{1,0:T(8,128)(2,1)}, f32[2048,256]{1,0:T(8,128)S(1)}) custom-call(s32[1,4]{1,0:T(1,128)S(1)} %copy-done.6, s32[2,4]{1,0:T(2,128)S(1)} %bitcast.18, bf16[256,256]{1,0:T(8,128)(2,1)S(1)} %copy-done.2, bf16[1024,256]{1,0:T(8,128)(2,1)S(1)} %get-tuple-element.34.rest_0_, bf16[1024,256]{1,0:T(8,128)(2,1)S(1)} %get-tuple-element.35.rest_1_, ...), custom_call_target="tpu_custom_call" | custom-call | tf_op jit(solution)/shard_map/self/pallas_call | solution.py:355
  47.0 3.1 %collective-permute-done.8.rest_2_ = bf16[2,128,256]{2,1,0:T(8,128)(2,1)S(1)} collective-permute-done((bf16[2,128,256]{2,1,0:T(8,128)(2,1)S(1)}, bf16[2,128,256]{2,1,0:T(8,128)(2,1)S(1)}, u32[]{:S(2)}, u32[]{:S(2)}) %collective-permute-start.8) | collective-permute-done | bytes 131104 | tf_op jit(solution)/shard_map/ppermute | solution.py:273
  50.0 0.0 collective-permute-done.9.rest_3_
  50.0 0.0 collective-permute-done.11.rest_5_
  50.0 0.0 collective-permute-done.12.rest_6_
  50.0 0.0 collective-permute-done.13.rest_7_
  50.1 1.9 %final.1 = bf16[2048,256]{1,0:T(8,128)(2,1)} custom-call(s32[2,4]{1,0:T(2,128)S(1)} %bitcast.20, f32[2048,256]{1,0:T(8,128)S(1)} %get-tuple-element.39.self_grad, bf16[2,128,256]{2,1,0:T(8,128)(2,1)S(1)} %get-tuple-element.40.rest_0_, bf16[2,128,256]{2,1,0:T(8,128)(2,1)S(1)} %collective-permute-done.7.rest_1_, ...), custom_call_target="tpu_custom_call" | custom-call | tf_op jit(solution)/shard_map/final/pallas_call | solution.py:373
  (10 shorter events, 0.0 us)
Async XLA Ops:
  0.6 20.4 %copy-start.9 = (s32[6]{0:T(128)S(1)}, s32[6]{0:T(128)}, u32[]{:S(2)}) copy-start(s32[6]{0:T(128)} %hub_ids.3) | copy-start | bytes 76
  2.7 7.9 %collective-permute-start.2 = (bf16[256,256]{1,0:T(8,128)(2,1)S(1)}, bf16[256,256]{1,0:T(8,128)(2,1)S(1)}, u32[]{:S(2)}, u32[]{:S(2)}) collective-permute-start(bf16[256,256]{1,0:T(8,128)(2,1)S(1)} %get-tuple-element.28), channel_id=1, source_target_pairs={{0,24},{4,28},{8,16},{12,20},{16,8},{20,12},{24,0},{28,4},{1,25},{... | collective-permute-start | bytes 393224 | tf_op jit(solution)/shard_map/ppermute | solution.py:273
  6.7 6.3 %collective-permute-start.1 = (bf16[256,256]{1,0:T(8,128)(2,1)S(1)}, bf16[256,256]{1,0:T(8,128)(2,1)S(1)}, u32[]{:S(2)}, u32[]{:S(2)}) collective-permute-start(bf16[256,256]{1,0:T(8,128)(2,1)S(1)} %get-tuple-element.28), channel_id=1, source_target_pairs={{0,16},{4,20},{8,24},{12,28},{16,0},{20,4},{24,8},{28,12},{1,17},{... | collective-permute-start | bytes 393224 | tf_op jit(solution)/shard_map/ppermute | solution.py:273
  7.2 6.1 %collective-permute-start = (bf16[256,256]{1,0:T(8,128)(2,1)S(1)}, bf16[256,256]{1,0:T(8,128)(2,1)S(1)}, u32[]{:S(2)}, u32[]{:S(2)}) collective-permute-start(bf16[256,256]{1,0:T(8,128)(2,1)S(1)} %get-tuple-element.28), channel_id=1, source_target_pairs={{0,8},{4,12},{8,0},{12,4},{16,24},{20,28},{24,16},{28,20},{1,9},{5... | collective-permute-start | bytes 393224 | tf_op jit(solution)/shard_map/ppermute | solution.py:273
  13.3 7.7 %collective-permute-start.3 = (bf16[4,256,256]{2,1,0:T(8,128)(2,1)S(1)}, bf16[4,256,256]{2,1,0:T(8,128)(2,1)S(1)}, u32[]{:S(2)}, u32[]{:S(2)}) collective-permute-start(bf16[4,256,256]{2,1,0:T(8,128)(2,1)S(1)} %pad_maximum_fusion.same), channel_id=1, source_target_pairs={{0,4},{4,0},{8,12},{12,8},{16,20},{20,16},{24,28},{28,24},{1,5},{5... | collective-permute-start | bytes 1572872 | tf_op jit(solution)/shard_map/ppermute | solution.py:273
  13.4 11.9 %collective-permute-start.4 = (bf16[2,128,256]{2,1,0:T(8,128)(2,1)S(1)}, bf16[2,128,256]{2,1,0:T(8,128)(2,1)S(1)}, u32[]{:S(2)}, u32[]{:S(2)}) collective-permute-start(bf16[2,128,256]{2,1,0:T(8,128)(2,1)S(1)} %get-tuple-element.31), channel_id=1, source_target_pairs={{0,1},{1,0},{2,3},{3,2},{4,5},{5,4},{6,7},{7,6},{8,9},{9,8},{10,11... | collective-permute-start | bytes 393224 | tf_op jit(solution)/shard_map/ppermute | solution.py:273
  15.1 12.9 %collective-permute-start.5 = (bf16[2,128,256]{2,1,0:T(8,128)(2,1)S(1)}, bf16[2,128,256]{2,1,0:T(8,128)(2,1)S(1)}, u32[]{:S(2)}, u32[]{:S(2)}) collective-permute-start(bf16[2,128,256]{2,1,0:T(8,128)(2,1)S(1)} %get-tuple-element.32), channel_id=1, source_target_pairs={{0,2},{1,3},{2,0},{3,1},{4,6},{5,7},{6,4},{7,5},{8,10},{9,11},{10,... | collective-permute-start | bytes 393224 | tf_op jit(solution)/shard_map/ppermute | solution.py:273
  17.7 10.3 %collective-permute-start.6 = (bf16[2,128,256]{2,1,0:T(8,128)(2,1)S(1)}, bf16[2,128,256]{2,1,0:T(8,128)(2,1)S(1)}, u32[]{:S(2)}, u32[]{:S(2)}) collective-permute-start(bf16[2,128,256]{2,1,0:T(8,128)(2,1)S(1)} %get-tuple-element.33), channel_id=1, source_target_pairs={{0,3},{1,2},{2,1},{3,0},{4,7},{5,6},{6,5},{7,4},{8,11},{9,10},{10,... | collective-permute-start | bytes 393224 | tf_op jit(solution)/shard_map/ppermute | solution.py:273
  20.9 2.6 %copy-start = (bf16[2048,256]{1,0:T(8,128)(2,1)S(1)}, bf16[2048,256]{1,0:T(8,128)(2,1)}, u32[]{:S(2)}) copy-start(bf16[2048,256]{1,0:T(8,128)(2,1)} %feats.5) | copy-start | bytes 3145732
  20.9 2.6 %copy-start.1 = (bf16[2048,256]{1,0:T(8,128)(2,1)S(1)}, bf16[2048,256]{1,0:T(8,128)(2,1)}, u32[]{:S(2)}) copy-start(bf16[2048,256]{1,0:T(8,128)(2,1)} %cot.3) | copy-start | bytes 3145732
  20.9 2.6 %copy-start.2 = (bf16[256,256]{1,0:T(8,128)(2,1)S(1)}, bf16[256,256]{1,0:T(8,128)(2,1)}, u32[]{:S(2)}) copy-start(bf16[256,256]{1,0:T(8,128)(2,1)} %w_self.5) | copy-start | bytes 393220
  21.0 2.6 %copy-start.3 = (bf16[256,256]{1,0:T(8,128)(2,1)S(1)}, bf16[256,256]{1,0:T(8,128)(2,1)}, u32[]{:S(2)}) copy-start(bf16[256,256]{1,0:T(8,128)(2,1)} %w_neigh.3) | copy-start | bytes 393220
  21.0 2.6 %copy-start.5 = (s32[1,4,2]{1,2,0:T(2,128)S(1)}, s32[1,4,2]{1,2,0:T(2,128)}, u32[]{:S(2)}) copy-start(s32[1,4,2]{1,2,0:T(2,128)} %param.19) | copy-start | bytes 100
  21.0 2.6 %copy-start.6 = (s32[1,4]{1,0:T(1,128)S(1)}, s32[1,4]{1,0:T(1,128)}, u32[]{:S(2)}) copy-start(s32[1,4]{1,0:T(1,128)} %count.7) | copy-start | bytes 52
  21.0 2.6 %copy-start.8 = (f32[256]{0:T(256)S(1)}, f32[256]{0:T(256)}, u32[]{:S(2)}) copy-start(f32[256]{0:T(256)} %param.14) | copy-start | bytes 3076
  21.0 7.0 %copy-start.4 = (bf16[1,4,2,128,128]{4,3,2,1,0:T(8,128)(2,1)S(1)}, bf16[1,4,2,128,128]{4,3,2,1,0:T(8,128)(2,1)}, u32[]{:S(2)}) copy-start(bf16[1,4,2,128,128]{4,3,2,1,0:T(8,128)(2,1)} %param.20) | copy-start | bytes 786436
  31.1 18.9 %copy-start.7 = (s32[1,4,2]{1,2,0:T(2,128)S(1)}, s32[1,4,2]{1,2,0:T(2,128)}, u32[]{:S(2)}) copy-start(s32[1,4,2]{1,2,0:T(2,128)} %param.17) | copy-start | bytes 100
  34.5 5.0 %collective-permute-start.10 = (bf16[4,256,256]{2,1,0:T(8,128)(2,1)S(1)}, bf16[4,256,256]{2,1,0:T(8,128)(2,1)S(1)}, u32[]{:S(2)}, u32[]{:S(2)}) collective-permute-start(bf16[4,256,256]{2,1,0:T(8,128)(2,1)S(1)} %get-tuple-element.47), channel_id=1, source_target_pairs={{0,4},{4,0},{8,12},{12,8},{16,20},{20,16},{24,28},{28,24},{1,5},{5... | collective-permute-start | bytes 1572872 | tf_op jit(solution)/shard_map/ppermute | solution.py:273
  34.6 8.6 %collective-permute-start.7 = (bf16[2,128,256]{2,1,0:T(8,128)(2,1)S(1)}, bf16[2,128,256]{2,1,0:T(8,128)(2,1)S(1)}, u32[]{:S(2)}, u32[]{:S(2)}) collective-permute-start(bf16[2,128,256]{2,1,0:T(8,128)(2,1)S(1)} %get-tuple-element.41), channel_id=1, source_target_pairs={{0,1},{1,0},{2,3},{3,2},{4,5},{5,4},{6,7},{7,6},{8,9},{9,8},{10,11... | collective-permute-start | bytes 393224 | tf_op jit(solution)/shard_map/ppermute | solution.py:273
  37.1 12.9 %collective-permute-start.8 = (bf16[2,128,256]{2,1,0:T(8,128)(2,1)S(1)}, bf16[2,128,256]{2,1,0:T(8,128)(2,1)S(1)}, u32[]{:S(2)}, u32[]{:S(2)}) collective-permute-start(bf16[2,128,256]{2,1,0:T(8,128)(2,1)S(1)} %get-tuple-element.42), channel_id=1, source_target_pairs={{0,2},{1,3},{2,0},{3,1},{4,6},{5,7},{6,4},{7,5},{8,10},{9,11},{10,... | collective-permute-start | bytes 393224 | tf_op jit(solution)/shard_map/ppermute | solution.py:273
  37.9 12.1 %collective-permute-start.9 = (bf16[2,128,256]{2,1,0:T(8,128)(2,1)S(1)}, bf16[2,128,256]{2,1,0:T(8,128)(2,1)S(1)}, u32[]{:S(2)}, u32[]{:S(2)}) collective-permute-start(bf16[2,128,256]{2,1,0:T(8,128)(2,1)S(1)} %get-tuple-element.43), channel_id=1, source_target_pairs={{0,3},{1,2},{2,1},{3,0},{4,7},{5,6},{6,5},{7,4},{8,11},{9,10},{10,... | collective-permute-start | bytes 393224 | tf_op jit(solution)/shard_map/ppermute | solution.py:273
  39.7 10.4 %collective-permute-start.11 = (bf16[256,256]{1,0:T(8,128)(2,1)S(1)}, bf16[256,256]{1,0:T(8,128)(2,1)S(1)}, u32[]{:S(2)}, u32[]{:S(2)}) collective-permute-start(bf16[256,256]{1,0:T(8,128)(2,1)S(1)} %get-tuple-element.49), channel_id=1, source_target_pairs={{0,8},{4,12},{8,0},{12,4},{16,24},{20,28},{24,16},{28,20},{1,9},{5... | collective-permute-start | bytes 393224 | tf_op jit(solution)/shard_map/ppermute | solution.py:273
  41.5 8.6 %collective-permute-start.12 = (bf16[256,256]{1,0:T(8,128)(2,1)S(1)}, bf16[256,256]{1,0:T(8,128)(2,1)S(1)}, u32[]{:S(2)}, u32[]{:S(2)}) collective-permute-start(bf16[256,256]{1,0:T(8,128)(2,1)S(1)} %get-tuple-element.50), channel_id=1, source_target_pairs={{0,16},{4,20},{8,24},{12,28},{16,0},{20,4},{24,8},{28,12},{1,17},{... | collective-permute-start | bytes 393224 | tf_op jit(solution)/shard_map/ppermute | solution.py:273
  43.2 6.8 %collective-permute-start.13 = (bf16[256,256]{1,0:T(8,128)(2,1)S(1)}, bf16[256,256]{1,0:T(8,128)(2,1)S(1)}, u32[]{:S(2)}, u32[]{:S(2)}) collective-permute-start(bf16[256,256]{1,0:T(8,128)(2,1)S(1)} %get-tuple-element.51), channel_id=1, source_target_pairs={{0,24},{4,28},{8,16},{12,20},{16,8},{20,12},{24,0},{28,4},{1,25},{... | collective-permute-start | bytes 393224 | tf_op jit(solution)/shard_map/ppermute | solution.py:273

commit v2 on v1

--- a/solution.py
+++ b/solution.py
@@ -69,27 +69,6 @@
         deg[at, :] = jnp.broadcast_to(1.0 + jnp.sum(lanes, axis=1, keepdims=True), (chunk, 128))
 
 
-def hub_forward_kernel(hub_ids, adj, same, other, raw, blocks, *, chunk):
-    row = lax.axis_index("row")
-    sections, nodes, hub_rows = adj.shape
-    for s in range(sections):
-        away = hub_ids[s] ^ row
-        at = pl.ds(s * hub_rows, hub_rows)
-
-        @pl.when(away & 1 == 0)
-        def _(away=away, at=at):
-            blocks[at, :] = same[away >> 1]
-
-        @pl.when(away & 1 == 1)
-        def _(away=away, at=at):
-            blocks[at, :] = other[away >> 1]
-
-    for start in range(0, nodes, chunk):
-        at = pl.ds(start, chunk)
-        weights = jnp.concatenate([adj[s, at, :] for s in range(sections)], axis=1)
-        raw[at, :] = jnp.dot(weights, blocks[...], preferred_element_type=F32)
-
-
 def dense(raw, deg, feats, cot, w_self, w_neigh, bias):
     inverse = 1.0 / deg
     inverse = jnp.concatenate([inverse] * (raw.shape[1] // inverse.shape[1]), axis=1)
@@ -106,11 +85,51 @@
     return out, grad, agg_grad
 
 
+def forward_kernel(
+    count, dst, hub_ids, adj, same, other, deg, feats, cot, w_self, w_neigh, bias,
+    raw, *rest, peers, slots, tile, chunk, group
+):
+    results, (blocks, order, place) = rest[:-3], rest[-3:]
+    row = lax.axis_index("row")
+    sections, nodes, hub_rows = adj.shape
+    for s in range(sections):
+        away = hub_ids[s] ^ row
+        at = pl.ds(s * hub_rows, hub_rows)
+
+        @pl.when(away & 1 == 0)
+        def _(away=away, at=at):
+            blocks[at, :] = same[away >> 1]
+
+        @pl.when(away & 1 == 1)
+        def _(away=away, at=at):
+            blocks[at, :] = other[away >> 1]
+
+    tiles = nodes // tile
+    if results:
+        tile_order(count, dst, order, place, peers=peers, slots=slots, tiles=tiles)
+    for start in range(0, nodes, chunk):
+        at = pl.ds(start, chunk)
+        weights = jnp.concatenate([adj[s, at, :] for s in range(sections)], axis=1)
+        raw[at, :] = jnp.dot(weights, blocks[...], preferred_element_type=F32)
+    if results:
+        out, grad, turned = results
+        first = tiles - out.shape[0] // tile
+        for start in range(first, tiles, group):
+            here = pl.ds((start - first) * tile, group * tile)
+            there = [rows_at(order[i], tile) for i in range(start, start + group)]
+            o, g, a = dense(
+                *[jnp.concatenate([x[at, :] for at in there]) for x in (raw, deg, feats, cot)], w_self, w_neigh, bias
+            )
+            out[here, :] = o
+            grad[here, :] = g
+            turned[:, here] = a.T
+
+
 def landed_kernel(count, dst, raw_in, deg_in, feats, cot, adj, w_self, w_neigh, bias, *rest, peers, slots, tile, group):
     inc = rest[:peers]
-    out, grad, agg_grad = rest[peers : peers + 3]
+    out, grad, turned = rest[peers : peers + 3]
     back = rest[peers + 3 : 2 * peers + 3]
-    raw, deg, order, place = rest[2 * peers + 3 :]
+    raw, deg, agg_grad, order, place = rest[2 * peers + 3 :]
     col = lax.axis_index("col")
     tile_order(count, dst, order, place, peers=peers, slots=slots, tiles=raw_in.shape[0] // tile)
     first = raw.shape[0] // tile
@@ -118,17 +137,24 @@
         at = rows_at(order[i], tile)
         raw[pl.ds(i * tile, tile), :] = raw_in[at, :]
         deg[pl.ds(i * tile, tile), :] = deg_in[at, :]
+    parts = []
     for d in range(peers):
         p = col ^ d
         for k in range(slots):
-
-            @pl.when(k < count[0, p])
-            def _(d=d, k=k, p=p):
-                at = rows_at(place[dst[k, p]], tile)
-                weights = adj[p, k]
-                raw[at, :] += jnp.dot(weights, inc[d][k], preferred_element_type=F32)
-                deg[at, :] += jnp.sum(weights.astype(F32), axis=1, keepdims=True)
-
+            weights = adj[p, k]
+            parts.append(
+                (
+                    k < count[0, p],
+                    dst[k, p],
+                    jnp.dot(weights, inc[d][k], preferred_element_type=F32),
+                    jnp.sum(weights.astype(F32), axis=1, keepdims=True),
+                )
+            )
+    for alive, target, part, lanes in parts:
+        at = rows_at(jnp.where(alive, place[target], 0), tile)
+        scale = jnp.where(alive, 1.0, 0.0).astype(F32)
+        raw[at, :] += part * scale
+        deg[at, :] += lanes * scale
     for start in range(0, first, group):
         here = pl.ds(start * tile, group * tile)
         there = [rows_at(order[i], tile) for i in range(start, start + group)]
@@ -144,6 +170,7 @@
         out[here, :] = o
         grad[here, :] = g
         agg_grad[here, :] = a
+        turned[:, here] = a.T
     for d in range(peers):
         p = col ^ d
         for k in range(slots):
@@ -153,52 +180,20 @@
             back[d][k] = (part * jnp.where(alive, 1.0, 0.0).astype(F32)).astype(BF16)
 
 
-def others_kernel(
-    count, dst, raw, deg, feats, cot, w_self, w_neigh, bias, out, grad, agg_grad, order, place, *, peers, slots, tile, group
-):
-    tiles = raw.shape[0] // tile
-    first = tiles - out.shape[0] // tile
-    tile_order(count, dst, order, place, peers=peers, slots=slots, tiles=tiles)
-    for start in range(first, tiles, group):
-        here = pl.ds((start - first) * tile, group * tile)
-        there = [rows_at(order[i], tile) for i in range(start, start + group)]
-        o, g, a = dense(
-            *[jnp.concatenate([x[at, :] for at in there]) for x in (raw, deg, feats, cot)], w_self, w_neigh, bias
-        )
-        out[here, :] = o
-        grad[here, :] = g
-        agg_grad[here, :] = a
-
-
 def hub_backward_kernel(count, dst, hub_ids, adj, *rest, peers, slots, tile):
-    pieces, (even, odd, agg_grad, order, place) = rest[:-5], rest[-5:]
+    pieces, (even, odd, acc, order, place) = rest[:-5], rest[-5:]
     row = lax.axis_index("row")
-    sections = adj.shape[0]
-    tiles = agg_grad.shape[0] // tile
-    tile_order(count, dst, order, place, peers=peers, slots=slots, tiles=tiles)
-    i = 0
-    for piece in pieces:
-        for j in range(piece.shape[0] // tile):
-            agg_grad[rows_at(order[i], tile), :] = piece[pl.ds(j * tile, tile), :]
-            i += 1
-    turned = agg_grad[...].T
-    owner = [hub_ids[s] ^ row for s in range(sections)]
-    for ref in (even, odd):
-        ref[...] = jnp.zeros_like(ref)
-    parts = [jnp.dot(turned, adj[s], preferred_element_type=F32) for s in range(sections)]
+    sections, nodes, _ = adj.shape
+    tile_order(count, dst, order, place, peers=peers, slots=slots, tiles=nodes // tile)
+    there = [rows_at(order[i], tile) for i in range(nodes // tile)]
+    acc[...] = jnp.zeros_like(acc)
     for s in range(sections):
-        total = parts[s]
-        for other in range(sections):
-            if other != s:
-                total = total + parts[other] * jnp.where(owner[other] == owner[s], 1.0, 0.0).astype(F32)
-
-        @pl.when(owner[s] & 1 == 0)
-        def _(s=s, total=total):
-            even[owner[s] >> 1] = total.astype(BF16)
-
-        @pl.when(owner[s] & 1 == 1)
-        def _(s=s, total=total):
-            odd[owner[s] >> 1] = total.astype(BF16)
+        turned = jnp.concatenate([piece[...] for piece in pieces], axis=1)
+        weights = jnp.concatenate([adj[s, at, :] for at in there])
+        acc[hub_ids[s] ^ row] += jnp.dot(turned, weights, preferred_element_type=F32)
+    for e in range(even.shape[0]):
+        even[e] = acc[2 * e].astype(BF16)
+        odd[e] = acc[2 * e + 1].astype(BF16)
 
 
 def self_kernel(count, dst, w_self, *rest, peers, slots, tile):
@@ -229,25 +224,33 @@
         out[...] = (even[e].astype(F32) + came[e].astype(F32)).astype(BF16)
 
 
-def final_kernel(send, self_grad, *rest, peers, slots, tile, chunk):
-    back, hub, (out, total, done, sems) = rest[:peers], rest[peers:-4], rest[-4:]
+def tiles_kernel(send, self_grad, *rest, peers, slots, tile, chunk):
+    back, (out, head, total, done, sems) = rest[:peers], rest[peers:]
     col = lax.axis_index("col")
     total[...] = self_grad[...]
     for d in range(peers):
         for k in range(slots):
             total[rows_at(send[k, col ^ d], tile), :] += back[d][k].astype(F32)
-    come = hub[0][...].astype(F32)
-    for h in hub[1:]:
-        come = come + h[...].astype(F32)
-    total[0 : come.shape[1], :] += come.T
+    head[...] = total[pl.ds(0, head.shape[0]), :]
     copies = []
-    for i, start in enumerate(range(0, total.shape[0], chunk)):
+    for i, start in enumerate(range(head.shape[0], total.shape[0], chunk)):
         at = pl.ds(start, chunk)
         done[at, :] = total[at, :].astype(BF16)
         copies.append(pltpu.make_async_copy(done.at[at], out.at[at], sems.at[i]))
         copies[-1].start()
     for copy in copies:
         copy.wait()
+
+
+def head_kernel(head, *rest):
+    hub, (_, out, done, sem) = rest[:-4], rest[-4:]
+    come = hub[0][...].astype(F32)
+    for h in hub[1:]:
+        come = come + h[...].astype(F32)
+    done[...] = (head[...] + come.T).astype(BF16)
+    copy = pltpu.make_async_copy(done, out.at[pl.ds(0, done.shape[0])], sem)
+    copy.start()
+    copy.wait()
 
 
 def shards(
@@ -298,43 +301,34 @@
         compiler_params=params,
         name="load",
     )(pltpu.with_memory_space_constraint(adj, pltpu.HBM))
-    raw = pl.pallas_call(
-        functools.partial(hub_forward_kernel, chunk=256),
-        in_specs=[SMEM, VMEM, VMEM, VMEM],
-        out_specs=VMEM,
-        scratch_shapes=[pltpu.VMEM((sections * hub_rows, width), BF16)],
-        out_shape=shape((nodes, width), F32),
+    tables = [pltpu.SMEM((tiles,), jnp.int32), pltpu.SMEM((tiles,), jnp.int32)]
+
+    def results(number):
+        if not number:
+            return []
+        return [shape((number * tile, out_width), BF16)] * 2 + [shape((width, number * tile), BF16)]
+
+    raw, *others = pl.pallas_call(
+        functools.partial(forward_kernel, chunk=256, group=group, **sizes),
+        in_specs=[SMEM] * 3 + [VMEM] * 9,
+        out_specs=[VMEM] * (1 + len(results(tiles - first))),
+        scratch_shapes=[pltpu.VMEM((sections * hub_rows, width), BF16)] + tables,
+        out_shape=[shape((nodes, width), F32)] + results(tiles - first),
         compiler_params=params,
         cost_estimate=cost(2 * sections * nodes * hub_rows * width),
-        name="hub_forward",
-    )(hub_ids, adj, same, other)
-
-    tables = [pltpu.SMEM((tiles,), jnp.int32), pltpu.SMEM((tiles,), jnp.int32)]
-
-    def results(number):
-        return [shape((number * tile, n), BF16) for n in (out_width, out_width, width)]
-
-    others = []
-    if first < tiles:
-        others = pl.pallas_call(
-            functools.partial(others_kernel, group=group, **sizes),
-            in_specs=[SMEM, SMEM] + [VMEM] * 7,
-            out_specs=[VMEM] * 3,
-            scratch_shapes=tables,
-            out_shape=results(tiles - first),
-            compiler_params=params,
-            name="others",
-        )(count, dst, raw, deg, features, cotangent, w_self, w_neigh, bias)
+        name="forward",
+    )(count, dst, hub_ids, adj, same, other, deg, features, cotangent, w_self, w_neigh, bias)
     landed = pl.pallas_call(
         functools.partial(landed_kernel, group=group, **sizes),
         in_specs=[SMEM, SMEM] + [VMEM] * (8 + peers),
         out_specs=[VMEM] * (3 + peers),
-        scratch_shapes=[pltpu.VMEM((first * tile, width), F32), pltpu.VMEM((first * tile, 128), F32)] + tables,
+        scratch_shapes=[pltpu.VMEM((first * tile, n), t) for n, t in ((width, F32), (128, F32), (width, BF16))]
+        + tables,
         out_shape=results(first) + [pair] * peers,
         compiler_params=params,
         name="landed",
     )(count, dst, raw, deg, features, cotangent, weights, w_self, w_neigh, bias, *incoming)
-    outs, grads, agg_grads = zip(*([landed[:3]] + ([others] if others else [])))
+    outs, grads, turned = zip(*([landed[:3]] + ([others] if others else [])))
     going = landed[3:]
     returned = [going[0]] + [None] * (peers - 1)
     for d in order:
@@ -343,14 +337,14 @@
     half = shape((n_row // 2, width, hub_rows), BF16)
     even, odd = pl.pallas_call(
         functools.partial(hub_backward_kernel, **sizes),
-        in_specs=[SMEM] * 3 + [VMEM] * (1 + len(agg_grads)),
+        in_specs=[SMEM] * 3 + [VMEM] * (1 + len(turned)),
         out_specs=[VMEM] * 2,
-        scratch_shapes=[pltpu.VMEM((nodes, width), BF16)] + tables,
+        scratch_shapes=[pltpu.VMEM((n_row, width, hub_rows), F32)] + tables,
         out_shape=[half, half],
         compiler_params=params,
         cost_estimate=cost(2 * sections * nodes * hub_rows * width),
         name="hub_backward",
-    )(count, dst, hub_ids, adj, *agg_grads)
+    )(count, dst, hub_ids, adj, *turned)
     came = across(odd, "row", n_row, 1)
     output, self_grad = pl.pallas_call(
         functools.partial(self_kernel, **sizes),
@@ -370,24 +364,35 @@
     )(even, came)
     hubs = [sums[0]] + [across(sums[d // 2], "row", n_row, d) for d in range(2, n_row, 2)]
 
-    feature_grad = pl.pallas_call(
-        functools.partial(final_kernel, chunk=nodes // 4, **sizes),
-        in_specs=[SMEM] + [VMEM] * (1 + peers + len(hubs)),
-        out_specs=ANY,
+    chunk = 2 * tile
+    feature_grad, head = pl.pallas_call(
+        functools.partial(tiles_kernel, chunk=chunk, **sizes),
+        in_specs=[SMEM] + [VMEM] * (1 + peers),
+        out_specs=[HBM, VMEM],
         scratch_shapes=[
             pltpu.VMEM((nodes, width), F32),
             pltpu.VMEM((nodes, width), BF16),
-            pltpu.SemaphoreType.DMA((4,)),
+            pltpu.SemaphoreType.DMA(((nodes - hub_rows) // chunk,)),
         ],
+        out_shape=[shape((nodes, width), BF16), shape((hub_rows, width), F32)],
+        compiler_params=params,
+        name="tiles_done",
+    )(send, self_grad, *returned)
+    feature_grad = pl.pallas_call(
+        head_kernel,
+        in_specs=[VMEM] * (1 + len(hubs)) + [HBM],
+        out_specs=HBM,
+        scratch_shapes=[pltpu.VMEM((hub_rows, width), BF16), pltpu.SemaphoreType.DMA],
         out_shape=shape((nodes, width), BF16),
-        compiler_params=params,
-        name="final",
-    )(send, self_grad, *returned, *hubs)
+        input_output_aliases={1 + len(hubs): 0},
+        compiler_params=params,
+        name="head",
+    )(head, *hubs, feature_grad)
     return (output, feature_grad)
 
 
 def exchange_order(n_col):
-    return sorted(range(1, n_col), key=lambda d: (d != n_col // 2, -d))
+    return sorted(range(1, n_col), key=lambda d: (d != n_col // 2, d))
 
 
 def solution(mesh):

time: 52.1 us -> 51.6 us (level)
  Pallas kernels: 19.8 us -> 18.6 us
  waiting for transfers between devices: 12.9 us -> 13.5 us
    pallas_call x1, Pallas kernels: 3.39 us -> 2.64 us  [shards(): pl.pallas_call(functools.partial(hub_backward_kernel, **sizes), in_specs=...]
    pallas_call x1, Pallas kernels: 3.11 us -> 2.44 us  [shards(): pl.pallas_call(functools.partial(landed_kernel, group=group, **sizes), in...]
    ppermute x14, waiting for transfers between devices: 12.9 us -> 13.5 us  [across(): return lax.ppermute(x, axis, [(i, i ^ d) for i in range(size)])]
  transfers between devices with their start and end apart: 14 -> 14, of which waited for: 6 -> 6; matrix products, arithmetic and copies ran while one was open for 0% -> 0% of each run, Pallas kernels for 18% -> 21%
where the time goes in v2:
time: 51.6 us; the launch traced here: 51.4 us
  Pallas kernels  18.6 us (36%)
  starting transfers between devices  18.3 us (35%)
  waiting for transfers between devices  13.5 us (26%)
  between operations  0.9 us (2%)
    ppermute x14, starting transfers between devices, across(): return lax.ppermute(x, axis, [(i, i ^ d) for i in range(size)])  18.3 us
    ppermute x14, waiting for transfers between devices, across(): return lax.ppermute(x, axis, [(i, i ^ d) for i in range(size)])  13.5 us
    pallas_call x1, Pallas kernels, shards(): pl.pallas_call(functools.partial(forward_kernel, chunk=256, group=group,...  3.69 us
    pallas_call x1, Pallas kernels, shards(): pl.pallas_call(functools.partial(load_kernel, chunk=nodes // 8), in_specs...  3.04 us
    pallas_call x1, Pallas kernels, shards(): pl.pallas_call(functools.partial(hub_backward_kernel, **sizes), in_specs=...  2.64 us
    pallas_call x1, Pallas kernels, shards(): pl.pallas_call(functools.partial(landed_kernel, group=group, **sizes), in...  2.44 us
    pallas_call x1, Pallas kernels, shards(): pl.pallas_call(functools.partial(pick_kernel, tile=tile), in_specs=[SMEM,...  2.08 us
    pallas_call x1, Pallas kernels, shards(): pl.pallas_call(functools.partial(self_kernel, **sizes), in_specs=[SMEM] *...  1.98 us
  transfers between devices with their start and end apart: 14, of which 6 were waited for; matrix products, arithmetic and copies ran while one was open for 0% of the time, Pallas kernels for 21%

profile of v2, /device:TPU:0, one launch (start us, length us, event | category | flops | bytes accessed | tf_op | source)
XLA Modules:
  0.0 51.4 jit_solution(16497053749019944287)
XLA Ops:
  0.6 0.0 copy-start
  0.6 0.0 copy-start.6
  0.7 0.0 copy-start.2
  0.7 0.0 copy-start.1
  0.7 0.0 copy-start.9
  0.7 0.0 copy-start.3
  0.7 0.0 copy-start.5
  0.7 0.0 copy-start.7
  0.7 2.1 %pick.1 = (bf16[256,256]{1,0:T(8,128)(2,1)S(1)}, bf16[2,128,256]{2,1,0:T(8,128)(2,1)S(1)}, bf16[2,128,256]{2,1,0:T(8,128)(2,1)S(1)}, bf16[2,128,256]{2,1,0:T(8,128)(2,1)S(1)}, bf16[2,128,256]{2,1,0:T(8,128)(2,1)S(1)}) custom-call(s32[2,4]{1,0:T(2,128)} %bitcast.21, bf16[2048,256]{1,0:T(8,128)(2,1)} %feats.5), custom_call_target="tpu_custom_call" | custom-call | tf_op jit(solution)/shard_map/pick/pallas_call | solution.py:280
  2.8 4.0 %collective-permute-start.2 = (bf16[256,256]{1,0:T(8,128)(2,1)S(1)}, bf16[256,256]{1,0:T(8,128)(2,1)S(1)}, u32[]{:S(2)}, u32[]{:S(2)}) collective-permute-start(bf16[256,256]{1,0:T(8,128)(2,1)S(1)} %get-tuple-element.31), channel_id=1, source_target_pairs={{0,24},{4,28},{8,16},{12,20},{16,8},{20,12},{24,0},{28,4},{1,25},{... | collective-permute-start | bytes 393224 | tf_op jit(solution)/shard_map/ppermute | solution.py:276
  6.8 0.5 collective-permute-start.1
  7.3 0.1 collective-permute-start
  7.4 3.2 %collective-permute-done.2 = bf16[256,256]{1,0:T(8,128)(2,1)S(1)} collective-permute-done((bf16[256,256]{1,0:T(8,128)(2,1)S(1)}, bf16[256,256]{1,0:T(8,128)(2,1)S(1)}, u32[]{:S(2)}, u32[]{:S(2)}) %collective-permute-start.2) | collective-permute-done | bytes 131104 | tf_op jit(solution)/shard_map/ppermute | solution.py:276
  10.7 2.4 %collective-permute-done.1 = bf16[256,256]{1,0:T(8,128)(2,1)S(1)} collective-permute-done((bf16[256,256]{1,0:T(8,128)(2,1)S(1)}, bf16[256,256]{1,0:T(8,128)(2,1)S(1)}, u32[]{:S(2)}, u32[]{:S(2)}) %collective-permute-start.1) | collective-permute-done | bytes 131104 | tf_op jit(solution)/shard_map/ppermute | solution.py:276
  13.1 0.3 collective-permute-done
  13.3 0.1 pad_maximum_fusion.same
  13.4 0.1 collective-permute-start.3
  13.5 1.6 %collective-permute-start.4 = (bf16[2,128,256]{2,1,0:T(8,128)(2,1)S(1)}, bf16[2,128,256]{2,1,0:T(8,128)(2,1)S(1)}, u32[]{:S(2)}, u32[]{:S(2)}) collective-permute-start(bf16[2,128,256]{2,1,0:T(8,128)(2,1)S(1)} %get-tuple-element.35), channel_id=1, source_target_pairs={{0,1},{1,0},{2,3},{3,2},{4,5},{5,4},{6,7},{7,6},{8,9},{9,8},{10,11... | collective-permute-start | bytes 393224 | tf_op jit(solution)/shard_map/ppermute | solution.py:276
  15.1 2.6 %collective-permute-start.5 = (bf16[2,128,256]{2,1,0:T(8,128)(2,1)S(1)}, bf16[2,128,256]{2,1,0:T(8,128)(2,1)S(1)}, u32[]{:S(2)}, u32[]{:S(2)}) collective-permute-start(bf16[2,128,256]{2,1,0:T(8,128)(2,1)S(1)} %get-tuple-element.36), channel_id=1, source_target_pairs={{0,2},{1,3},{2,0},{3,1},{4,6},{5,7},{6,4},{7,5},{8,10},{9,11},{10,... | collective-permute-start | bytes 393224 | tf_op jit(solution)/shard_map/ppermute | solution.py:276
  17.7 0.2 collective-permute-start.6
  18.0 3.0 %load.1 = (bf16[6,2048,256]{2,1,0:T(8,128)(2,1)S(1)}, f32[2048,128]{1,0:T(8,128)S(1)}) custom-call(bf16[6,2048,256]{2,1,0:T(8,128)(2,1)} %bitcast.23), custom_call_target="tpu_custom_call" | custom-call | tf_op jit(solution)/shard_map/load/pallas_call | solution.py:295
  21.0 0.0 copy-start.4
  21.0 0.0 collective-permute-done.3.other
  21.1 3.7 %forward.1 = (f32[2048,256]{1,0:T(8,128)S(1)}, bf16[1024,256]{1,0:T(8,128)(2,1)S(1)}, bf16[1024,256]{1,0:T(8,128)(2,1)S(1)}, bf16[256,1024]{1,0:T(8,128)(2,1)S(1)}) custom-call(s32[1,4]{1,0:T(1,128)S(1)} %copy-done.6, s32[2,4]{1,0:T(2,128)S(1)} %bitcast.15, s32[6]{0:T(128)S(1)} %copy-done.9, bf16[6,2048,256]{2,1,0:T(8,128)(2,1)S(1)} %get-tuple-element.30.adj, ...), custom_call_target="tpu_custom_call" | custom-call | flops 1610612736 | bytes 4194304 | tf_op jit(solution)/shard_map/forward/pallas_call | solution.py:311
  24.8 0.0 collective-permute-done.4.rest_1_
  24.8 3.3 %collective-permute-done.5.rest_2_ = bf16[2,128,256]{2,1,0:T(8,128)(2,1)S(1)} collective-permute-done((bf16[2,128,256]{2,1,0:T(8,128)(2,1)S(1)}, bf16[2,128,256]{2,1,0:T(8,128)(2,1)S(1)}, u32[]{:S(2)}, u32[]{:S(2)}) %collective-permute-start.5) | collective-permute-done | bytes 131104 | tf_op jit(solution)/shard_map/ppermute | solution.py:276
  28.1 0.0 collective-permute-done.6.rest_3_
  28.1 2.4 %landed.1 = (bf16[1024,256]{1,0:T(8,128)(2,1)S(1)}, bf16[1024,256]{1,0:T(8,128)(2,1)S(1)}, bf16[256,1024]{1,0:T(8,128)(2,1)S(1)}, bf16[2,128,256]{2,1,0:T(8,128)...) custom-call(s32[1,4]{1,0:T(1,128)S(1)} %copy-done.6, ...), custom_call_target="tpu_custom_call" | custom-call | tf_op jit(solution)/shard_map/landed/pallas_call | solution.py:321
  30.5 0.0 copy-start.8
  30.5 2.6 %hub_backward.1 = (bf16[4,256,256]{2,1,0:T(8,128)(2,1)S(1)}, bf16[4,256,256]{2,1,0:T(8,128)(2,1)S(1)}) custom-call(s32[1,4]{1,0:T(1,128)S(1)} %copy-done.6, s32[2,4]{1,0:T(2,128)S(1)} %bitcast.17, s32[6]{0:T(128)S(1)} %copy-done.9, bf16[6,2048,256]{2,1,0:T(8,128)(2,1)S(1)} %get-tuple-element.30.adj, bf16[256,1024]{1,0:T(8,128)(2,1)S(1)} %get-tuple-element.49.rest_0_, ...), custom_call_target="tpu_custom_call" | custom-call | flops 1610612736 | bytes 4194304 | tf_op jit(solution)/shard_map/hub_backward/pallas_call | solution.py:338
  33.2 0.1 collective-permute-start.10
  33.3 2.6 %collective-permute-start.7 = (bf16[2,128,256]{2,1,0:T(8,128)(2,1)S(1)}, bf16[2,128,256]{2,1,0:T(8,128)(2,1)S(1)}, u32[]{:S(2)}, u32[]{:S(2)}) collective-permute-start(bf16[2,128,256]{2,1,0:T(8,128)(2,1)S(1)} %get-tuple-element.45), channel_id=1, source_target_pairs={{0,1},{1,0},{2,3},{3,2},{4,5},{5,4},{6,7},{7,6},{8,9},{9,8},{10,11... | collective-permute-start | bytes 393224 | tf_op jit(solution)/shard_map/ppermute | solution.py:276
  35.9 1.1 %collective-permute-start.8 = (bf16[2,128,256]{2,1,0:T(8,128)(2,1)S(1)}, bf16[2,128,256]{2,1,0:T(8,128)(2,1)S(1)}, u32[]{:S(2)}, u32[]{:S(2)}) collective-permute-start(bf16[2,128,256]{2,1,0:T(8,128)(2,1)S(1)} %get-tuple-element.46), channel_id=1, source_target_pairs={{0,2},{1,3},{2,0},{3,1},{4,6},{5,7},{6,4},{7,5},{8,10},{9,11},{10,... | collective-permute-start | bytes 393224 | tf_op jit(solution)/shard_map/ppermute | solution.py:276
  37.0 1.4 %collective-permute-start.9 = (bf16[2,128,256]{2,1,0:T(8,128)(2,1)S(1)}, bf16[2,128,256]{2,1,0:T(8,128)(2,1)S(1)}, u32[]{:S(2)}, u32[]{:S(2)}) collective-permute-start(bf16[2,128,256]{2,1,0:T(8,128)(2,1)S(1)} %get-tuple-element.47), channel_id=1, source_target_pairs={{0,3},{1,2},{2,1},{3,0},{4,7},{5,6},{6,5},{7,4},{8,11},{9,10},{10,... | collective-permute-start | bytes 393224 | tf_op jit(solution)/shard_map/ppermute | solution.py:276
  38.3 0.0 collective-permute-done.10.came
  38.3 0.1 pair_add.1
  38.5 1.6 %collective-permute-start.11 = (bf16[256,256]{1,0:T(8,128)(2,1)S(1)}, bf16[256,256]{1,0:T(8,128)(2,1)S(1)}, u32[]{:S(2)}, u32[]{:S(2)}) collective-permute-start(bf16[256,256]{1,0:T(8,128)(2,1)S(1)} %get-tuple-element.54), channel_id=1, source_target_pairs={{0,8},{4,12},{8,0},{12,4},{16,24},{20,28},{24,16},{28,20},{1,9},{5... | collective-permute-start | bytes 393224 | tf_op jit(solution)/shard_map/ppermute | solution.py:276
  40.1 0.7 %collective-permute-start.12 = (bf16[256,256]{1,0:T(8,128)(2,1)S(1)}, bf16[256,256]{1,0:T(8,128)(2,1)S(1)}, u32[]{:S(2)}, u32[]{:S(2)}) collective-permute-start(bf16[256,256]{1,0:T(8,128)(2,1)S(1)} %get-tuple-element.55), channel_id=1, source_target_pairs={{0,16},{4,20},{8,24},{12,28},{16,0},{20,4},{24,8},{28,12},{1,17},{... | collective-permute-start | bytes 393224 | tf_op jit(solution)/shard_map/ppermute | solution.py:276
  40.8 1.3 %collective-permute-done.7.rest_1_ = bf16[2,128,256]{2,1,0:T(8,128)(2,1)S(1)} collective-permute-done((bf16[2,128,256]{2,1,0:T(8,128)(2,1)S(1)}, bf16[2,128,256]{2,1,0:T(8,128)(2,1)S(1)}, u32[]{:S(2)}, u32[]{:S(2)}) %collective-permute-start.7) | collective-permute-done | bytes 131104 | tf_op jit(solution)/shard_map/ppermute | solution.py:276
  42.1 1.7 %collective-permute-start.13 = (bf16[256,256]{1,0:T(8,128)(2,1)S(1)}, bf16[256,256]{1,0:T(8,128)(2,1)S(1)}, u32[]{:S(2)}, u32[]{:S(2)}) collective-permute-start(bf16[256,256]{1,0:T(8,128)(2,1)S(1)} %get-tuple-element.56), channel_id=1, source_target_pairs={{0,24},{4,28},{8,16},{12,20},{16,8},{20,12},{24,0},{28,4},{1,25},{... | collective-permute-start | bytes 393224 | tf_op jit(solution)/shard_map/ppermute | solution.py:276
  43.8 2.0 %self.1 = (bf16[2048,256]{1,0:T(8,128)(2,1)}, f32[2048,256]{1,0:T(8,128)S(1)}) custom-call(s32[1,4]{1,0:T(1,128)S(1)} %copy-done.6, s32[2,4]{1,0:T(2,128)S(1)} %bitcast.18, bf16[256,256]{1,0:T(8,128)(2,1)S(1)} %copy-done.2, bf16[1024,256]{1,0:T(8,128)(2,1)S(1)} %get-tuple-element.38.rest_0_, bf16[1024,256]{1,0:T(8,128)(2,1)S(1)} %get-tuple-element.39.rest_1_, ...), custom_call_target="tpu_custom_call" | custom-call | tf_op jit(solution)/shard_map/self/pallas_call | solution.py:349
  45.8 3.0 %collective-permute-done.8.rest_2_ = bf16[2,128,256]{2,1,0:T(8,128)(2,1)S(1)} collective-permute-done((bf16[2,128,256]{2,1,0:T(8,128)(2,1)S(1)}, bf16[2,128,256]{2,1,0:T(8,128)(2,1)S(1)}, u32[]{:S(2)}, u32[]{:S(2)}) %collective-permute-start.8) | collective-permute-done | bytes 131104 | tf_op jit(solution)/shard_map/ppermute | solution.py:276
  48.8 0.0 collective-permute-done.9.rest_3_
  48.8 1.8 %tiles_done.1 = (bf16[2048,256]{1,0:T(8,128)(2,1)}, f32[256,256]{1,0:T(8,128)S(1)}) custom-call(s32[2,4]{1,0:T(2,128)S(1)} %bitcast.22, f32[2048,256]{1,0:T(8,128)S(1)} %get-tuple-element.43.self_grad, bf16[2,128,256]{2,1,0:T(8,128)(2,1)S(1)} %get-tuple-element.44.rest_0_, bf16[2,128,256]{2,1,0:T(8,128)(2,1)S(1)} %collective-permute-done.7.rest_1_, ...), custom_call_target="tpu_custom_call" | custom-call | tf_op jit(solution)/shard_map/tiles_done/pallas_call | solution.py:368
  50.6 0.0 collective-permute-done.11.rest_1_
  50.6 0.0 collective-permute-done.12.rest_2_
  50.6 0.0 collective-permute-done.13.rest_3_
  50.6 0.8 %head.1 = bf16[2048,256]{1,0:T(8,128)(2,1)} custom-call(f32[256,256]{1,0:T(8,128)S(1)} %get-tuple-element.48.head, bf16[256,256]{1,0:T(8,128)(2,1)S(1)} %get-tuple-element.53.rest_0_, bf16[256,256]{1,0:T(8,128)(2,1)S(1)} %collective-permute-done.11.rest_1_, bf16[256,256]{1,0:T(8,128)(2,1)S(1)} %collective-permute-done.12.rest_2_, ...), custom_call_target="tpu_custom_call", output_to_operand_aliasing={{}: (5, {})} | custom-call | tf_op jit(solution)/shard_map/head/pallas_call | solution.py:381
  (10 shorter events, 0.0 us)
Async XLA Ops:
  0.6 20.4 %copy-start = (bf16[2048,256]{1,0:T(8,128)(2,1)S(1)}, bf16[2048,256]{1,0:T(8,128)(2,1)}, u32[]{:S(2)}) copy-start(bf16[2048,256]{1,0:T(8,128)(2,1)} %feats.5) | copy-start | bytes 3145732
  0.6 20.4 %copy-start.6 = (s32[1,4]{1,0:T(1,128)S(1)}, s32[1,4]{1,0:T(1,128)}, u32[]{:S(2)}) copy-start(s32[1,4]{1,0:T(1,128)} %count.7) | copy-start | bytes 52
  0.7 20.4 %copy-start.2 = (bf16[256,256]{1,0:T(8,128)(2,1)S(1)}, bf16[256,256]{1,0:T(8,128)(2,1)}, u32[]{:S(2)}) copy-start(bf16[256,256]{1,0:T(8,128)(2,1)} %w_self.5) | copy-start | bytes 393220
  0.7 20.4 %copy-start.1 = (bf16[2048,256]{1,0:T(8,128)(2,1)S(1)}, bf16[2048,256]{1,0:T(8,128)(2,1)}, u32[]{:S(2)}) copy-start(bf16[2048,256]{1,0:T(8,128)(2,1)} %cot.3) | copy-start | bytes 3145732
  0.7 20.4 %copy-start.9 = (s32[6]{0:T(128)S(1)}, s32[6]{0:T(128)}, u32[]{:S(2)}) copy-start(s32[6]{0:T(128)} %hub_ids.3) | copy-start | bytes 76
  0.7 20.4 %copy-start.3 = (bf16[256,256]{1,0:T(8,128)(2,1)S(1)}, bf16[256,256]{1,0:T(8,128)(2,1)}, u32[]{:S(2)}) copy-start(bf16[256,256]{1,0:T(8,128)(2,1)} %w_neigh.3) | copy-start | bytes 393220
  0.7 20.4 %copy-start.5 = (s32[1,4,2]{1,2,0:T(2,128)S(1)}, s32[1,4,2]{1,2,0:T(2,128)}, u32[]{:S(2)}) copy-start(s32[1,4,2]{1,2,0:T(2,128)} %param.19) | copy-start | bytes 100
  0.7 20.4 %copy-start.7 = (f32[256]{0:T(256)S(1)}, f32[256]{0:T(256)}, u32[]{:S(2)}) copy-start(f32[256]{0:T(256)} %param.14) | copy-start | bytes 3076
  2.8 7.9 %collective-permute-start.2 = (bf16[256,256]{1,0:T(8,128)(2,1)S(1)}, bf16[256,256]{1,0:T(8,128)(2,1)S(1)}, u32[]{:S(2)}, u32[]{:S(2)}) collective-permute-start(bf16[256,256]{1,0:T(8,128)(2,1)S(1)} %get-tuple-element.31), channel_id=1, source_target_pairs={{0,24},{4,28},{8,16},{12,20},{16,8},{20,12},{24,0},{28,4},{1,25},{... | collective-permute-start | bytes 393224 | tf_op jit(solution)/shard_map/ppermute | solution.py:276
  6.8 6.3 %collective-permute-start.1 = (bf16[256,256]{1,0:T(8,128)(2,1)S(1)}, bf16[256,256]{1,0:T(8,128)(2,1)S(1)}, u32[]{:S(2)}, u32[]{:S(2)}) collective-permute-start(bf16[256,256]{1,0:T(8,128)(2,1)S(1)} %get-tuple-element.31), channel_id=1, source_target_pairs={{0,16},{4,20},{8,24},{12,28},{16,0},{20,4},{24,8},{28,12},{1,17},{... | collective-permute-start | bytes 393224 | tf_op jit(solution)/shard_map/ppermute | solution.py:276
  7.3 6.1 %collective-permute-start = (bf16[256,256]{1,0:T(8,128)(2,1)S(1)}, bf16[256,256]{1,0:T(8,128)(2,1)S(1)}, u32[]{:S(2)}, u32[]{:S(2)}) collective-permute-start(bf16[256,256]{1,0:T(8,128)(2,1)S(1)} %get-tuple-element.31), channel_id=1, source_target_pairs={{0,8},{4,12},{8,0},{12,4},{16,24},{20,28},{24,16},{28,20},{1,9},{5... | collective-permute-start | bytes 393224 | tf_op jit(solution)/shard_map/ppermute | solution.py:276
  13.4 7.6 %collective-permute-start.3 = (bf16[4,256,256]{2,1,0:T(8,128)(2,1)S(1)}, bf16[4,256,256]{2,1,0:T(8,128)(2,1)S(1)}, u32[]{:S(2)}, u32[]{:S(2)}) collective-permute-start(bf16[4,256,256]{2,1,0:T(8,128)(2,1)S(1)} %pad_maximum_fusion.same), channel_id=1, source_target_pairs={{0,4},{4,0},{8,12},{12,8},{16,20},{20,16},{24,28},{28,24},{1,5},{5... | collective-permute-start | bytes 1572872 | tf_op jit(solution)/shard_map/ppermute | solution.py:276
  13.5 11.3 %collective-permute-start.4 = (bf16[2,128,256]{2,1,0:T(8,128)(2,1)S(1)}, bf16[2,128,256]{2,1,0:T(8,128)(2,1)S(1)}, u32[]{:S(2)}, u32[]{:S(2)}) collective-permute-start(bf16[2,128,256]{2,1,0:T(8,128)(2,1)S(1)} %get-tuple-element.35), channel_id=1, source_target_pairs={{0,1},{1,0},{2,3},{3,2},{4,5},{5,4},{6,7},{7,6},{8,9},{9,8},{10,11... | collective-permute-start | bytes 393224 | tf_op jit(solution)/shard_map/ppermute | solution.py:276
  15.1 12.9 %collective-permute-start.5 = (bf16[2,128,256]{2,1,0:T(8,128)(2,1)S(1)}, bf16[2,128,256]{2,1,0:T(8,128)(2,1)S(1)}, u32[]{:S(2)}, u32[]{:S(2)}) collective-permute-start(bf16[2,128,256]{2,1,0:T(8,128)(2,1)S(1)} %get-tuple-element.36), channel_id=1, source_target_pairs={{0,2},{1,3},{2,0},{3,1},{4,6},{5,7},{6,4},{7,5},{8,10},{9,11},{10,... | collective-permute-start | bytes 393224 | tf_op jit(solution)/shard_map/ppermute | solution.py:276
  17.7 10.3 %collective-permute-start.6 = (bf16[2,128,256]{2,1,0:T(8,128)(2,1)S(1)}, bf16[2,128,256]{2,1,0:T(8,128)(2,1)S(1)}, u32[]{:S(2)}, u32[]{:S(2)}) collective-permute-start(bf16[2,128,256]{2,1,0:T(8,128)(2,1)S(1)} %get-tuple-element.37), channel_id=1, source_target_pairs={{0,3},{1,2},{2,1},{3,0},{4,7},{5,6},{6,5},{7,4},{8,11},{9,10},{10,... | collective-permute-start | bytes 393224 | tf_op jit(solution)/shard_map/ppermute | solution.py:276
  21.0 7.1 %copy-start.4 = (bf16[1,4,2,128,128]{4,3,2,1,0:T(8,128)(2,1)S(1)}, bf16[1,4,2,128,128]{4,3,2,1,0:T(8,128)(2,1)}, u32[]{:S(2)}) copy-start(bf16[1,4,2,128,128]{4,3,2,1,0:T(8,128)(2,1)} %param.20) | copy-start | bytes 786436
  30.5 18.3 %copy-start.8 = (s32[1,4,2]{1,2,0:T(2,128)S(1)}, s32[1,4,2]{1,2,0:T(2,128)}, u32[]{:S(2)}) copy-start(s32[1,4,2]{1,2,0:T(2,128)} %param.17) | copy-start | bytes 100
  33.2 5.2 %collective-permute-start.10 = (bf16[4,256,256]{2,1,0:T(8,128)(2,1)S(1)}, bf16[4,256,256]{2,1,0:T(8,128)(2,1)S(1)}, u32[]{:S(2)}, u32[]{:S(2)}) collective-permute-start(bf16[4,256,256]{2,1,0:T(8,128)(2,1)S(1)} %get-tuple-element.52), channel_id=1, source_target_pairs={{0,4},{4,0},{8,12},{12,8},{16,20},{20,16},{24,28},{28,24},{1,5},{5... | collective-permute-start | bytes 1572872 | tf_op jit(solution)/shard_map/ppermute | solution.py:276
  33.3 8.8 %collective-permute-start.7 = (bf16[2,128,256]{2,1,0:T(8,128)(2,1)S(1)}, bf16[2,128,256]{2,1,0:T(8,128)(2,1)S(1)}, u32[]{:S(2)}, u32[]{:S(2)}) collective-permute-start(bf16[2,128,256]{2,1,0:T(8,128)(2,1)S(1)} %get-tuple-element.45), channel_id=1, source_target_pairs={{0,1},{1,0},{2,3},{3,2},{4,5},{5,4},{6,7},{7,6},{8,9},{9,8},{10,11... | collective-permute-start | bytes 393224 | tf_op jit(solution)/shard_map/ppermute | solution.py:276
  35.9 12.9 %collective-permute-start.8 = (bf16[2,128,256]{2,1,0:T(8,128)(2,1)S(1)}, bf16[2,128,256]{2,1,0:T(8,128)(2,1)S(1)}, u32[]{:S(2)}, u32[]{:S(2)}) collective-permute-start(bf16[2,128,256]{2,1,0:T(8,128)(2,1)S(1)} %get-tuple-element.46), channel_id=1, source_target_pairs={{0,2},{1,3},{2,0},{3,1},{4,6},{5,7},{6,4},{7,5},{8,10},{9,11},{10,... | collective-permute-start | bytes 393224 | tf_op jit(solution)/shard_map/ppermute | solution.py:276
  37.0 11.8 %collective-permute-start.9 = (bf16[2,128,256]{2,1,0:T(8,128)(2,1)S(1)}, bf16[2,128,256]{2,1,0:T(8,128)(2,1)S(1)}, u32[]{:S(2)}, u32[]{:S(2)}) collective-permute-start(bf16[2,128,256]{2,1,0:T(8,128)(2,1)S(1)} %get-tuple-element.47), channel_id=1, source_target_pairs={{0,3},{1,2},{2,1},{3,0},{4,7},{5,6},{6,5},{7,4},{8,11},{9,10},{10,... | collective-permute-start | bytes 393224 | tf_op jit(solution)/shard_map/ppermute | solution.py:276
  38.5 12.1 %collective-permute-start.11 = (bf16[256,256]{1,0:T(8,128)(2,1)S(1)}, bf16[256,256]{1,0:T(8,128)(2,1)S(1)}, u32[]{:S(2)}, u32[]{:S(2)}) collective-permute-start(bf16[256,256]{1,0:T(8,128)(2,1)S(1)} %get-tuple-element.54), channel_id=1, source_target_pairs={{0,8},{4,12},{8,0},{12,4},{16,24},{20,28},{24,16},{28,20},{1,9},{5... | collective-permute-start | bytes 393224 | tf_op jit(solution)/shard_map/ppermute | solution.py:276
  40.1 10.5 %collective-permute-start.12 = (bf16[256,256]{1,0:T(8,128)(2,1)S(1)}, bf16[256,256]{1,0:T(8,128)(2,1)S(1)}, u32[]{:S(2)}, u32[]{:S(2)}) collective-permute-start(bf16[256,256]{1,0:T(8,128)(2,1)S(1)} %get-tuple-element.55), channel_id=1, source_target_pairs={{0,16},{4,20},{8,24},{12,28},{16,0},{20,4},{24,8},{28,12},{1,17},{... | collective-permute-start | bytes 393224 | tf_op jit(solution)/shard_map/ppermute | solution.py:276
  42.1 8.5 %collective-permute-start.13 = (bf16[256,256]{1,0:T(8,128)(2,1)S(1)}, bf16[256,256]{1,0:T(8,128)(2,1)S(1)}, u32[]{:S(2)}, u32[]{:S(2)}) collective-permute-start(bf16[256,256]{1,0:T(8,128)(2,1)S(1)} %get-tuple-element.56), channel_id=1, source_target_pairs={{0,24},{4,28},{8,16},{12,20},{16,8},{20,12},{24,0},{28,4},{1,25},{... | collective-permute-start | bytes 393224 | tf_op jit(solution)/shard_map/ppermute | solution.py:276

commit v3 on v2

--- a/solution.py
+++ b/solution.py
@@ -52,32 +52,16 @@
         back = back - (1 - bit)
 
 
-def load_kernel(adj, kept, deg, sems, *, chunk):
-    sections, nodes, _ = kept.shape
-    copies = []
-    for i, start in enumerate(range(0, nodes, chunk)):
-        at = pl.ds(start, chunk)
-        copies.append(pltpu.make_async_copy(adj.at[:, at, :], kept.at[:, at, :], sems.at[i]))
-        copies[-1].start()
-    for i, copy in enumerate(copies):
-        copy.wait()
-        at = pl.ds(i * chunk, chunk)
-        wide = jnp.concatenate([kept[s, at, :] for s in range(sections)], axis=1).astype(F32)
-        lanes = wide[:, 0:128]
-        for c in range(128, wide.shape[1], 128):
-            lanes = lanes + wide[:, c : c + 128]
-        deg[at, :] = jnp.broadcast_to(1.0 + jnp.sum(lanes, axis=1, keepdims=True), (chunk, 128))
-
-
-def dense(raw, deg, feats, cot, w_self, w_neigh, bias):
+def early_kernel(count, dst, feats, w_self, bias, order, place, own, *, peers, slots, tile):
+    tile_order(count, dst, order, place, peers=peers, slots=slots, tiles=feats.shape[0] // tile)
+    own[...] = jnp.dot(feats[...], w_self[...], preferred_element_type=F32) + bias[...]
+
+
+def dense(raw, deg, own, cot, w_neigh):
     inverse = 1.0 / deg
     inverse = jnp.concatenate([inverse] * (raw.shape[1] // inverse.shape[1]), axis=1)
     agg = (raw * inverse).astype(BF16)
-    pre = (
-        jnp.dot(feats, w_self[...], preferred_element_type=F32)
-        + jnp.dot(agg, w_neigh[...], preferred_element_type=F32)
-        + bias[...]
-    )
+    pre = own + jnp.dot(agg, w_neigh[...], preferred_element_type=F32)
     sig = 0.5 * jnp.tanh(0.5 * pre) + 0.5
     out = (pre * sig).astype(BF16)
     grad = (cot.astype(F32) * sig * (1.0 + pre * (1.0 - sig))).astype(BF16)
@@ -86,10 +70,9 @@
 
 
 def forward_kernel(
-    count, dst, hub_ids, adj, same, other, deg, feats, cot, w_self, w_neigh, bias,
-    raw, *rest, peers, slots, tile, chunk, group
+    order, hub_ids, adj, same, other, own, cot, w_neigh, raw, deg, *rest, tile, chunk, group
 ):
-    results, (blocks, order, place) = rest[:-3], rest[-3:]
+    results, blocks = rest[:-1], rest[-1]
     row = lax.axis_index("row")
     sections, nodes, hub_rows = adj.shape
     for s in range(sections):
@@ -105,12 +88,15 @@
             blocks[at, :] = other[away >> 1]
 
     tiles = nodes // tile
-    if results:
-        tile_order(count, dst, order, place, peers=peers, slots=slots, tiles=tiles)
     for start in range(0, nodes, chunk):
         at = pl.ds(start, chunk)
         weights = jnp.concatenate([adj[s, at, :] for s in range(sections)], axis=1)
         raw[at, :] = jnp.dot(weights, blocks[...], preferred_element_type=F32)
+        wide = weights.astype(F32)
+        lanes = wide[:, 0:128]
+        for c in range(128, wide.shape[1], 128):
+            lanes = lanes + wide[:, c : c + 128]
+        deg[at, :] = jnp.broadcast_to(1.0 + jnp.sum(lanes, axis=1, keepdims=True), (chunk, 128))
     if results:
         out, grad, turned = results
         first = tiles - out.shape[0] // tile
@@ -118,20 +104,19 @@
             here = pl.ds((start - first) * tile, group * tile)
             there = [rows_at(order[i], tile) for i in range(start, start + group)]
             o, g, a = dense(
-                *[jnp.concatenate([x[at, :] for at in there]) for x in (raw, deg, feats, cot)], w_self, w_neigh, bias
+                *[jnp.concatenate([x[at, :] for at in there]) for x in (raw, deg, own, cot)], w_neigh
             )
             out[here, :] = o
             grad[here, :] = g
             turned[:, here] = a.T
 
 
-def landed_kernel(count, dst, raw_in, deg_in, feats, cot, adj, w_self, w_neigh, bias, *rest, peers, slots, tile, group):
+def landed_kernel(count, dst, order, place, raw_in, deg_in, own, cot, adj, w_neigh, *rest, peers, slots, tile, group):
     inc = rest[:peers]
     out, grad, turned = rest[peers : peers + 3]
     back = rest[peers + 3 : 2 * peers + 3]
-    raw, deg, agg_grad, order, place = rest[2 * peers + 3 :]
+    raw, deg, agg_grad = rest[2 * peers + 3 :]
     col = lax.axis_index("col")
-    tile_order(count, dst, order, place, peers=peers, slots=slots, tiles=raw_in.shape[0] // tile)
     first = raw.shape[0] // tile
     for i in range(first):
         at = rows_at(order[i], tile)
@@ -161,11 +146,9 @@
         o, g, a = dense(
             raw[here, :],
             deg[here, :],
-            jnp.concatenate([feats[at, :] for at in there]),
+            jnp.concatenate([own[at, :] for at in there]),
             jnp.concatenate([cot[at, :] for at in there]),
-            w_self,
             w_neigh,
-            bias,
         )
         out[here, :] = o
         grad[here, :] = g
@@ -180,11 +163,10 @@
             back[d][k] = (part * jnp.where(alive, 1.0, 0.0).astype(F32)).astype(BF16)
 
 
-def hub_backward_kernel(count, dst, hub_ids, adj, *rest, peers, slots, tile):
-    pieces, (even, odd, acc, order, place) = rest[:-5], rest[-5:]
+def hub_backward_kernel(order, hub_ids, adj, *rest, tile):
+    pieces, (even, odd, acc) = rest[:-3], rest[-3:]
     row = lax.axis_index("row")
     sections, nodes, _ = adj.shape
-    tile_order(count, dst, order, place, peers=peers, slots=slots, tiles=nodes // tile)
     there = [rows_at(order[i], tile) for i in range(nodes // tile)]
     acc[...] = jnp.zeros_like(acc)
     for s in range(sections):
@@ -196,10 +178,8 @@
         odd[e] = acc[2 * e + 1].astype(BF16)
 
 
-def self_kernel(count, dst, w_self, *rest, peers, slots, tile):
-    pieces, (out, self_grad, order, place, sems) = rest[:-5], rest[-5:]
-    tiles = self_grad.shape[0] // tile
-    tile_order(count, dst, order, place, peers=peers, slots=slots, tiles=tiles)
+def self_kernel(order, w_self, *rest, tile):
+    pieces, (out, self_grad, sems) = rest[:-3], rest[-3:]
     copies = []
     i = 0
     for outs, grads in zip(pieces[: len(pieces) // 2], pieces[len(pieces) // 2 :]):
@@ -284,6 +264,7 @@
         scratch_shapes=[pltpu.SemaphoreType.DMA((peers * slots + 1,))],
         out_shape=[shape((hub_rows, width), BF16)] + [pair] * peers,
         compiler_params=params,
+        cost_estimate=pl.CostEstimate(flops=1000000000, transcendentals=0, bytes_accessed=0),
         name="pick",
     )(pltpu.with_memory_space_constraint(send, pltpu.HBM), pltpu.with_memory_space_constraint(features, pltpu.HBM))
     incoming = [picked[0]] + [None] * (peers - 1)
@@ -292,42 +273,40 @@
     same = jnp.stack([own_hub] + [across(own_hub, "row", n_row, d) for d in range(2, n_row, 2)])
     other = across(same, "row", n_row, 1)
 
-    adj, deg = pl.pallas_call(
-        functools.partial(load_kernel, chunk=nodes // 8),
-        in_specs=[HBM],
-        out_specs=[VMEM, VMEM],
-        scratch_shapes=[pltpu.SemaphoreType.DMA((8,))],
-        out_shape=[shape(adj.shape, BF16), shape((nodes, 128), F32)],
-        compiler_params=params,
-        name="load",
-    )(pltpu.with_memory_space_constraint(adj, pltpu.HBM))
-    tables = [pltpu.SMEM((tiles,), jnp.int32), pltpu.SMEM((tiles,), jnp.int32)]
+    tile_at, place, own = pl.pallas_call(
+        functools.partial(early_kernel, **sizes),
+        in_specs=[SMEM] * 2 + [VMEM] * 3,
+        out_specs=[SMEM] * 2 + [VMEM],
+        out_shape=[shape((tiles,), jnp.int32)] * 2 + [shape((nodes, out_width), F32)],
+        compiler_params=params,
+        cost_estimate=pl.CostEstimate(flops=10000000000, transcendentals=0, bytes_accessed=0),
+        name="early",
+    )(count, dst, features, w_self, bias)
 
     def results(number):
         if not number:
             return []
         return [shape((number * tile, out_width), BF16)] * 2 + [shape((width, number * tile), BF16)]
 
-    raw, *others = pl.pallas_call(
-        functools.partial(forward_kernel, chunk=256, group=group, **sizes),
-        in_specs=[SMEM] * 3 + [VMEM] * 9,
-        out_specs=[VMEM] * (1 + len(results(tiles - first))),
-        scratch_shapes=[pltpu.VMEM((sections * hub_rows, width), BF16)] + tables,
-        out_shape=[shape((nodes, width), F32)] + results(tiles - first),
+    raw, deg, *others = pl.pallas_call(
+        functools.partial(forward_kernel, tile=tile, chunk=256, group=group),
+        in_specs=[SMEM] * 2 + [VMEM] * 6,
+        out_specs=[VMEM] * (2 + len(results(tiles - first))),
+        scratch_shapes=[pltpu.VMEM((sections * hub_rows, width), BF16)],
+        out_shape=[shape((nodes, width), F32), shape((nodes, 128), F32)] + results(tiles - first),
         compiler_params=params,
         cost_estimate=cost(2 * sections * nodes * hub_rows * width),
         name="forward",
-    )(count, dst, hub_ids, adj, same, other, deg, features, cotangent, w_self, w_neigh, bias)
+    )(tile_at, hub_ids, adj, same, other, own, cotangent, w_neigh)
     landed = pl.pallas_call(
         functools.partial(landed_kernel, group=group, **sizes),
-        in_specs=[SMEM, SMEM] + [VMEM] * (8 + peers),
+        in_specs=[SMEM] * 4 + [VMEM] * (6 + peers),
         out_specs=[VMEM] * (3 + peers),
-        scratch_shapes=[pltpu.VMEM((first * tile, n), t) for n, t in ((width, F32), (128, F32), (width, BF16))]
-        + tables,
+        scratch_shapes=[pltpu.VMEM((first * tile, n), t) for n, t in ((width, F32), (128, F32), (width, BF16))],
         out_shape=results(first) + [pair] * peers,
         compiler_params=params,
         name="landed",
-    )(count, dst, raw, deg, features, cotangent, weights, w_self, w_neigh, bias, *incoming)
+    )(count, dst, tile_at, place, raw, deg, own, cotangent, weights, w_neigh, *incoming)
     outs, grads, turned = zip(*([landed[:3]] + ([others] if others else [])))
     going = landed[3:]
     returned = [going[0]] + [None] * (peers - 1)
@@ -336,25 +315,25 @@
 
     half = shape((n_row // 2, width, hub_rows), BF16)
     even, odd = pl.pallas_call(
-        functools.partial(hub_backward_kernel, **sizes),
-        in_specs=[SMEM] * 3 + [VMEM] * (1 + len(turned)),
+        functools.partial(hub_backward_kernel, tile=tile),
+        in_specs=[SMEM] * 2 + [VMEM] * (1 + len(turned)),
         out_specs=[VMEM] * 2,
-        scratch_shapes=[pltpu.VMEM((n_row, width, hub_rows), F32)] + tables,
+        scratch_shapes=[pltpu.VMEM((n_row, width, hub_rows), F32)],
         out_shape=[half, half],
         compiler_params=params,
         cost_estimate=cost(2 * sections * nodes * hub_rows * width),
         name="hub_backward",
-    )(count, dst, hub_ids, adj, *turned)
+    )(tile_at, hub_ids, adj, *turned)
     came = across(odd, "row", n_row, 1)
     output, self_grad = pl.pallas_call(
-        functools.partial(self_kernel, **sizes),
-        in_specs=[SMEM] * 2 + [VMEM] * (1 + 2 * len(outs)),
+        functools.partial(self_kernel, tile=tile),
+        in_specs=[SMEM] + [VMEM] * (1 + 2 * len(outs)),
         out_specs=[HBM, VMEM],
-        scratch_shapes=tables + [pltpu.SemaphoreType.DMA((tiles,))],
+        scratch_shapes=[pltpu.SemaphoreType.DMA((tiles,))],
         out_shape=[shape((nodes, out_width), BF16), shape((nodes, width), F32)],
         compiler_params=params,
         name="self",
-    )(count, dst, w_self, *outs, *grads)
+    )(tile_at, w_self, *outs, *grads)
     block = shape((width, hub_rows), BF16)
     sums = pl.pallas_call(
         pair_add_kernel,

time: 51.6 us -> 44 us (0.85)
  waiting for transfers between devices: 13.5 us -> 1.72 us
  starting transfers between devices: 18.3 us -> 23.2 us
  Pallas kernels: 18.6 us -> 16.8 us
  local copies, waits for them, and re-layouts: 0.05 us -> 1.27 us
    ppermute x14, waiting for transfers between devices: 13.5 us -> 1.72 us  [across(): return lax.ppermute(x, axis, [(i, i ^ d) for i in range(size)])]
    ppermute x14, starting transfers between devices: 18.3 us -> 23.2 us  [across(): return lax.ppermute(x, axis, [(i, i ^ d) for i in range(size)])]
    pallas_call x4, Pallas kernels: 11.3 us -> 9.89 us  [the longest x1 3.73 us: shards(): pl.pallas_call(functools.partial(forward_kernel, tile=tile, chunk=256, gr...]
    unnamed x20 -> x24, local copies, waits for them, and re-layouts: 0.05 us -> 1.27 us
  transfers between devices with their start and end apart: 14 -> 14, of which waited for: 6 -> 2; matrix products, arithmetic and copies ran while one was open for 0% -> 0% of each run, Pallas kernels for 21% -> 21%
where the time goes in v3:
time: 44 us; the launch traced here: 43.9 us
  starting transfers between devices  23.2 us (53%)
  Pallas kernels  16.8 us (38%)
  waiting for transfers between devices  1.72 us (4%)
  local copies, waits for them, and re-layouts  1.27 us (3%)
  between operations  0.88 us (2%)
    ppermute x14, starting transfers between devices, across(): return lax.ppermute(x, axis, [(i, i ^ d) for i in range(size)])  23.2 us
    pallas_call x1, Pallas kernels, shards(): pl.pallas_call(functools.partial(forward_kernel, tile=tile, chunk=256, gr...  3.73 us
    pallas_call x1, Pallas kernels, shards(): pl.pallas_call(functools.partial(hub_backward_kernel, tile=tile), in_spec...  2.63 us
    pallas_call x1, Pallas kernels, shards(): pl.pallas_call(functools.partial(pick_kernel, tile=tile), in_specs=[SMEM,...  2.08 us
    pallas_call x1, Pallas kernels, shards(): pl.pallas_call(functools.partial(landed_kernel, group=group, **sizes), in...  2.07 us
    pallas_call x1, Pallas kernels, shards(): pl.pallas_call(functools.partial(self_kernel, tile=tile), in_specs=[SMEM]...  1.98 us
    pallas_call x1, Pallas kernels, shards(): pl.pallas_call(functools.partial(tiles_kernel, chunk=chunk, **sizes), in_...  1.79 us
    ppermute x14, waiting for transfers between devices, across(): return lax.ppermute(x, axis, [(i, i ^ d) for i in range(size)])  1.72 us
  transfers between devices with their start and end apart: 14, of which 2 were waited for; matrix products, arithmetic and copies ran while one was open for 0% of the time, Pallas kernels for 21%

profile of v3, /device:TPU:0, one launch (start us, length us, event | category | flops | bytes accessed | tf_op | source)
XLA Modules:
  0.0 43.9 jit_solution(11375497613698777399)
XLA Ops:
  0.6 0.0 copy-start.3
  0.7 2.1 %pick.1 = (bf16[256,256]{1,0:T(8,128)(2,1)S(1)}, bf16[2,128,256]{2,1,0:T(8,128)(2,1)S(1)}, bf16[2,128,256]{2,1,0:T(8,128)(2,1)S(1)}, bf16[2,128,256]{2,1,0:T(8,128)(2,1)S(1)}, bf16[2,128,256]{2,1,0:T(8,128)(2,1)S(1)}) custom-call(s32[2,4]{1,0:T(2,128)} %bitcast.21, bf16[2048,256]{1,0:T(8,128)(2,1)} %feats.3), custom_call_target="tpu_custom_call" | custom-call | flops 1000000000 | tf_op jit(solution)/shard_map/pick/pallas_call | solution.py:260
  2.8 4.0 %collective-permute-start.2 = (bf16[256,256]{1,0:T(8,128)(2,1)S(1)}, bf16[256,256]{1,0:T(8,128)(2,1)S(1)}, u32[]{:S(2)}, u32[]{:S(2)}) collective-permute-start(bf16[256,256]{1,0:T(8,128)(2,1)S(1)} %get-tuple-element.34), channel_id=1, source_target_pairs={{0,24},{4,28},{8,16},{12,20},{16,8},{20,12},{24,0},{28,4},{1,25},{... | collective-permute-start | bytes 393224 | tf_op jit(solution)/shard_map/ppermute | solution.py:256
  6.8 0.5 %collective-permute-start.1 = (bf16[256,256]{1,0:T(8,128)(2,1)S(1)}, bf16[256,256]{1,0:T(8,128)(2,1)S(1)}, u32[]{:S(2)}, u32[]{:S(2)}) collective-permute-start(bf16[256,256]{1,0:T(8,128)(2,1)S(1)} %get-tuple-element.34), channel_id=1, source_target_pairs={{0,16},{4,20},{8,24},{12,28},{16,0},{20,4},{24,8},{28,12},{1,17},{... | collective-permute-start | bytes 393224 | tf_op jit(solution)/shard_map/ppermute | solution.py:256
  7.3 0.1 collective-permute-start
  7.4 2.0 %collective-permute-start.4 = (bf16[2,128,256]{2,1,0:T(8,128)(2,1)S(1)}, bf16[2,128,256]{2,1,0:T(8,128)(2,1)S(1)}, u32[]{:S(2)}, u32[]{:S(2)}) collective-permute-start(bf16[2,128,256]{2,1,0:T(8,128)(2,1)S(1)} %get-tuple-element.39), channel_id=1, source_target_pairs={{0,1},{1,0},{2,3},{3,2},{4,5},{5,4},{6,7},{7,6},{8,9},{9,8},{10,11... | collective-permute-start | bytes 393224 | tf_op jit(solution)/shard_map/ppermute | solution.py:256
  9.4 2.6 %collective-permute-start.5 = (bf16[2,128,256]{2,1,0:T(8,128)(2,1)S(1)}, bf16[2,128,256]{2,1,0:T(8,128)(2,1)S(1)}, u32[]{:S(2)}, u32[]{:S(2)}) collective-permute-start(bf16[2,128,256]{2,1,0:T(8,128)(2,1)S(1)} %get-tuple-element.40), channel_id=1, source_target_pairs={{0,2},{1,3},{2,0},{3,1},{4,6},{5,7},{6,4},{7,5},{8,10},{9,11},{10,... | collective-permute-start | bytes 393224 | tf_op jit(solution)/shard_map/ppermute | solution.py:256
  12.0 0.0 collective-permute-done.2
  12.0 2.4 %collective-permute-start.6 = (bf16[2,128,256]{2,1,0:T(8,128)(2,1)S(1)}, bf16[2,128,256]{2,1,0:T(8,128)(2,1)S(1)}, u32[]{:S(2)}, u32[]{:S(2)}) collective-permute-start(bf16[2,128,256]{2,1,0:T(8,128)(2,1)S(1)} %get-tuple-element.41), channel_id=1, source_target_pairs={{0,3},{1,2},{2,1},{3,0},{4,7},{5,6},{6,5},{7,4},{8,11},{9,10},{10,... | collective-permute-start | bytes 393224 | tf_op jit(solution)/shard_map/ppermute | solution.py:256
  14.4 0.0 collective-permute-done.1
  14.4 0.0 collective-permute-done
  14.4 0.1 pad_maximum_fusion.same
  14.5 0.1 collective-permute-start.3
  14.6 0.0 slice-start
  14.6 0.0 slice-start.1
  14.6 0.0 copy-start
  14.7 0.0 copy-start.1
  14.7 0.0 copy-start.4
  14.7 1.5 %early.1 = (s32[16]{0:T(128)S(1)}, s32[16]{0:T(128)S(1)}, f32[2048,256]{1,0:T(8,128)S(1)}) custom-call(s32[1,4]{1,0:T(1,128)S(1)} %copy-done.7, s32[2,4]{1,0:T(2,128)S(1)} %bitcast.19, bf16[2048,256]{1,0:T(8,128)(2,1)S(1)} %copy-done.8, bf16[256,256]{1,0:T(8,128)(2,1)S(1)} %copy-done.3, f32[1,256]{1,0:T(1,128)S(1)} %bitcast.23), custom_call_target="tpu_custom_call" | custom-call | flops 10000000000 | tf_op jit(solution)/shard_map/early/pallas_call | solution.py:276
  16.2 0.2 collective-permute-done.3.other
  16.5 0.3 slice-done
  16.8 0.7 %slice-done.1 = s8[2097152]{0:T(1024)(128)(4,1)S(1)} async-done(((s8[6291456]{0:T(1024)(128)(4,1)}), s8[2097152]{0:T(1024)(128)(4,1)S(1)}, s32[]{:S(2)}) %slice-start.1) | async-done | bytes 2097176
  17.5 0.2 copy-done
  17.7 3.7 %forward.1 = (f32[2048,256]{1,0:T(8,128)S(1)}, f32[2048,128]{1,0:T(8,128)S(1)}, bf16[1024,256]{1,0:T(8,128)(2,1)S(1)}, bf16[1024,256]{1,0:T(8,128)(2,1)S(1)}, bf16[256,1024]{1,0:T(8,128)(2,1)S(1)}) custom-call(s32[16]{0:T(128)S(1)} %get-tuple-element.32.order, s32[6]{0:T(128)S(1)} %copy-done.4, bf16[6,2048,256]{2,1,0:T(8,128)(2,1)S(1)} %bitcast.15, ...), custom_call_target="tpu_custom_call" | custom-call | flops 1610612736 | bytes 4194304 | tf_op jit(solution)/shard_map/forward/pallas_call | solution.py:291
  21.4 0.0 collective-permute-done.4.rest_1_
  21.4 0.0 collective-permute-done.5.rest_2_
  21.5 0.0 collective-permute-done.6.rest_3_
  21.5 2.1 %landed.1 = (bf16[1024,256]{1,0:T(8,128)(2,1)S(1)}, bf16[1024,256]{1,0:T(8,128)(2,1)S(1)}, bf16[256,1024]{1,0:T(8,128)(2,1)S(1)}, bf16[2,128,256]{2,1,0:T(8,128)...) custom-call(s32[1,4]{1,0:T(1,128)S(1)} %copy-done.7, ...), custom_call_target="tpu_custom_call" | custom-call | tf_op jit(solution)/shard_map/landed/pallas_call | solution.py:301
  23.6 2.6 %hub_backward.1 = (bf16[4,256,256]{2,1,0:T(8,128)(2,1)S(1)}, bf16[4,256,256]{2,1,0:T(8,128)(2,1)S(1)}) custom-call(s32[16]{0:T(128)S(1)} %get-tuple-element.32.order, s32[6]{0:T(128)S(1)} %copy-done.4, bf16[6,2048,256]{2,1,0:T(8,128)(2,1)S(1)} %bitcast.16, bf16[256,1024]{1,0:T(8,128)(2,1)S(1)} %get-tuple-element.53.rest_0_, ...), custom_call_target="tpu_custom_call" | custom-call | flops 1610612736 | bytes 4194304 | tf_op jit(solution)/shard_map/hub_backward/pallas_call | solution.py:317
  26.2 0.0 copy-start.6
  26.2 0.6 %collective-permute-start.10 = (bf16[4,256,256]{2,1,0:T(8,128)(2,1)S(1)}, bf16[4,256,256]{2,1,0:T(8,128)(2,1)S(1)}, u32[]{:S(2)}, u32[]{:S(2)}) collective-permute-start(bf16[4,256,256]{2,1,0:T(8,128)(2,1)S(1)} %get-tuple-element.56), channel_id=1, source_target_pairs={{0,4},{4,0},{8,12},{12,8},{16,20},{20,16},{24,28},{28,24},{1,5},{5... | collective-permute-start | bytes 1572872 | tf_op jit(solution)/shard_map/ppermute | solution.py:256
  26.8 1.5 %collective-permute-start.7 = (bf16[2,128,256]{2,1,0:T(8,128)(2,1)S(1)}, bf16[2,128,256]{2,1,0:T(8,128)(2,1)S(1)}, u32[]{:S(2)}, u32[]{:S(2)}) collective-permute-start(bf16[2,128,256]{2,1,0:T(8,128)(2,1)S(1)} %get-tuple-element.49), channel_id=1, source_target_pairs={{0,1},{1,0},{2,3},{3,2},{4,5},{5,4},{6,7},{7,6},{8,9},{9,8},{10,11... | collective-permute-start | bytes 393224 | tf_op jit(solution)/shard_map/ppermute | solution.py:256
  28.3 1.5 %collective-permute-start.8 = (bf16[2,128,256]{2,1,0:T(8,128)(2,1)S(1)}, bf16[2,128,256]{2,1,0:T(8,128)(2,1)S(1)}, u32[]{:S(2)}, u32[]{:S(2)}) collective-permute-start(bf16[2,128,256]{2,1,0:T(8,128)(2,1)S(1)} %get-tuple-element.50), channel_id=1, source_target_pairs={{0,2},{1,3},{2,0},{3,1},{4,6},{5,7},{6,4},{7,5},{8,10},{9,11},{10,... | collective-permute-start | bytes 393224 | tf_op jit(solution)/shard_map/ppermute | solution.py:256
  29.8 1.3 %collective-permute-start.9 = (bf16[2,128,256]{2,1,0:T(8,128)(2,1)S(1)}, bf16[2,128,256]{2,1,0:T(8,128)(2,1)S(1)}, u32[]{:S(2)}, u32[]{:S(2)}) collective-permute-start(bf16[2,128,256]{2,1,0:T(8,128)(2,1)S(1)} %get-tuple-element.51), channel_id=1, source_target_pairs={{0,3},{1,2},{2,1},{3,0},{4,7},{5,6},{6,5},{7,4},{8,11},{9,10},{10,... | collective-permute-start | bytes 393224 | tf_op jit(solution)/shard_map/ppermute | solution.py:256
  31.1 0.0 collective-permute-done.10.came
  31.1 0.1 pair_add.1
  31.3 2.3 %collective-permute-start.11 = (bf16[256,256]{1,0:T(8,128)(2,1)S(1)}, bf16[256,256]{1,0:T(8,128)(2,1)S(1)}, u32[]{:S(2)}, u32[]{:S(2)}) collective-permute-start(bf16[256,256]{1,0:T(8,128)(2,1)S(1)} %get-tuple-element.58), channel_id=1, source_target_pairs={{0,8},{4,12},{8,0},{12,4},{16,24},{20,28},{24,16},{28,20},{1,9},{5... | collective-permute-start | bytes 393224 | tf_op jit(solution)/shard_map/ppermute | solution.py:256
  33.6 1.5 %collective-permute-start.12 = (bf16[256,256]{1,0:T(8,128)(2,1)S(1)}, bf16[256,256]{1,0:T(8,128)(2,1)S(1)}, u32[]{:S(2)}, u32[]{:S(2)}) collective-permute-start(bf16[256,256]{1,0:T(8,128)(2,1)S(1)} %get-tuple-element.59), channel_id=1, source_target_pairs={{0,16},{4,20},{8,24},{12,28},{16,0},{20,4},{24,8},{28,12},{1,17},{... | collective-permute-start | bytes 393224 | tf_op jit(solution)/shard_map/ppermute | solution.py:256
  35.1 0.0 collective-permute-done.7.rest_1_
  35.1 2.7 %collective-permute-start.13 = (bf16[256,256]{1,0:T(8,128)(2,1)S(1)}, bf16[256,256]{1,0:T(8,128)(2,1)S(1)}, u32[]{:S(2)}, u32[]{:S(2)}) collective-permute-start(bf16[256,256]{1,0:T(8,128)(2,1)S(1)} %get-tuple-element.60), channel_id=1, source_target_pairs={{0,24},{4,28},{8,16},{12,20},{16,8},{20,12},{24,0},{28,4},{1,25},{... | collective-permute-start | bytes 393224 | tf_op jit(solution)/shard_map/ppermute | solution.py:256
  37.8 2.0 %self.1 = (bf16[2048,256]{1,0:T(8,128)(2,1)}, f32[2048,256]{1,0:T(8,128)S(1)}) custom-call(s32[16]{0:T(128)S(1)} %get-tuple-element.32.order, bf16[256,256]{1,0:T(8,128)(2,1)S(1)} %copy-done.3, bf16[1024,256]{1,0:T(8,128)(2,1)S(1)} %get-tuple-element.42.rest_0_, bf16[1024,256]{1,0:T(8,128)(2,1)S(1)} %get-tuple-element.43.rest_1_, ...), custom_call_target="tpu_custom_call" | custom-call | tf_op jit(solution)/shard_map/self/pallas_call | solution.py:328
  39.8 1.4 %collective-permute-done.8.rest_2_ = bf16[2,128,256]{2,1,0:T(8,128)(2,1)S(1)} collective-permute-done((bf16[2,128,256]{2,1,0:T(8,128)(2,1)S(1)}, bf16[2,128,256]{2,1,0:T(8,128)(2,1)S(1)}, u32[]{:S(2)}, u32[]{:S(2)}) %collective-permute-start.8) | collective-permute-done | bytes 131104 | tf_op jit(solution)/shard_map/ppermute | solution.py:256
  41.2 0.0 collective-permute-done.9.rest_3_
  41.2 1.8 %tiles_done.1 = (bf16[2048,256]{1,0:T(8,128)(2,1)}, f32[256,256]{1,0:T(8,128)S(1)}) custom-call(s32[2,4]{1,0:T(2,128)S(1)} %bitcast.22, f32[2048,256]{1,0:T(8,128)S(1)} %get-tuple-element.47.self_grad, bf16[2,128,256]{2,1,0:T(8,128)(2,1)S(1)} %get-tuple-element.48.rest_0_, bf16[2,128,256]{2,1,0:T(8,128)(2,1)S(1)} %collective-permute-done.7.rest_1_, ...), custom_call_target="tpu_custom_call" | custom-call | tf_op jit(solution)/shard_map/tiles_done/pallas_call | solution.py:347
  43.0 0.0 collective-permute-done.11.rest_1_
  43.0 0.0 collective-permute-done.12.rest_2_
  43.1 0.0 collective-permute-done.13.rest_3_
  43.1 0.8 %head.1 = bf16[2048,256]{1,0:T(8,128)(2,1)} custom-call(f32[256,256]{1,0:T(8,128)S(1)} %get-tuple-element.52.head, bf16[256,256]{1,0:T(8,128)(2,1)S(1)} %get-tuple-element.57.rest_0_, bf16[256,256]{1,0:T(8,128)(2,1)S(1)} %collective-permute-done.11.rest_1_, bf16[256,256]{1,0:T(8,128)(2,1)S(1)} %collective-permute-done.12.rest_2_, ...), custom_call_target="tpu_custom_call", output_to_operand_aliasing={{}: (5, {})} | custom-call | tf_op jit(solution)/shard_map/head/pallas_call | solution.py:360
  (15 shorter events, 0.0 us)
Async XLA Ops:
  0.6 14.0 %copy-start.3 = (bf16[256,256]{1,0:T(8,128)(2,1)S(1)}, bf16[256,256]{1,0:T(8,128)(2,1)}, u32[]{:S(2)}) copy-start(bf16[256,256]{1,0:T(8,128)(2,1)} %w_self.3) | copy-start | bytes 393220
  0.6 14.0 %copy-start.5 = (s32[1,4,2]{1,2,0:T(2,128)S(1)}, s32[1,4,2]{1,2,0:T(2,128)}, u32[]{:S(2)}) copy-start(s32[1,4,2]{1,2,0:T(2,128)} %param.19) | copy-start | bytes 100
  0.7 14.0 %copy-start.7 = (s32[1,4]{1,0:T(1,128)S(1)}, s32[1,4]{1,0:T(1,128)}, u32[]{:S(2)}) copy-start(s32[1,4]{1,0:T(1,128)} %count.3) | copy-start | bytes 52
  0.7 14.0 %copy-start.8 = (bf16[2048,256]{1,0:T(8,128)(2,1)S(1)}, bf16[2048,256]{1,0:T(8,128)(2,1)}, u32[]{:S(2)}) copy-start(bf16[2048,256]{1,0:T(8,128)(2,1)} %feats.3) | copy-start | bytes 3145732
  0.7 14.0 %copy-start.9 = (f32[256]{0:T(256)S(1)}, f32[256]{0:T(256)}, u32[]{:S(2)}) copy-start(f32[256]{0:T(256)} %param.14) | copy-start | bytes 3076
  2.8 9.2 %collective-permute-start.2 = (bf16[256,256]{1,0:T(8,128)(2,1)S(1)}, bf16[256,256]{1,0:T(8,128)(2,1)S(1)}, u32[]{:S(2)}, u32[]{:S(2)}) collective-permute-start(bf16[256,256]{1,0:T(8,128)(2,1)S(1)} %get-tuple-element.34), channel_id=1, source_target_pairs={{0,24},{4,28},{8,16},{12,20},{16,8},{20,12},{24,0},{28,4},{1,25},{... | collective-permute-start | bytes 393224 | tf_op jit(solution)/shard_map/ppermute | solution.py:256
  6.8 7.7 %collective-permute-start.1 = (bf16[256,256]{1,0:T(8,128)(2,1)S(1)}, bf16[256,256]{1,0:T(8,128)(2,1)S(1)}, u32[]{:S(2)}, u32[]{:S(2)}) collective-permute-start(bf16[256,256]{1,0:T(8,128)(2,1)S(1)} %get-tuple-element.34), channel_id=1, source_target_pairs={{0,16},{4,20},{8,24},{12,28},{16,0},{20,4},{24,8},{28,12},{1,17},{... | collective-permute-start | bytes 393224 | tf_op jit(solution)/shard_map/ppermute | solution.py:256
  7.3 7.2 %collective-permute-start = (bf16[256,256]{1,0:T(8,128)(2,1)S(1)}, bf16[256,256]{1,0:T(8,128)(2,1)S(1)}, u32[]{:S(2)}, u32[]{:S(2)}) collective-permute-start(bf16[256,256]{1,0:T(8,128)(2,1)S(1)} %get-tuple-element.34), channel_id=1, source_target_pairs={{0,8},{4,12},{8,0},{12,4},{16,24},{20,28},{24,16},{28,20},{1,9},{5... | collective-permute-start | bytes 393224 | tf_op jit(solution)/shard_map/ppermute | solution.py:256
  7.4 14.0 %collective-permute-start.4 = (bf16[2,128,256]{2,1,0:T(8,128)(2,1)S(1)}, bf16[2,128,256]{2,1,0:T(8,128)(2,1)S(1)}, u32[]{:S(2)}, u32[]{:S(2)}) collective-permute-start(bf16[2,128,256]{2,1,0:T(8,128)(2,1)S(1)} %get-tuple-element.39), channel_id=1, source_target_pairs={{0,1},{1,0},{2,3},{3,2},{4,5},{5,4},{6,7},{7,6},{8,9},{9,8},{10,11... | collective-permute-start | bytes 393224 | tf_op jit(solution)/shard_map/ppermute | solution.py:256
  9.4 12.1 %collective-permute-start.5 = (bf16[2,128,256]{2,1,0:T(8,128)(2,1)S(1)}, bf16[2,128,256]{2,1,0:T(8,128)(2,1)S(1)}, u32[]{:S(2)}, u32[]{:S(2)}) collective-permute-start(bf16[2,128,256]{2,1,0:T(8,128)(2,1)S(1)} %get-tuple-element.40), channel_id=1, source_target_pairs={{0,2},{1,3},{2,0},{3,1},{4,6},{5,7},{6,4},{7,5},{8,10},{9,11},{10,... | collective-permute-start | bytes 393224 | tf_op jit(solution)/shard_map/ppermute | solution.py:256
  12.0 9.5 %collective-permute-start.6 = (bf16[2,128,256]{2,1,0:T(8,128)(2,1)S(1)}, bf16[2,128,256]{2,1,0:T(8,128)(2,1)S(1)}, u32[]{:S(2)}, u32[]{:S(2)}) collective-permute-start(bf16[2,128,256]{2,1,0:T(8,128)(2,1)S(1)} %get-tuple-element.41), channel_id=1, source_target_pairs={{0,3},{1,2},{2,1},{3,0},{4,7},{5,6},{6,5},{7,4},{8,11},{9,10},{10,... | collective-permute-start | bytes 393224 | tf_op jit(solution)/shard_map/ppermute | solution.py:256
  14.5 2.0 %collective-permute-start.3 = (bf16[4,256,256]{2,1,0:T(8,128)(2,1)S(1)}, bf16[4,256,256]{2,1,0:T(8,128)(2,1)S(1)}, u32[]{:S(2)}, u32[]{:S(2)}) collective-permute-start(bf16[4,256,256]{2,1,0:T(8,128)(2,1)S(1)} %pad_maximum_fusion.same), channel_id=1, source_target_pairs={{0,4},{4,0},{8,12},{12,8},{16,20},{20,16},{24,28},{28,24},{1,5},{5... | collective-permute-start | bytes 1572872 | tf_op jit(solution)/shard_map/ppermute | solution.py:256
  14.6 2.2 %slice-start = ((s8[6291456]{0:T(1024)(128)(4,1)}), s8[4194304]{0:T(1024)(128)(4,1)S(1)}, s32[]{:S(2)}) async-start(s8[6291456]{0:T(1024)(128)(4,1)} %bitcast.13), calls=%async_computation | async-start | bytes 8388608
  14.6 2.8 %slice-start.1 = ((s8[6291456]{0:T(1024)(128)(4,1)}), s8[2097152]{0:T(1024)(128)(4,1)S(1)}, s32[]{:S(2)}) async-start(s8[6291456]{0:T(1024)(128)(4,1)} %bitcast.13), calls=%async_computation.1 | async-start | bytes 4194304
  14.6 3.0 %copy-start = (bf16[2048,256]{1,0:T(8,128)(2,1)S(1)}, bf16[2048,256]{1,0:T(8,128)(2,1)}, u32[]{:S(2)}) copy-start(bf16[2048,256]{1,0:T(8,128)(2,1)} %cot.3) | copy-start | bytes 3145732
  14.7 3.0 %copy-start.1 = (bf16[256,256]{1,0:T(8,128)(2,1)S(1)}, bf16[256,256]{1,0:T(8,128)(2,1)}, u32[]{:S(2)}) copy-start(bf16[256,256]{1,0:T(8,128)(2,1)} %w_neigh.3) | copy-start | bytes 393220
  14.7 3.0 %copy-start.4 = (s32[6]{0:T(128)S(1)}, s32[6]{0:T(128)}, u32[]{:S(2)}) copy-start(s32[6]{0:T(128)} %hub_ids.3) | copy-start | bytes 76
  17.7 3.8 %copy-start.2 = (bf16[1,4,2,128,128]{4,3,2,1,0:T(8,128)(2,1)S(1)}, bf16[1,4,2,128,128]{4,3,2,1,0:T(8,128)(2,1)}, u32[]{:S(2)}) copy-start(bf16[1,4,2,128,128]{4,3,2,1,0:T(8,128)(2,1)} %param.20) | copy-start | bytes 786436
  26.2 15.0 %copy-start.6 = (s32[1,4,2]{1,2,0:T(2,128)S(1)}, s32[1,4,2]{1,2,0:T(2,128)}, u32[]{:S(2)}) copy-start(s32[1,4,2]{1,2,0:T(2,128)} %param.17) | copy-start | bytes 100
  26.2 4.9 %collective-permute-start.10 = (bf16[4,256,256]{2,1,0:T(8,128)(2,1)S(1)}, bf16[4,256,256]{2,1,0:T(8,128)(2,1)S(1)}, u32[]{:S(2)}, u32[]{:S(2)}) collective-permute-start(bf16[4,256,256]{2,1,0:T(8,128)(2,1)S(1)} %get-tuple-element.56), channel_id=1, source_target_pairs={{0,4},{4,0},{8,12},{12,8},{16,20},{20,16},{24,28},{28,24},{1,5},{5... | collective-permute-start | bytes 1572872 | tf_op jit(solution)/shard_map/ppermute | solution.py:256
  26.8 8.4 %collective-permute-start.7 = (bf16[2,128,256]{2,1,0:T(8,128)(2,1)S(1)}, bf16[2,128,256]{2,1,0:T(8,128)(2,1)S(1)}, u32[]{:S(2)}, u32[]{:S(2)}) collective-permute-start(bf16[2,128,256]{2,1,0:T(8,128)(2,1)S(1)} %get-tuple-element.49), channel_id=1, source_target_pairs={{0,1},{1,0},{2,3},{3,2},{4,5},{5,4},{6,7},{7,6},{8,9},{9,8},{10,11... | collective-permute-start | bytes 393224 | tf_op jit(solution)/shard_map/ppermute | solution.py:256
  28.3 12.9 %collective-permute-start.8 = (bf16[2,128,256]{2,1,0:T(8,128)(2,1)S(1)}, bf16[2,128,256]{2,1,0:T(8,128)(2,1)S(1)}, u32[]{:S(2)}, u32[]{:S(2)}) collective-permute-start(bf16[2,128,256]{2,1,0:T(8,128)(2,1)S(1)} %get-tuple-element.50), channel_id=1, source_target_pairs={{0,2},{1,3},{2,0},{3,1},{4,6},{5,7},{6,4},{7,5},{8,10},{9,11},{10,... | collective-permute-start | bytes 393224 | tf_op jit(solution)/shard_map/ppermute | solution.py:256
  29.8 11.4 %collective-permute-start.9 = (bf16[2,128,256]{2,1,0:T(8,128)(2,1)S(1)}, bf16[2,128,256]{2,1,0:T(8,128)(2,1)S(1)}, u32[]{:S(2)}, u32[]{:S(2)}) collective-permute-start(bf16[2,128,256]{2,1,0:T(8,128)(2,1)S(1)} %get-tuple-element.51), channel_id=1, source_target_pairs={{0,3},{1,2},{2,1},{3,0},{4,7},{5,6},{6,5},{7,4},{8,11},{9,10},{10,... | collective-permute-start | bytes 393224 | tf_op jit(solution)/shard_map/ppermute | solution.py:256
  31.3 11.8 %collective-permute-start.11 = (bf16[256,256]{1,0:T(8,128)(2,1)S(1)}, bf16[256,256]{1,0:T(8,128)(2,1)S(1)}, u32[]{:S(2)}, u32[]{:S(2)}) collective-permute-start(bf16[256,256]{1,0:T(8,128)(2,1)S(1)} %get-tuple-element.58), channel_id=1, source_target_pairs={{0,8},{4,12},{8,0},{12,4},{16,24},{20,28},{24,16},{28,20},{1,9},{5... | collective-permute-start | bytes 393224 | tf_op jit(solution)/shard_map/ppermute | solution.py:256
  33.6 9.4 %collective-permute-start.12 = (bf16[256,256]{1,0:T(8,128)(2,1)S(1)}, bf16[256,256]{1,0:T(8,128)(2,1)S(1)}, u32[]{:S(2)}, u32[]{:S(2)}) collective-permute-start(bf16[256,256]{1,0:T(8,128)(2,1)S(1)} %get-tuple-element.59), channel_id=1, source_target_pairs={{0,16},{4,20},{8,24},{12,28},{16,0},{20,4},{24,8},{28,12},{1,17},{... | collective-permute-start | bytes 393224 | tf_op jit(solution)/shard_map/ppermute | solution.py:256
  35.1 7.9 %collective-permute-start.13 = (bf16[256,256]{1,0:T(8,128)(2,1)S(1)}, bf16[256,256]{1,0:T(8,128)(2,1)S(1)}, u32[]{:S(2)}, u32[]{:S(2)}) collective-permute-start(bf16[256,256]{1,0:T(8,128)(2,1)S(1)} %get-tuple-element.60), channel_id=1, source_target_pairs={{0,24},{4,28},{8,16},{12,20},{16,8},{20,12},{24,0},{28,4},{1,25},{... | collective-permute-start | bytes 393224 | tf_op jit(solution)/shard_map/ppermute | solution.py:256

commit v4 on v3

--- a/solution.py
+++ b/solution.py
@@ -21,20 +21,24 @@
     return pl.ds(pl.multiple_of(index * size, size), size)
 
 
-def pick_kernel(send, feats, hub, *rest, tile):
-    outs, sems = rest[:-1], rest[-1]
+def pick_kernel(send_in, feats_in, feats, hub, *rest):
+    outs, (send, sems) = rest[:-2], rest[-2:]
     col = lax.axis_index("col")
-    slots = outs[0].shape[0]
-    copies = []
-    for d, out in enumerate(outs):
-        for k in range(slots):
-            at = rows_at(send[k, col ^ d], tile)
-            copies.append(pltpu.make_async_copy(feats.at[at], out.at[k], sems.at[d * slots + k]))
-    copies.append(pltpu.make_async_copy(feats.at[pl.ds(0, hub.shape[0])], hub, sems.at[len(copies)]))
+    slots, tile, _ = outs[0].shape
+    parts = sems.shape[0] - 1
+    rows = feats.shape[0] // parts
+    copies = [pltpu.make_async_copy(send_in, send, sems.at[parts])]
+    for i in range(parts):
+        at = pl.ds(i * rows, rows)
+        copies.append(pltpu.make_async_copy(feats_in.at[at], feats.at[at], sems.at[i]))
     for copy in copies:
         copy.start()
     for copy in copies:
         copy.wait()
+    hub[...] = feats[pl.ds(0, hub.shape[0]), :]
+    for d, out in enumerate(outs):
+        for k in range(slots):
+            out[k] = feats[rows_at(send[k, col ^ d], tile), :]
 
 
 def tile_order(count, dst, order, place, *, peers, slots, tiles):
@@ -257,12 +261,12 @@
 
     order = exchange_order(n_col)
     pair = shape((slots, tile, width), BF16)
-    own_hub, *picked = pl.pallas_call(
-        functools.partial(pick_kernel, tile=tile),
-        in_specs=[SMEM, HBM],
-        out_specs=[VMEM] * (peers + 1),
-        scratch_shapes=[pltpu.SemaphoreType.DMA((peers * slots + 1,))],
-        out_shape=[shape((hub_rows, width), BF16)] + [pair] * peers,
+    feats, own_hub, *picked = pl.pallas_call(
+        pick_kernel,
+        in_specs=[HBM, HBM],
+        out_specs=[VMEM] * (peers + 2),
+        scratch_shapes=[pltpu.SMEM(send.shape, jnp.int32), pltpu.SemaphoreType.DMA((5,))],
+        out_shape=[shape((nodes, width), BF16), shape((hub_rows, width), BF16)] + [pair] * peers,
         compiler_params=params,
         cost_estimate=pl.CostEstimate(flops=1000000000, transcendentals=0, bytes_accessed=0),
         name="pick",
@@ -281,7 +285,7 @@
         compiler_params=params,
         cost_estimate=pl.CostEstimate(flops=10000000000, transcendentals=0, bytes_accessed=0),
         name="early",
-    )(count, dst, features, w_self, bias)
+    )(count, dst, feats, w_self, bias)
 
     def results(number):
         if not number:

time: 44 us -> 43.3 us (0.984)
  Pallas kernels: 16.8 us -> 16 us
    pallas_call x1, Pallas kernels: 2.08 us -> 1.34 us  [shards(): pl.pallas_call(pick_kernel, in_specs=[HBM, HBM], out_specs=[VMEM] * (peer...]
    unnamed x24 -> x22, local copies, waits for them, and re-layouts: 1.27 us -> 1.26 us
where the time goes in v4:
time: 43.3 us; the launch traced here: 43.1 us
  starting transfers between devices  23.2 us (54%)
  Pallas kernels  16 us (37%)
  waiting for transfers between devices  1.77 us (4%)
  local copies, waits for them, and re-layouts  1.26 us (3%)
  between operations  0.86 us (2%)
    ppermute x14, starting transfers between devices, across(): return lax.ppermute(x, axis, [(i, i ^ d) for i in range(size)])  23.2 us
    pallas_call x1, Pallas kernels, shards(): pl.pallas_call(functools.partial(forward_kernel, tile=tile, chunk=256, gr...  3.73 us
    pallas_call x1, Pallas kernels, shards(): pl.pallas_call(functools.partial(hub_backward_kernel, tile=tile), in_spec...  2.63 us
    pallas_call x1, Pallas kernels, shards(): pl.pallas_call(functools.partial(landed_kernel, group=group, **sizes), in...  2.07 us
    pallas_call x1, Pallas kernels, shards(): pl.pallas_call(functools.partial(self_kernel, tile=tile), in_specs=[SMEM]...  1.97 us
    pallas_call x1, Pallas kernels, shards(): pl.pallas_call(functools.partial(tiles_kernel, chunk=chunk, **sizes), in_...  1.79 us
    ppermute x14, waiting for transfers between devices, across(): return lax.ppermute(x, axis, [(i, i ^ d) for i in range(size)])  1.77 us
    pallas_call x1, Pallas kernels, shards(): pl.pallas_call(functools.partial(early_kernel, **sizes), in_specs=[SMEM]...  1.55 us
  transfers between devices with their start and end apart: 14, of which 2 were waited for; matrix products, arithmetic and copies ran while one was open for 0% of the time, Pallas kernels for 21%

profile of v4, /device:TPU:0, one launch (start us, length us, event | category | flops | bytes accessed | tf_op | source)
XLA Modules:
  0.0 43.1 jit_solution(14648643199824194645)
XLA Ops:
  0.6 0.0 copy-start.3
  0.7 1.3 %pick.1 = (bf16[2048,256]{1,0:T(8,128)(2,1)S(1)}, bf16[256,256]{1,0:T(8,128)(2,1)S(1)}, bf16[2,128,256]{2,1,0:T(8,128)(2,1)S(1)}, bf16[2,128,256]{2,1,0:T(8,128)...) custom-call(s32[2,4]{1,0:T(2,128)} %bitcast.21, bf16[2048,256]{1,0:T(8,128)(2,1)} %feats_in.1), custom_call_target="tpu_custom_call" | custom-call | flops 1000000000 | tf_op jit(solution)/shard_map/pick/pallas_call | solution.py:264
  2.0 4.0 %collective-permute-start.2 = (bf16[256,256]{1,0:T(8,128)(2,1)S(1)}, bf16[256,256]{1,0:T(8,128)(2,1)S(1)}, u32[]{:S(2)}, u32[]{:S(2)}) collective-permute-start(bf16[256,256]{1,0:T(8,128)(2,1)S(1)} %get-tuple-element.36), channel_id=1, source_target_pairs={{0,24},{4,28},{8,16},{12,20},{16,8},{20,12},{24,0},{28,4},{1,25},{... | collective-permute-start | bytes 393224 | tf_op jit(solution)/shard_map/ppermute | solution.py:260
  6.0 0.5 %collective-permute-start.1 = (bf16[256,256]{1,0:T(8,128)(2,1)S(1)}, bf16[256,256]{1,0:T(8,128)(2,1)S(1)}, u32[]{:S(2)}, u32[]{:S(2)}) collective-permute-start(bf16[256,256]{1,0:T(8,128)(2,1)S(1)} %get-tuple-element.36), channel_id=1, source_target_pairs={{0,16},{4,20},{8,24},{12,28},{16,0},{20,4},{24,8},{28,12},{1,17},{... | collective-permute-start | bytes 393224 | tf_op jit(solution)/shard_map/ppermute | solution.py:260
  6.5 0.1 collective-permute-start
  6.7 2.0 %collective-permute-start.4 = (bf16[2,128,256]{2,1,0:T(8,128)(2,1)S(1)}, bf16[2,128,256]{2,1,0:T(8,128)(2,1)S(1)}, u32[]{:S(2)}, u32[]{:S(2)}) collective-permute-start(bf16[2,128,256]{2,1,0:T(8,128)(2,1)S(1)} %get-tuple-element.41), channel_id=1, source_target_pairs={{0,1},{1,0},{2,3},{3,2},{4,5},{5,4},{6,7},{7,6},{8,9},{9,8},{10,11... | collective-permute-start | bytes 393224 | tf_op jit(solution)/shard_map/ppermute | solution.py:260
  8.6 2.6 %collective-permute-start.5 = (bf16[2,128,256]{2,1,0:T(8,128)(2,1)S(1)}, bf16[2,128,256]{2,1,0:T(8,128)(2,1)S(1)}, u32[]{:S(2)}, u32[]{:S(2)}) collective-permute-start(bf16[2,128,256]{2,1,0:T(8,128)(2,1)S(1)} %get-tuple-element.42), channel_id=1, source_target_pairs={{0,2},{1,3},{2,0},{3,1},{4,6},{5,7},{6,4},{7,5},{8,10},{9,11},{10,... | collective-permute-start | bytes 393224 | tf_op jit(solution)/shard_map/ppermute | solution.py:260
  11.2 0.0 collective-permute-done.2
  11.2 2.4 %collective-permute-start.6 = (bf16[2,128,256]{2,1,0:T(8,128)(2,1)S(1)}, bf16[2,128,256]{2,1,0:T(8,128)(2,1)S(1)}, u32[]{:S(2)}, u32[]{:S(2)}) collective-permute-start(bf16[2,128,256]{2,1,0:T(8,128)(2,1)S(1)} %get-tuple-element.43), channel_id=1, source_target_pairs={{0,3},{1,2},{2,1},{3,0},{4,7},{5,6},{6,5},{7,4},{8,11},{9,10},{10,... | collective-permute-start | bytes 393224 | tf_op jit(solution)/shard_map/ppermute | solution.py:260
  13.7 0.0 collective-permute-done.1
  13.7 0.0 collective-permute-done
  13.7 0.1 pad_maximum_fusion.same
  13.7 0.1 collective-permute-start.3
  13.8 0.0 slice-start
  13.9 0.0 slice-start.1
  13.9 0.0 copy-start
  13.9 0.0 copy-start.1
  13.9 0.0 copy-start.4
  13.9 1.5 %early.1 = (s32[16]{0:T(128)S(1)}, s32[16]{0:T(128)S(1)}, f32[2048,256]{1,0:T(8,128)S(1)}) custom-call(s32[1,4]{1,0:T(1,128)S(1)} %copy-done.7, s32[2,4]{1,0:T(2,128)S(1)} %bitcast.19, bf16[2048,256]{1,0:T(8,128)(2,1)S(1)} %get-tuple-element.33.feats, bf16[256,256]{1,0:T(8,128)(2,1)S(1)} %copy-done.3, f32[1,256]{1,0:T(1,128)S(1)} %bitcast.23), custom_call_target="tpu_custom_call" | custom-call | flops 10000000000 | tf_op jit(solution)/shard_map/early/pallas_call | solution.py:280
  15.5 0.2 collective-permute-done.3.other
  15.7 0.3 slice-done
  16.0 0.7 %slice-done.1 = s8[2097152]{0:T(1024)(128)(4,1)S(1)} async-done(((s8[6291456]{0:T(1024)(128)(4,1)}), s8[2097152]{0:T(1024)(128)(4,1)S(1)}, s32[]{:S(2)}) %slice-start.1) | async-done | bytes 2097176
  16.7 0.2 copy-done
  16.9 3.7 %forward.1 = (f32[2048,256]{1,0:T(8,128)S(1)}, f32[2048,128]{1,0:T(8,128)S(1)}, bf16[1024,256]{1,0:T(8,128)(2,1)S(1)}, bf16[1024,256]{1,0:T(8,128)(2,1)S(1)}, bf16[256,1024]{1,0:T(8,128)(2,1)S(1)}) custom-call(s32[16]{0:T(128)S(1)} %get-tuple-element.34.order, s32[6]{0:T(128)S(1)} %copy-done.4, bf16[6,2048,256]{2,1,0:T(8,128)(2,1)S(1)} %bitcast.15, ...), custom_call_target="tpu_custom_call" | custom-call | flops 1610612736 | bytes 4194304 | tf_op jit(solution)/shard_map/forward/pallas_call | solution.py:295
  20.7 0.0 collective-permute-done.4.rest_1_
  20.7 0.0 collective-permute-done.5.rest_2_
  20.7 0.0 collective-permute-done.6.rest_3_
  20.7 2.1 %landed.1 = (bf16[1024,256]{1,0:T(8,128)(2,1)S(1)}, bf16[1024,256]{1,0:T(8,128)(2,1)S(1)}, bf16[256,1024]{1,0:T(8,128)(2,1)S(1)}, bf16[2,128,256]{2,1,0:T(8,128)...) custom-call(s32[1,4]{1,0:T(1,128)S(1)} %copy-done.7, ...), custom_call_target="tpu_custom_call" | custom-call | tf_op jit(solution)/shard_map/landed/pallas_call | solution.py:305
  22.8 2.6 %hub_backward.1 = (bf16[4,256,256]{2,1,0:T(8,128)(2,1)S(1)}, bf16[4,256,256]{2,1,0:T(8,128)(2,1)S(1)}) custom-call(s32[16]{0:T(128)S(1)} %get-tuple-element.34.order, s32[6]{0:T(128)S(1)} %copy-done.4, bf16[6,2048,256]{2,1,0:T(8,128)(2,1)S(1)} %bitcast.16, bf16[256,1024]{1,0:T(8,128)(2,1)S(1)} %get-tuple-element.55.rest_0_, ...), custom_call_target="tpu_custom_call" | custom-call | flops 1610612736 | bytes 4194304 | tf_op jit(solution)/shard_map/hub_backward/pallas_call | solution.py:321
  25.4 0.0 copy-start.6
  25.4 0.6 %collective-permute-start.10 = (bf16[4,256,256]{2,1,0:T(8,128)(2,1)S(1)}, bf16[4,256,256]{2,1,0:T(8,128)(2,1)S(1)}, u32[]{:S(2)}, u32[]{:S(2)}) collective-permute-start(bf16[4,256,256]{2,1,0:T(8,128)(2,1)S(1)} %get-tuple-element.58), channel_id=1, source_target_pairs={{0,4},{4,0},{8,12},{12,8},{16,20},{20,16},{24,28},{28,24},{1,5},{5... | collective-permute-start | bytes 1572872 | tf_op jit(solution)/shard_map/ppermute | solution.py:260
  26.0 1.5 %collective-permute-start.7 = (bf16[2,128,256]{2,1,0:T(8,128)(2,1)S(1)}, bf16[2,128,256]{2,1,0:T(8,128)(2,1)S(1)}, u32[]{:S(2)}, u32[]{:S(2)}) collective-permute-start(bf16[2,128,256]{2,1,0:T(8,128)(2,1)S(1)} %get-tuple-element.51), channel_id=1, source_target_pairs={{0,1},{1,0},{2,3},{3,2},{4,5},{5,4},{6,7},{7,6},{8,9},{9,8},{10,11... | collective-permute-start | bytes 393224 | tf_op jit(solution)/shard_map/ppermute | solution.py:260
  27.5 1.5 %collective-permute-start.8 = (bf16[2,128,256]{2,1,0:T(8,128)(2,1)S(1)}, bf16[2,128,256]{2,1,0:T(8,128)(2,1)S(1)}, u32[]{:S(2)}, u32[]{:S(2)}) collective-permute-start(bf16[2,128,256]{2,1,0:T(8,128)(2,1)S(1)} %get-tuple-element.52), channel_id=1, source_target_pairs={{0,2},{1,3},{2,0},{3,1},{4,6},{5,7},{6,4},{7,5},{8,10},{9,11},{10,... | collective-permute-start | bytes 393224 | tf_op jit(solution)/shard_map/ppermute | solution.py:260
  29.1 1.3 %collective-permute-start.9 = (bf16[2,128,256]{2,1,0:T(8,128)(2,1)S(1)}, bf16[2,128,256]{2,1,0:T(8,128)(2,1)S(1)}, u32[]{:S(2)}, u32[]{:S(2)}) collective-permute-start(bf16[2,128,256]{2,1,0:T(8,128)(2,1)S(1)} %get-tuple-element.53), channel_id=1, source_target_pairs={{0,3},{1,2},{2,1},{3,0},{4,7},{5,6},{6,5},{7,4},{8,11},{9,10},{10,... | collective-permute-start | bytes 393224 | tf_op jit(solution)/shard_map/ppermute | solution.py:260
  30.4 0.0 collective-permute-done.10.came
  30.4 0.1 pair_add.1
  30.5 2.3 %collective-permute-start.11 = (bf16[256,256]{1,0:T(8,128)(2,1)S(1)}, bf16[256,256]{1,0:T(8,128)(2,1)S(1)}, u32[]{:S(2)}, u32[]{:S(2)}) collective-permute-start(bf16[256,256]{1,0:T(8,128)(2,1)S(1)} %get-tuple-element.60), channel_id=1, source_target_pairs={{0,8},{4,12},{8,0},{12,4},{16,24},{20,28},{24,16},{28,20},{1,9},{5... | collective-permute-start | bytes 393224 | tf_op jit(solution)/shard_map/ppermute | solution.py:260
  32.8 1.5 %collective-permute-start.12 = (bf16[256,256]{1,0:T(8,128)(2,1)S(1)}, bf16[256,256]{1,0:T(8,128)(2,1)S(1)}, u32[]{:S(2)}, u32[]{:S(2)}) collective-permute-start(bf16[256,256]{1,0:T(8,128)(2,1)S(1)} %get-tuple-element.61), channel_id=1, source_target_pairs={{0,16},{4,20},{8,24},{12,28},{16,0},{20,4},{24,8},{28,12},{1,17},{... | collective-permute-start | bytes 393224 | tf_op jit(solution)/shard_map/ppermute | solution.py:260
  34.4 0.0 collective-permute-done.7.rest_1_
  34.4 2.7 %collective-permute-start.13 = (bf16[256,256]{1,0:T(8,128)(2,1)S(1)}, bf16[256,256]{1,0:T(8,128)(2,1)S(1)}, u32[]{:S(2)}, u32[]{:S(2)}) collective-permute-start(bf16[256,256]{1,0:T(8,128)(2,1)S(1)} %get-tuple-element.62), channel_id=1, source_target_pairs={{0,24},{4,28},{8,16},{12,20},{16,8},{20,12},{24,0},{28,4},{1,25},{... | collective-permute-start | bytes 393224 | tf_op jit(solution)/shard_map/ppermute | solution.py:260
  37.0 2.0 %self.1 = (bf16[2048,256]{1,0:T(8,128)(2,1)}, f32[2048,256]{1,0:T(8,128)S(1)}) custom-call(s32[16]{0:T(128)S(1)} %get-tuple-element.34.order, bf16[256,256]{1,0:T(8,128)(2,1)S(1)} %copy-done.3, bf16[1024,256]{1,0:T(8,128)(2,1)S(1)} %get-tuple-element.44.rest_0_, bf16[1024,256]{1,0:T(8,128)(2,1)S(1)} %get-tuple-element.45.rest_1_, ...), custom_call_target="tpu_custom_call" | custom-call | tf_op jit(solution)/shard_map/self/pallas_call | solution.py:332
  39.0 1.5 %collective-permute-done.8.rest_2_ = bf16[2,128,256]{2,1,0:T(8,128)(2,1)S(1)} collective-permute-done((bf16[2,128,256]{2,1,0:T(8,128)(2,1)S(1)}, bf16[2,128,256]{2,1,0:T(8,128)(2,1)S(1)}, u32[]{:S(2)}, u32[]{:S(2)}) %collective-permute-start.8) | collective-permute-done | bytes 131104 | tf_op jit(solution)/shard_map/ppermute | solution.py:260
  40.5 0.0 collective-permute-done.9.rest_3_
  40.5 1.8 %tiles_done.1 = (bf16[2048,256]{1,0:T(8,128)(2,1)}, f32[256,256]{1,0:T(8,128)S(1)}) custom-call(s32[2,4]{1,0:T(2,128)S(1)} %bitcast.22, f32[2048,256]{1,0:T(8,128)S(1)} %get-tuple-element.49.self_grad, bf16[2,128,256]{2,1,0:T(8,128)(2,1)S(1)} %get-tuple-element.50.rest_0_, bf16[2,128,256]{2,1,0:T(8,128)(2,1)S(1)} %collective-permute-done.7.rest_1_, ...), custom_call_target="tpu_custom_call" | custom-call | tf_op jit(solution)/shard_map/tiles_done/pallas_call | solution.py:351
  42.3 0.0 collective-permute-done.11.rest_1_
  42.3 0.0 collective-permute-done.12.rest_2_
  42.3 0.0 collective-permute-done.13.rest_3_
  42.3 0.8 %head.1 = bf16[2048,256]{1,0:T(8,128)(2,1)} custom-call(f32[256,256]{1,0:T(8,128)S(1)} %get-tuple-element.54.head, bf16[256,256]{1,0:T(8,128)(2,1)S(1)} %get-tuple-element.59.rest_0_, bf16[256,256]{1,0:T(8,128)(2,1)S(1)} %collective-permute-done.11.rest_1_, bf16[256,256]{1,0:T(8,128)(2,1)S(1)} %collective-permute-done.12.rest_2_, ...), custom_call_target="tpu_custom_call", output_to_operand_aliasing={{}: (5, {})} | custom-call | tf_op jit(solution)/shard_map/head/pallas_call | solution.py:364
  (13 shorter events, 0.0 us)
Async XLA Ops:
  0.6 13.2 %copy-start.3 = (bf16[256,256]{1,0:T(8,128)(2,1)S(1)}, bf16[256,256]{1,0:T(8,128)(2,1)}, u32[]{:S(2)}) copy-start(bf16[256,256]{1,0:T(8,128)(2,1)} %w_self.3) | copy-start | bytes 393220
  0.6 13.2 %copy-start.5 = (s32[1,4,2]{1,2,0:T(2,128)S(1)}, s32[1,4,2]{1,2,0:T(2,128)}, u32[]{:S(2)}) copy-start(s32[1,4,2]{1,2,0:T(2,128)} %param.19) | copy-start | bytes 100
  0.7 13.2 %copy-start.7 = (s32[1,4]{1,0:T(1,128)S(1)}, s32[1,4]{1,0:T(1,128)}, u32[]{:S(2)}) copy-start(s32[1,4]{1,0:T(1,128)} %count.3) | copy-start | bytes 52
  0.7 13.2 %copy-start.8 = (f32[256]{0:T(256)S(1)}, f32[256]{0:T(256)}, u32[]{:S(2)}) copy-start(f32[256]{0:T(256)} %param.14) | copy-start | bytes 3076
  2.0 9.2 %collective-permute-start.2 = (bf16[256,256]{1,0:T(8,128)(2,1)S(1)}, bf16[256,256]{1,0:T(8,128)(2,1)S(1)}, u32[]{:S(2)}, u32[]{:S(2)}) collective-permute-start(bf16[256,256]{1,0:T(8,128)(2,1)S(1)} %get-tuple-element.36), channel_id=1, source_target_pairs={{0,24},{4,28},{8,16},{12,20},{16,8},{20,12},{24,0},{28,4},{1,25},{... | collective-permute-start | bytes 393224 | tf_op jit(solution)/shard_map/ppermute | solution.py:260
  6.0 7.7 %collective-permute-start.1 = (bf16[256,256]{1,0:T(8,128)(2,1)S(1)}, bf16[256,256]{1,0:T(8,128)(2,1)S(1)}, u32[]{:S(2)}, u32[]{:S(2)}) collective-permute-start(bf16[256,256]{1,0:T(8,128)(2,1)S(1)} %get-tuple-element.36), channel_id=1, source_target_pairs={{0,16},{4,20},{8,24},{12,28},{16,0},{20,4},{24,8},{28,12},{1,17},{... | collective-permute-start | bytes 393224 | tf_op jit(solution)/shard_map/ppermute | solution.py:260
  6.5 7.1 %collective-permute-start = (bf16[256,256]{1,0:T(8,128)(2,1)S(1)}, bf16[256,256]{1,0:T(8,128)(2,1)S(1)}, u32[]{:S(2)}, u32[]{:S(2)}) collective-permute-start(bf16[256,256]{1,0:T(8,128)(2,1)S(1)} %get-tuple-element.36), channel_id=1, source_target_pairs={{0,8},{4,12},{8,0},{12,4},{16,24},{20,28},{24,16},{28,20},{1,9},{5... | collective-permute-start | bytes 393224 | tf_op jit(solution)/shard_map/ppermute | solution.py:260
  6.7 14.0 %collective-permute-start.4 = (bf16[2,128,256]{2,1,0:T(8,128)(2,1)S(1)}, bf16[2,128,256]{2,1,0:T(8,128)(2,1)S(1)}, u32[]{:S(2)}, u32[]{:S(2)}) collective-permute-start(bf16[2,128,256]{2,1,0:T(8,128)(2,1)S(1)} %get-tuple-element.41), channel_id=1, source_target_pairs={{0,1},{1,0},{2,3},{3,2},{4,5},{5,4},{6,7},{7,6},{8,9},{9,8},{10,11... | collective-permute-start | bytes 393224 | tf_op jit(solution)/shard_map/ppermute | solution.py:260
  8.6 12.1 %collective-permute-start.5 = (bf16[2,128,256]{2,1,0:T(8,128)(2,1)S(1)}, bf16[2,128,256]{2,1,0:T(8,128)(2,1)S(1)}, u32[]{:S(2)}, u32[]{:S(2)}) collective-permute-start(bf16[2,128,256]{2,1,0:T(8,128)(2,1)S(1)} %get-tuple-element.42), channel_id=1, source_target_pairs={{0,2},{1,3},{2,0},{3,1},{4,6},{5,7},{6,4},{7,5},{8,10},{9,11},{10,... | collective-permute-start | bytes 393224 | tf_op jit(solution)/shard_map/ppermute | solution.py:260
  11.2 9.5 %collective-permute-start.6 = (bf16[2,128,256]{2,1,0:T(8,128)(2,1)S(1)}, bf16[2,128,256]{2,1,0:T(8,128)(2,1)S(1)}, u32[]{:S(2)}, u32[]{:S(2)}) collective-permute-start(bf16[2,128,256]{2,1,0:T(8,128)(2,1)S(1)} %get-tuple-element.43), channel_id=1, source_target_pairs={{0,3},{1,2},{2,1},{3,0},{4,7},{5,6},{6,5},{7,4},{8,11},{9,10},{10,... | collective-permute-start | bytes 393224 | tf_op jit(solution)/shard_map/ppermute | solution.py:260
  13.7 2.0 %collective-permute-start.3 = (bf16[4,256,256]{2,1,0:T(8,128)(2,1)S(1)}, bf16[4,256,256]{2,1,0:T(8,128)(2,1)S(1)}, u32[]{:S(2)}, u32[]{:S(2)}) collective-permute-start(bf16[4,256,256]{2,1,0:T(8,128)(2,1)S(1)} %pad_maximum_fusion.same), channel_id=1, source_target_pairs={{0,4},{4,0},{8,12},{12,8},{16,20},{20,16},{24,28},{28,24},{1,5},{5... | collective-permute-start | bytes 1572872 | tf_op jit(solution)/shard_map/ppermute | solution.py:260
  13.8 2.2 %slice-start = ((s8[6291456]{0:T(1024)(128)(4,1)}), s8[4194304]{0:T(1024)(128)(4,1)S(1)}, s32[]{:S(2)}) async-start(s8[6291456]{0:T(1024)(128)(4,1)} %bitcast.13), calls=%async_computation | async-start | bytes 8388608
  13.9 2.8 %slice-start.1 = ((s8[6291456]{0:T(1024)(128)(4,1)}), s8[2097152]{0:T(1024)(128)(4,1)S(1)}, s32[]{:S(2)}) async-start(s8[6291456]{0:T(1024)(128)(4,1)} %bitcast.13), calls=%async_computation.1 | async-start | bytes 4194304
  13.9 3.0 %copy-start = (bf16[2048,256]{1,0:T(8,128)(2,1)S(1)}, bf16[2048,256]{1,0:T(8,128)(2,1)}, u32[]{:S(2)}) copy-start(bf16[2048,256]{1,0:T(8,128)(2,1)} %cot.3) | copy-start | bytes 3145732
  13.9 3.0 %copy-start.1 = (bf16[256,256]{1,0:T(8,128)(2,1)S(1)}, bf16[256,256]{1,0:T(8,128)(2,1)}, u32[]{:S(2)}) copy-start(bf16[256,256]{1,0:T(8,128)(2,1)} %w_neigh.3) | copy-start | bytes 393220
  13.9 3.0 %copy-start.4 = (s32[6]{0:T(128)S(1)}, s32[6]{0:T(128)}, u32[]{:S(2)}) copy-start(s32[6]{0:T(128)} %hub_ids.3) | copy-start | bytes 76
  16.9 3.8 %copy-start.2 = (bf16[1,4,2,128,128]{4,3,2,1,0:T(8,128)(2,1)S(1)}, bf16[1,4,2,128,128]{4,3,2,1,0:T(8,128)(2,1)}, u32[]{:S(2)}) copy-start(bf16[1,4,2,128,128]{4,3,2,1,0:T(8,128)(2,1)} %param.20) | copy-start | bytes 786436
  25.4 15.1 %copy-start.6 = (s32[1,4,2]{1,2,0:T(2,128)S(1)}, s32[1,4,2]{1,2,0:T(2,128)}, u32[]{:S(2)}) copy-start(s32[1,4,2]{1,2,0:T(2,128)} %param.17) | copy-start | bytes 100
  25.4 5.0 %collective-permute-start.10 = (bf16[4,256,256]{2,1,0:T(8,128)(2,1)S(1)}, bf16[4,256,256]{2,1,0:T(8,128)(2,1)S(1)}, u32[]{:S(2)}, u32[]{:S(2)}) collective-permute-start(bf16[4,256,256]{2,1,0:T(8,128)(2,1)S(1)} %get-tuple-element.58), channel_id=1, source_target_pairs={{0,4},{4,0},{8,12},{12,8},{16,20},{20,16},{24,28},{28,24},{1,5},{5... | collective-permute-start | bytes 1572872 | tf_op jit(solution)/shard_map/ppermute | solution.py:260
  26.0 8.4 %collective-permute-start.7 = (bf16[2,128,256]{2,1,0:T(8,128)(2,1)S(1)}, bf16[2,128,256]{2,1,0:T(8,128)(2,1)S(1)}, u32[]{:S(2)}, u32[]{:S(2)}) collective-permute-start(bf16[2,128,256]{2,1,0:T(8,128)(2,1)S(1)} %get-tuple-element.51), channel_id=1, source_target_pairs={{0,1},{1,0},{2,3},{3,2},{4,5},{5,4},{6,7},{7,6},{8,9},{9,8},{10,11... | collective-permute-start | bytes 393224 | tf_op jit(solution)/shard_map/ppermute | solution.py:260
  27.5 12.9 %collective-permute-start.8 = (bf16[2,128,256]{2,1,0:T(8,128)(2,1)S(1)}, bf16[2,128,256]{2,1,0:T(8,128)(2,1)S(1)}, u32[]{:S(2)}, u32[]{:S(2)}) collective-permute-start(bf16[2,128,256]{2,1,0:T(8,128)(2,1)S(1)} %get-tuple-element.52), channel_id=1, source_target_pairs={{0,2},{1,3},{2,0},{3,1},{4,6},{5,7},{6,4},{7,5},{8,10},{9,11},{10,... | collective-permute-start | bytes 393224 | tf_op jit(solution)/shard_map/ppermute | solution.py:260
  29.1 11.4 %collective-permute-start.9 = (bf16[2,128,256]{2,1,0:T(8,128)(2,1)S(1)}, bf16[2,128,256]{2,1,0:T(8,128)(2,1)S(1)}, u32[]{:S(2)}, u32[]{:S(2)}) collective-permute-start(bf16[2,128,256]{2,1,0:T(8,128)(2,1)S(1)} %get-tuple-element.53), channel_id=1, source_target_pairs={{0,3},{1,2},{2,1},{3,0},{4,7},{5,6},{6,5},{7,4},{8,11},{9,10},{10,... | collective-permute-start | bytes 393224 | tf_op jit(solution)/shard_map/ppermute | solution.py:260
  30.5 11.8 %collective-permute-start.11 = (bf16[256,256]{1,0:T(8,128)(2,1)S(1)}, bf16[256,256]{1,0:T(8,128)(2,1)S(1)}, u32[]{:S(2)}, u32[]{:S(2)}) collective-permute-start(bf16[256,256]{1,0:T(8,128)(2,1)S(1)} %get-tuple-element.60), channel_id=1, source_target_pairs={{0,8},{4,12},{8,0},{12,4},{16,24},{20,28},{24,16},{28,20},{1,9},{5... | collective-permute-start | bytes 393224 | tf_op jit(solution)/shard_map/ppermute | solution.py:260
  32.8 9.5 %collective-permute-start.12 = (bf16[256,256]{1,0:T(8,128)(2,1)S(1)}, bf16[256,256]{1,0:T(8,128)(2,1)S(1)}, u32[]{:S(2)}, u32[]{:S(2)}) collective-permute-start(bf16[256,256]{1,0:T(8,128)(2,1)S(1)} %get-tuple-element.61), channel_id=1, source_target_pairs={{0,16},{4,20},{8,24},{12,28},{16,0},{20,4},{24,8},{28,12},{1,17},{... | collective-permute-start | bytes 393224 | tf_op jit(solution)/shard_map/ppermute | solution.py:260
  34.4 7.9 %collective-permute-start.13 = (bf16[256,256]{1,0:T(8,128)(2,1)S(1)}, bf16[256,256]{1,0:T(8,128)(2,1)S(1)}, u32[]{:S(2)}, u32[]{:S(2)}) collective-permute-start(bf16[256,256]{1,0:T(8,128)(2,1)S(1)} %get-tuple-element.62), channel_id=1, source_target_pairs={{0,24},{4,28},{8,16},{12,20},{16,8},{20,12},{24,0},{28,4},{1,25},{... | collective-permute-start | bytes 393224 | tf_op jit(solution)/shard_map/ppermute | solution.py:260

commit v5 on v4

--- a/solution.py
+++ b/solution.py
@@ -56,9 +56,19 @@
         back = back - (1 - bit)
 
 
-def early_kernel(count, dst, feats, w_self, bias, order, place, own, *, peers, slots, tile):
-    tile_order(count, dst, order, place, peers=peers, slots=slots, tiles=feats.shape[0] // tile)
+def early_kernel(feats, w_self, bias, own):
     own[...] = jnp.dot(feats[...], w_self[...], preferred_element_type=F32) + bias[...]
+
+
+def degree_kernel(adj, deg, *, chunk):
+    sections, nodes, hub_rows = adj.shape
+    for start in range(0, nodes, chunk):
+        at = pl.ds(start, chunk)
+        lanes = jnp.zeros((chunk, 128), F32)
+        for s in range(sections):
+            for c in range(0, hub_rows, 128):
+                lanes = lanes + adj[s, at, c : c + 128].astype(F32)
+        deg[at, :] = jnp.broadcast_to(1.0 + jnp.sum(lanes, axis=1, keepdims=True), (chunk, 128))
 
 
 def dense(raw, deg, own, cot, w_neigh):
@@ -67,14 +77,15 @@
     agg = (raw * inverse).astype(BF16)
     pre = own + jnp.dot(agg, w_neigh[...], preferred_element_type=F32)
     sig = 0.5 * jnp.tanh(0.5 * pre) + 0.5
-    out = (pre * sig).astype(BF16)
-    grad = (cot.astype(F32) * sig * (1.0 + pre * (1.0 - sig))).astype(BF16)
+    silu = pre * sig
+    out = silu.astype(BF16)
+    grad = (cot.astype(F32) * (sig + silu * (1.0 - sig))).astype(BF16)
     agg_grad = (lax.dot_general(grad, w_neigh[...], BY_LAST, preferred_element_type=F32) * inverse).astype(BF16)
     return out, grad, agg_grad
 
 
 def forward_kernel(
-    order, hub_ids, adj, same, other, own, cot, w_neigh, raw, deg, *rest, tile, chunk, group
+    order, hub_ids, adj, same, other, deg, own, cot, w_neigh, raw, *rest, tile, chunk, group
 ):
     results, blocks = rest[:-1], rest[-1]
     row = lax.axis_index("row")
@@ -96,11 +107,6 @@
         at = pl.ds(start, chunk)
         weights = jnp.concatenate([adj[s, at, :] for s in range(sections)], axis=1)
         raw[at, :] = jnp.dot(weights, blocks[...], preferred_element_type=F32)
-        wide = weights.astype(F32)
-        lanes = wide[:, 0:128]
-        for c in range(128, wide.shape[1], 128):
-            lanes = lanes + wide[:, c : c + 128]
-        deg[at, :] = jnp.broadcast_to(1.0 + jnp.sum(lanes, axis=1, keepdims=True), (chunk, 128))
     if results:
         out, grad, turned = results
         first = tiles - out.shape[0] // tile
@@ -183,7 +189,7 @@
 
 
 def self_kernel(order, w_self, *rest, tile):
-    pieces, (out, self_grad, sems) = rest[:-3], rest[-3:]
+    pieces, (out, total, self_grad, narrow, sems) = rest[:-5], rest[-5:]
     copies = []
     i = 0
     for outs, grads in zip(pieces[: len(pieces) // 2], pieces[len(pieces) // 2 :]):
@@ -197,8 +203,16 @@
     for grads in pieces[len(pieces) // 2 :]:
         through = lax.dot_general(grads[...], w_self[...], BY_LAST, preferred_element_type=F32)
         for j in range(grads.shape[0] // tile):
-            self_grad[rows_at(order[i], tile), :] = through[j * tile : (j + 1) * tile]
+            at = rows_at(order[i], tile)
+            self_grad[at, :] = through[j * tile : (j + 1) * tile]
+            narrow[at, :] = through[j * tile : (j + 1) * tile].astype(BF16)
             i += 1
+    parts = sems.shape[0] - len(copies)
+    rows = narrow.shape[0] // parts
+    for i in range(parts):
+        at = pl.ds(i * rows, rows)
+        copies.append(pltpu.make_async_copy(narrow.at[at], total.at[at], sems.at[len(copies)]))
+        copies[-1].start()
     for copy in copies:
         copy.wait()
 
@@ -208,22 +222,29 @@
         out[...] = (even[e].astype(F32) + came[e].astype(F32)).astype(BF16)
 
 
-def tiles_kernel(send, self_grad, *rest, peers, slots, tile, chunk):
-    back, (out, head, total, done, sems) = rest[:peers], rest[peers:]
+def tiles_kernel(send, self_grad, *rest, peers, slots, tile):
+    back, (_, out, head, total, done, sems) = rest[:peers], rest[peers:]
     col = lax.axis_index("col")
-    total[...] = self_grad[...]
-    for d in range(peers):
-        for k in range(slots):
-            total[rows_at(send[k, col ^ d], tile), :] += back[d][k].astype(F32)
-    head[...] = total[pl.ds(0, head.shape[0]), :]
+    targets = [send[k, col ^ d] for d in range(peers) for k in range(slots)]
+    spots = [rows_at(target, tile) for target in targets]
+    top = pl.ds(0, head.shape[0])
+    total[top, :] = self_grad[top, :]
+    for at in spots:
+        total[at, :] = self_grad[at, :]
+    for i, at in enumerate(spots):
+        total[at, :] += back[i // slots][i % slots].astype(F32)
     copies = []
-    for i, start in enumerate(range(head.shape[0], total.shape[0], chunk)):
-        at = pl.ds(start, chunk)
-        done[at, :] = total[at, :].astype(BF16)
-        copies.append(pltpu.make_async_copy(done.at[at], out.at[at], sems.at[i]))
-        copies[-1].start()
-    for copy in copies:
-        copy.wait()
+    for i, at in enumerate(spots):
+        fresh = targets[i] * tile >= head.shape[0]
+        for other in targets[:i]:
+            fresh = fresh & (other != targets[i])
+        done[i] = total[at, :].astype(BF16)
+        copy = pltpu.make_async_copy(done.at[i], out.at[at], sems.at[i])
+        pl.when(fresh)(copy.start)
+        copies.append((fresh, copy))
+    head[...] = total[top, :]
+    for fresh, copy in copies:
+        pl.when(fresh)(copy.wait)
 
 
 def head_kernel(head, *rest):
@@ -277,31 +298,48 @@
     same = jnp.stack([own_hub] + [across(own_hub, "row", n_row, d) for d in range(2, n_row, 2)])
     other = across(same, "row", n_row, 1)
 
-    tile_at, place, own = pl.pallas_call(
-        functools.partial(early_kernel, **sizes),
-        in_specs=[SMEM] * 2 + [VMEM] * 3,
-        out_specs=[SMEM] * 2 + [VMEM],
-        out_shape=[shape((tiles,), jnp.int32)] * 2 + [shape((nodes, out_width), F32)],
+    own = pl.pallas_call(
+        early_kernel,
+        in_specs=[VMEM] * 3,
+        out_specs=VMEM,
+        out_shape=shape((nodes, out_width), F32),
+        compiler_params=params,
+        cost_estimate=pl.CostEstimate(flops=1000000000, transcendentals=0, bytes_accessed=0),
+        name="early",
+    )(feats, w_self, bias)
+    tile_at, place = pl.pallas_call(
+        functools.partial(tile_order, peers=peers, slots=slots, tiles=tiles),
+        in_specs=[SMEM] * 2,
+        out_specs=[SMEM] * 2,
+        out_shape=[shape((tiles,), jnp.int32)] * 2,
         compiler_params=params,
         cost_estimate=pl.CostEstimate(flops=10000000000, transcendentals=0, bytes_accessed=0),
-        name="early",
-    )(count, dst, feats, w_self, bias)
+        name="tables",
+    )(count, dst)
 
     def results(number):
         if not number:
             return []
         return [shape((number * tile, out_width), BF16)] * 2 + [shape((width, number * tile), BF16)]
 
-    raw, deg, *others = pl.pallas_call(
+    deg = pl.pallas_call(
+        functools.partial(degree_kernel, chunk=256),
+        in_specs=[VMEM],
+        out_specs=VMEM,
+        out_shape=shape((nodes, 128), F32),
+        compiler_params=params,
+        name="degree",
+    )(adj)
+    raw, *others = pl.pallas_call(
         functools.partial(forward_kernel, tile=tile, chunk=256, group=group),
-        in_specs=[SMEM] * 2 + [VMEM] * 6,
-        out_specs=[VMEM] * (2 + len(results(tiles - first))),
+        in_specs=[SMEM] * 2 + [VMEM] * 7,
+        out_specs=[VMEM] * (1 + len(results(tiles - first))),
         scratch_shapes=[pltpu.VMEM((sections * hub_rows, width), BF16)],
-        out_shape=[shape((nodes, width), F32), shape((nodes, 128), F32)] + results(tiles - first),
+        out_shape=[shape((nodes, width), F32)] + results(tiles - first),
         compiler_params=params,
         cost_estimate=cost(2 * sections * nodes * hub_rows * width),
         name="forward",
-    )(tile_at, hub_ids, adj, same, other, own, cotangent, w_neigh)
+    )(tile_at, hub_ids, adj, same, other, deg, own, cotangent, w_neigh)
     landed = pl.pallas_call(
         functools.partial(landed_kernel, group=group, **sizes),
         in_specs=[SMEM] * 4 + [VMEM] * (6 + peers),
@@ -329,12 +367,12 @@
         name="hub_backward",
     )(tile_at, hub_ids, adj, *turned)
     came = across(odd, "row", n_row, 1)
-    output, self_grad = pl.pallas_call(
+    output, feature_grad, self_grad = pl.pallas_call(
         functools.partial(self_kernel, tile=tile),
         in_specs=[SMEM] + [VMEM] * (1 + 2 * len(outs)),
-        out_specs=[HBM, VMEM],
-        scratch_shapes=[pltpu.SemaphoreType.DMA((tiles,))],
-        out_shape=[shape((nodes, out_width), BF16), shape((nodes, width), F32)],
+        out_specs=[HBM, HBM, VMEM],
+        scratch_shapes=[pltpu.VMEM((nodes, width), BF16), pltpu.SemaphoreType.DMA((tiles + 4,))],
+        out_shape=[shape((nodes, out_width), BF16), shape((nodes, width), BF16), shape((nodes, width), F32)],
         compiler_params=params,
         name="self",
     )(tile_at, w_self, *outs, *grads)
@@ -347,26 +385,27 @@
     )(even, came)
     hubs = [sums[0]] + [across(sums[d // 2], "row", n_row, d) for d in range(2, n_row, 2)]
 
-    chunk = 2 * tile
+    whole = shape((nodes, width), BF16)
     feature_grad, head = pl.pallas_call(
-        functools.partial(tiles_kernel, chunk=chunk, **sizes),
-        in_specs=[SMEM] + [VMEM] * (1 + peers),
+        functools.partial(tiles_kernel, **sizes),
+        in_specs=[SMEM] + [VMEM] * (1 + peers) + [HBM],
         out_specs=[HBM, VMEM],
         scratch_shapes=[
             pltpu.VMEM((nodes, width), F32),
-            pltpu.VMEM((nodes, width), BF16),
-            pltpu.SemaphoreType.DMA(((nodes - hub_rows) // chunk,)),
+            pltpu.VMEM((peers * slots, tile, width), BF16),
+            pltpu.SemaphoreType.DMA((peers * slots,)),
         ],
-        out_shape=[shape((nodes, width), BF16), shape((hub_rows, width), F32)],
+        out_shape=[whole, shape((hub_rows, width), F32)],
+        input_output_aliases={2 + peers: 0},
         compiler_params=params,
         name="tiles_done",
-    )(send, self_grad, *returned)
+    )(send, self_grad, *returned, feature_grad)
     feature_grad = pl.pallas_call(
         head_kernel,
         in_specs=[VMEM] * (1 + len(hubs)) + [HBM],
         out_specs=HBM,
         scratch_shapes=[pltpu.VMEM((hub_rows, width), BF16), pltpu.SemaphoreType.DMA],
-        out_shape=shape((nodes, width), BF16),
+        out_shape=whole,
         input_output_aliases={1 + len(hubs): 0},
         compiler_params=params,
         name="head",

time: 43.3 us -> 44.2 us (1.021)
  starting transfers between devices: 23.2 us -> 19.8 us
  local copies, waits for them, and re-layouts: 1.26 us -> 4.06 us
  waiting for transfers between devices: 1.77 us -> 2.56 us
  Pallas kernels: 16 us -> 16.6 us
    ppermute x14, starting transfers between devices: 23.2 us -> 19.8 us  [across(): return lax.ppermute(x, axis, [(i, i ^ d) for i in range(size)])]
    unnamed x22 -> x24, local copies, waits for them, and re-layouts: 1.26 us -> 4.06 us
    ppermute x14, waiting for transfers between devices: 1.77 us -> 2.56 us  [across(): return lax.ppermute(x, axis, [(i, i ^ d) for i in range(size)])]
    pallas_call x2 -> x4, Pallas kernels: 3.34 us -> 4.08 us  [the longest x1 1.55 us: shards(): pl.pallas_call(functools.partial(tiles_kernel, **sizes), in_specs=[SMEM]...]
  transfers between devices with their start and end apart: 14 -> 14, of which waited for: 2 -> 3; matrix products, arithmetic and copies ran while one was open for 0% -> 0% of each run, Pallas kernels for 21% -> 22%
where the time goes in v5:
time: 44.2 us; the launch traced here: 44 us
  starting transfers between devices  19.8 us (45%)
  Pallas kernels  16.6 us (38%)
  local copies, waits for them, and re-layouts  4.06 us (9%)
  waiting for transfers between devices  2.56 us (6%)
  between operations  0.87 us (2%)
    ppermute x14, starting transfers between devices, across(): return lax.ppermute(x, axis, [(i, i ^ d) for i in range(size)])  19.8 us
    unnamed x24, local copies, waits for them, and re-layouts  4.06 us
    pallas_call x1, Pallas kernels, shards(): pl.pallas_call(functools.partial(forward_kernel, tile=tile, chunk=256, gr...  3.31 us
    pallas_call x1, Pallas kernels, shards(): pl.pallas_call(functools.partial(hub_backward_kernel, tile=tile), in_spec...  2.61 us
    ppermute x14, waiting for transfers between devices, across(): return lax.ppermute(x, axis, [(i, i ^ d) for i in range(size)])  2.56 us
    pallas_call x1, Pallas kernels, shards(): pl.pallas_call(functools.partial(self_kernel, tile=tile), in_specs=[SMEM]...  2.39 us
    pallas_call x1, Pallas kernels, shards(): pl.pallas_call(functools.partial(landed_kernel, group=group, **sizes), in...  2.03 us
    pallas_call x1, Pallas kernels, shards(): pl.pallas_call(functools.partial(tiles_kernel, **sizes), in_specs=[SMEM]...  1.55 us
  transfers between devices with their start and end apart: 14, of which 3 were waited for; matrix products, arithmetic and copies ran while one was open for 0% of the time, Pallas kernels for 22%

profile of v5, /device:TPU:0, one launch (start us, length us, event | category | flops | bytes accessed | tf_op | source)
XLA Modules:
  0.0 44.0 jit_solution(2852793569024069821)
XLA Ops:
  0.6 1.3 %pick.1 = (bf16[2048,256]{1,0:T(8,128)(2,1)S(1)}, bf16[256,256]{1,0:T(8,128)(2,1)S(1)}, bf16[2,128,256]{2,1,0:T(8,128)(2,1)S(1)}, bf16[2,128,256]{2,1,0:T(8,128)...) custom-call(s32[2,4]{1,0:T(2,128)} %bitcast.22, bf16[2048,256]{1,0:T(8,128)(2,1)} %feats_in.1), custom_call_target="tpu_custom_call" | custom-call | flops 1000000000 | tf_op jit(solution)/shard_map/pick/pallas_call | solution.py:285
  1.9 4.0 %collective-permute-start.2 = (bf16[256,256]{1,0:T(8,128)(2,1)S(1)}, bf16[256,256]{1,0:T(8,128)(2,1)S(1)}, u32[]{:S(2)}, u32[]{:S(2)}) collective-permute-start(bf16[256,256]{1,0:T(8,128)(2,1)S(1)} %get-tuple-element.34), channel_id=1, source_target_pairs={{0,24},{4,28},{8,16},{12,20},{16,8},{20,12},{24,0},{28,4},{1,25},{... | collective-permute-start | bytes 393224 | tf_op jit(solution)/shard_map/ppermute | solution.py:281
  5.9 0.5 %collective-permute-start.1 = (bf16[256,256]{1,0:T(8,128)(2,1)S(1)}, bf16[256,256]{1,0:T(8,128)(2,1)S(1)}, u32[]{:S(2)}, u32[]{:S(2)}) collective-permute-start(bf16[256,256]{1,0:T(8,128)(2,1)S(1)} %get-tuple-element.34), channel_id=1, source_target_pairs={{0,16},{4,20},{8,24},{12,28},{16,0},{20,4},{24,8},{28,12},{1,17},{... | collective-permute-start | bytes 393224 | tf_op jit(solution)/shard_map/ppermute | solution.py:281
  6.4 0.1 collective-permute-start
  6.6 2.0 %collective-permute-start.4 = (bf16[2,128,256]{2,1,0:T(8,128)(2,1)S(1)}, bf16[2,128,256]{2,1,0:T(8,128)(2,1)S(1)}, u32[]{:S(2)}, u32[]{:S(2)}) collective-permute-start(bf16[2,128,256]{2,1,0:T(8,128)(2,1)S(1)} %get-tuple-element.38), channel_id=1, source_target_pairs={{0,1},{1,0},{2,3},{3,2},{4,5},{5,4},{6,7},{7,6},{8,9},{9,8},{10,11... | collective-permute-start | bytes 393224 | tf_op jit(solution)/shard_map/ppermute | solution.py:281
  8.5 2.6 %collective-permute-start.5 = (bf16[2,128,256]{2,1,0:T(8,128)(2,1)S(1)}, bf16[2,128,256]{2,1,0:T(8,128)(2,1)S(1)}, u32[]{:S(2)}, u32[]{:S(2)}) collective-permute-start(bf16[2,128,256]{2,1,0:T(8,128)(2,1)S(1)} %get-tuple-element.39), channel_id=1, source_target_pairs={{0,2},{1,3},{2,0},{3,1},{4,6},{5,7},{6,4},{7,5},{8,10},{9,11},{10,... | collective-permute-start | bytes 393224 | tf_op jit(solution)/shard_map/ppermute | solution.py:281
  11.1 2.8 %copy-done = bf16[1,6,2048,256]{3,2,1,0:T(8,128)(2,1)S(1)} copy-done((bf16[1,6,2048,256]{3,2,1,0:T(8,128)(2,1)S(1)}, bf16[1,6,2048,256]{3,2,1,0:T(8,128)(2,1)}, u32[]{:S(2)}) %copy-start) | copy-done | bytes 6291480
  13.9 0.9 %degree.1.deg.deg_in = f32[2048,128]{1,0:T(8,128)S(1)} custom-call(bf16[6,2048,256]{2,1,0:T(8,128)(2,1)S(1)} %bitcast.13), custom_call_target="tpu_custom_call" | custom-call | tf_op jit(solution)/shard_map/degree/pallas_call | solution.py:325
  14.8 0.0 copy-done.4
  14.8 0.0 copy-start.8
  14.8 0.4 early.1.own
  15.3 0.0 collective-permute-done.2
  15.3 0.1 collective-permute-start.6
  15.4 0.0 collective-permute-done
  15.4 0.1 pad_maximum_fusion.same
  15.5 0.1 collective-permute-start.3
  15.5 0.0 slice-start
  15.6 0.0 slice-start.1
  15.6 0.0 copy-start.1
  15.6 0.0 copy-start.2
  15.6 0.0 copy-start.5
  15.6 1.2 %tables.1 = (s32[16]{0:T(128)S(1)}, s32[16]{0:T(128)S(1)}) custom-call(s32[1,4]{1,0:T(1,128)S(1)} %copy-done.8, s32[2,4]{1,0:T(2,128)S(1)} %bitcast.20), custom_call_target="tpu_custom_call" | custom-call | flops 10000000000 | tf_op jit(solution)/shard_map/tables/pallas_call | solution.py:310
  16.8 0.6 %collective-permute-done.3.other = bf16[4,256,256]{2,1,0:T(8,128)(2,1)S(1)} collective-permute-done((bf16[4,256,256]{2,1,0:T(8,128)(2,1)S(1)}, bf16[4,256,256]{2,1,0:T(8,128)(2,1)S(1)}, u32[]{:S(2)}, u32[]{:S(2)}) %collective-permute-start.3) | collective-permute-done | bytes 524320 | tf_op jit(solution)/shard_map/ppermute | solution.py:281
  17.4 0.3 slice-done
  17.7 0.7 %slice-done.1 = s8[2097152]{0:T(1024)(128)(4,1)S(1)} async-done(((s8[6291456]{0:T(1024)(128)(4,1)}), s8[2097152]{0:T(1024)(128)(4,1)S(1)}, s32[]{:S(2)}) %slice-start.1) | async-done | bytes 2097176
  18.4 0.2 copy-done.1
  18.7 3.3 %forward.1 = (f32[2048,256]{1,0:T(8,128)S(1)}, bf16[1024,256]{1,0:T(8,128)(2,1)S(1)}, bf16[1024,256]{1,0:T(8,128)(2,1)S(1)}, bf16[256,1024]{1,0:T(8,128)(2,1)S(1)}) custom-call(s32[16]{0:T(128)S(1)} %get-tuple-element.32.order, s32[6]{0:T(128)S(1)} %copy-done.5, bf16[6,2048,256]{2,1,0:T(8,128)(2,1)S(1)} %bitcast.16, ...), custom_call_target="tpu_custom_call" | custom-call | flops 1610612736 | bytes 4194304 | tf_op jit(solution)/shard_map/forward/pallas_call | solution.py:333
  22.0 0.0 collective-permute-done.4.rest_1_
  22.0 0.0 collective-permute-done.5.rest_2_
  22.0 0.2 collective-permute-done.6.rest_3_
  22.2 2.0 %landed.1 = (bf16[1024,256]{1,0:T(8,128)(2,1)S(1)}, bf16[1024,256]{1,0:T(8,128)(2,1)S(1)}, bf16[256,1024]{1,0:T(8,128)(2,1)S(1)}, bf16[2,128,256]{2,1,0:T(8,128)...) custom-call(s32[1,4]{1,0:T(1,128)S(1)} %copy-done.8, ...), custom_call_target="tpu_custom_call" | custom-call | tf_op jit(solution)/shard_map/landed/pallas_call | solution.py:343
  24.3 2.6 %hub_backward.1 = (bf16[4,256,256]{2,1,0:T(8,128)(2,1)S(1)}, bf16[4,256,256]{2,1,0:T(8,128)(2,1)S(1)}) custom-call(s32[16]{0:T(128)S(1)} %get-tuple-element.32.order, s32[6]{0:T(128)S(1)} %copy-done.5, bf16[6,2048,256]{2,1,0:T(8,128)(2,1)S(1)} %bitcast.17, bf16[256,1024]{1,0:T(8,128)(2,1)S(1)} %get-tuple-element.53.rest_0_, ...), custom_call_target="tpu_custom_call" | custom-call | flops 1610612736 | bytes 4194304 | tf_op jit(solution)/shard_map/hub_backward/pallas_call | solution.py:359
  26.9 0.0 copy-start.7
  26.9 0.4 collective-permute-start.10
  27.2 0.9 %collective-permute-start.7 = (bf16[2,128,256]{2,1,0:T(8,128)(2,1)S(1)}, bf16[2,128,256]{2,1,0:T(8,128)(2,1)S(1)}, u32[]{:S(2)}, u32[]{:S(2)}) collective-permute-start(bf16[2,128,256]{2,1,0:T(8,128)(2,1)S(1)} %get-tuple-element.48), channel_id=1, source_target_pairs={{0,1},{1,0},{2,3},{3,2},{4,5},{5,4},{6,7},{7,6},{8,9},{9,8},{10,11... | collective-permute-start | bytes 393224 | tf_op jit(solution)/shard_map/ppermute | solution.py:281
  28.1 3.5 %collective-permute-start.8 = (bf16[2,128,256]{2,1,0:T(8,128)(2,1)S(1)}, bf16[2,128,256]{2,1,0:T(8,128)(2,1)S(1)}, u32[]{:S(2)}, u32[]{:S(2)}) collective-permute-start(bf16[2,128,256]{2,1,0:T(8,128)(2,1)S(1)} %get-tuple-element.49), channel_id=1, source_target_pairs={{0,2},{1,3},{2,0},{3,1},{4,6},{5,7},{6,4},{7,5},{8,10},{9,11},{10,... | collective-permute-start | bytes 393224 | tf_op jit(solution)/shard_map/ppermute | solution.py:281
  31.6 0.0 collective-permute-start.9
  31.6 0.0 collective-permute-done.10.came
  31.6 0.1 pair_add.1
  31.8 1.7 %collective-permute-start.11 = (bf16[256,256]{1,0:T(8,128)(2,1)S(1)}, bf16[256,256]{1,0:T(8,128)(2,1)S(1)}, u32[]{:S(2)}, u32[]{:S(2)}) collective-permute-start(bf16[256,256]{1,0:T(8,128)(2,1)S(1)} %get-tuple-element.58), channel_id=1, source_target_pairs={{0,8},{4,12},{8,0},{12,4},{16,24},{20,28},{24,16},{28,20},{1,9},{5... | collective-permute-start | bytes 393224 | tf_op jit(solution)/shard_map/ppermute | solution.py:281
  33.5 1.5 %collective-permute-start.12 = (bf16[256,256]{1,0:T(8,128)(2,1)S(1)}, bf16[256,256]{1,0:T(8,128)(2,1)S(1)}, u32[]{:S(2)}, u32[]{:S(2)}) collective-permute-start(bf16[256,256]{1,0:T(8,128)(2,1)S(1)} %get-tuple-element.59), channel_id=1, source_target_pairs={{0,16},{4,20},{8,24},{12,28},{16,0},{20,4},{24,8},{28,12},{1,17},{... | collective-permute-start | bytes 393224 | tf_op jit(solution)/shard_map/ppermute | solution.py:281
  35.0 2.4 %collective-permute-start.13 = (bf16[256,256]{1,0:T(8,128)(2,1)S(1)}, bf16[256,256]{1,0:T(8,128)(2,1)S(1)}, u32[]{:S(2)}, u32[]{:S(2)}) collective-permute-start(bf16[256,256]{1,0:T(8,128)(2,1)S(1)} %get-tuple-element.60), channel_id=1, source_target_pairs={{0,24},{4,28},{8,16},{12,20},{16,8},{20,12},{24,0},{28,4},{1,25},{... | collective-permute-start | bytes 393224 | tf_op jit(solution)/shard_map/ppermute | solution.py:281
  37.5 2.4 %self.1 = (bf16[2048,256]{1,0:T(8,128)(2,1)}, bf16[2048,256]{1,0:T(8,128)(2,1)}, f32[2048,256]{1,0:T(8,128)S(1)}) custom-call(s32[16]{0:T(128)S(1)} %get-tuple-element.32.order, bf16[256,256]{1,0:T(8,128)(2,1)S(1)} %copy-done.4, bf16[1024,256]{1,0:T(8,128)(2,1)S(1)} %get-tuple-element.41.rest_0_, bf16[1024,256]{1,0:T(8,128)(2,1)S(1)} %get-tuple-element.42.rest_1_, ...), custom_call_target="tpu_custom_call" | custom-call | tf_op jit(solution)/shard_map/self/pallas_call | solution.py:370
  39.9 1.7 %collective-permute-done.8.rest_2_ = bf16[2,128,256]{2,1,0:T(8,128)(2,1)S(1)} collective-permute-done((bf16[2,128,256]{2,1,0:T(8,128)(2,1)S(1)}, bf16[2,128,256]{2,1,0:T(8,128)(2,1)S(1)}, u32[]{:S(2)}, u32[]{:S(2)}) %collective-permute-start.8) | collective-permute-done | bytes 131104 | tf_op jit(solution)/shard_map/ppermute | solution.py:281
  41.6 1.6 %tiles_done.1 = (bf16[2048,256]{1,0:T(8,128)(2,1)}, f32[256,256]{1,0:T(8,128)S(1)}) custom-call(s32[2,4]{1,0:T(2,128)S(1)} %bitcast.23, f32[2048,256]{1,0:T(8,128)S(1)} %get-tuple-element.46.self_grad, bf16[2,128,256]{2,1,0:T(8,128)(2,1)S(1)} %get-tuple-element.47.rest_0_, ...), custom_call_target="tpu_custom_call", output_to_operand_aliasing={{0}: (6, {})} | custom-call | tf_op jit(solution)/shard_map/tiles_done/pallas_call | solution.py:389
  43.2 0.0 collective-permute-done.12.rest_2_
  43.2 0.0 collective-permute-done.13.rest_3_
  43.2 0.8 %head.1 = bf16[2048,256]{1,0:T(8,128)(2,1)} custom-call(f32[256,256]{1,0:T(8,128)S(1)} %get-tuple-element.52.head, bf16[256,256]{1,0:T(8,128)(2,1)S(1)} %get-tuple-element.57.rest_0_, bf16[256,256]{1,0:T(8,128)(2,1)S(1)} %collective-permute-done.11.rest_1_, bf16[256,256]{1,0:T(8,128)(2,1)S(1)} %collective-permute-done.12.rest_2_, ...), custom_call_target="tpu_custom_call", output_to_operand_aliasing={{}: (5, {})} | custom-call | tf_op jit(solution)/shard_map/head/pallas_call | solution.py:403
  (17 shorter events, 0.0 us)
Async XLA Ops:
  1.9 13.3 %collective-permute-start.2 = (bf16[256,256]{1,0:T(8,128)(2,1)S(1)}, bf16[256,256]{1,0:T(8,128)(2,1)S(1)}, u32[]{:S(2)}, u32[]{:S(2)}) collective-permute-start(bf16[256,256]{1,0:T(8,128)(2,1)S(1)} %get-tuple-element.34), channel_id=1, source_target_pairs={{0,24},{4,28},{8,16},{12,20},{16,8},{20,12},{24,0},{28,4},{1,25},{... | collective-permute-start | bytes 393224 | tf_op jit(solution)/shard_map/ppermute | solution.py:281
  5.9 9.4 %collective-permute-start.1 = (bf16[256,256]{1,0:T(8,128)(2,1)S(1)}, bf16[256,256]{1,0:T(8,128)(2,1)S(1)}, u32[]{:S(2)}, u32[]{:S(2)}) collective-permute-start(bf16[256,256]{1,0:T(8,128)(2,1)S(1)} %get-tuple-element.34), channel_id=1, source_target_pairs={{0,16},{4,20},{8,24},{12,28},{16,0},{20,4},{24,8},{28,12},{1,17},{... | collective-permute-start | bytes 393224 | tf_op jit(solution)/shard_map/ppermute | solution.py:281
  6.4 8.9 %collective-permute-start = (bf16[256,256]{1,0:T(8,128)(2,1)S(1)}, bf16[256,256]{1,0:T(8,128)(2,1)S(1)}, u32[]{:S(2)}, u32[]{:S(2)}) collective-permute-start(bf16[256,256]{1,0:T(8,128)(2,1)S(1)} %get-tuple-element.34), channel_id=1, source_target_pairs={{0,8},{4,12},{8,0},{12,4},{16,24},{20,28},{24,16},{28,20},{1,9},{5... | collective-permute-start | bytes 393224 | tf_op jit(solution)/shard_map/ppermute | solution.py:281
  6.6 15.4 %collective-permute-start.4 = (bf16[2,128,256]{2,1,0:T(8,128)(2,1)S(1)}, bf16[2,128,256]{2,1,0:T(8,128)(2,1)S(1)}, u32[]{:S(2)}, u32[]{:S(2)}) collective-permute-start(bf16[2,128,256]{2,1,0:T(8,128)(2,1)S(1)} %get-tuple-element.38), channel_id=1, source_target_pairs={{0,1},{1,0},{2,3},{3,2},{4,5},{5,4},{6,7},{7,6},{8,9},{9,8},{10,11... | collective-permute-start | bytes 393224 | tf_op jit(solution)/shard_map/ppermute | solution.py:281
  8.5 13.5 %collective-permute-start.5 = (bf16[2,128,256]{2,1,0:T(8,128)(2,1)S(1)}, bf16[2,128,256]{2,1,0:T(8,128)(2,1)S(1)}, u32[]{:S(2)}, u32[]{:S(2)}) collective-permute-start(bf16[2,128,256]{2,1,0:T(8,128)(2,1)S(1)} %get-tuple-element.39), channel_id=1, source_target_pairs={{0,2},{1,3},{2,0},{3,1},{4,6},{5,7},{6,4},{7,5},{8,10},{9,11},{10,... | collective-permute-start | bytes 393224 | tf_op jit(solution)/shard_map/ppermute | solution.py:281
  11.1 2.8 %copy-start = (bf16[1,6,2048,256]{3,2,1,0:T(8,128)(2,1)S(1)}, bf16[1,6,2048,256]{3,2,1,0:T(8,128)(2,1)}, u32[]{:S(2)}) copy-start(bf16[1,6,2048,256]{3,2,1,0:T(8,128)(2,1)} %param.16) | copy-start | bytes 18874372
  13.9 0.9 %copy-start.4 = (bf16[256,256]{1,0:T(8,128)(2,1)S(1)}, bf16[256,256]{1,0:T(8,128)(2,1)}, u32[]{:S(2)}) copy-start(bf16[256,256]{1,0:T(8,128)(2,1)} %w_self.3) | copy-start | bytes 393220
  13.9 0.9 %copy-start.9 = (f32[256]{0:T(256)S(1)}, f32[256]{0:T(256)}, u32[]{:S(2)}) copy-start(f32[256]{0:T(256)} %param.14) | copy-start | bytes 3076
  14.8 0.7 %copy-start.6 = (s32[1,4,2]{1,2,0:T(2,128)S(1)}, s32[1,4,2]{1,2,0:T(2,128)}, u32[]{:S(2)}) copy-start(s32[1,4,2]{1,2,0:T(2,128)} %param.19) | copy-start | bytes 100
  14.8 0.7 %copy-start.8 = (s32[1,4]{1,0:T(1,128)S(1)}, s32[1,4]{1,0:T(1,128)}, u32[]{:S(2)}) copy-start(s32[1,4]{1,0:T(1,128)} %count.3) | copy-start | bytes 52
  15.3 6.9 %collective-permute-start.6 = (bf16[2,128,256]{2,1,0:T(8,128)(2,1)S(1)}, bf16[2,128,256]{2,1,0:T(8,128)(2,1)S(1)}, u32[]{:S(2)}, u32[]{:S(2)}) collective-permute-start(bf16[2,128,256]{2,1,0:T(8,128)(2,1)S(1)} %get-tuple-element.40), channel_id=1, source_target_pairs={{0,3},{1,2},{2,1},{3,0},{4,7},{5,6},{6,5},{7,4},{8,11},{9,10},{10,... | collective-permute-start | bytes 393224 | tf_op jit(solution)/shard_map/ppermute | solution.py:281
  15.5 2.0 %collective-permute-start.3 = (bf16[4,256,256]{2,1,0:T(8,128)(2,1)S(1)}, bf16[4,256,256]{2,1,0:T(8,128)(2,1)S(1)}, u32[]{:S(2)}, u32[]{:S(2)}) collective-permute-start(bf16[4,256,256]{2,1,0:T(8,128)(2,1)S(1)} %pad_maximum_fusion.same), channel_id=1, source_target_pairs={{0,4},{4,0},{8,12},{12,8},{16,20},{20,16},{24,28},{28,24},{1,5},{5... | collective-permute-start | bytes 1572872 | tf_op jit(solution)/shard_map/ppermute | solution.py:281
  15.5 2.2 %slice-start = ((s8[6291456]{0:T(1024)(128)(4,1)}), s8[4194304]{0:T(1024)(128)(4,1)S(1)}, s32[]{:S(2)}) async-start(s8[6291456]{0:T(1024)(128)(4,1)} %bitcast.14), calls=%async_computation | async-start | bytes 8388608
  15.6 2.8 %slice-start.1 = ((s8[6291456]{0:T(1024)(128)(4,1)}), s8[2097152]{0:T(1024)(128)(4,1)S(1)}, s32[]{:S(2)}) async-start(s8[6291456]{0:T(1024)(128)(4,1)} %bitcast.14), calls=%async_computation.1 | async-start | bytes 4194304
  15.6 3.1 %copy-start.1 = (bf16[2048,256]{1,0:T(8,128)(2,1)S(1)}, bf16[2048,256]{1,0:T(8,128)(2,1)}, u32[]{:S(2)}) copy-start(bf16[2048,256]{1,0:T(8,128)(2,1)} %cot.3) | copy-start | bytes 3145732
  15.6 3.1 %copy-start.2 = (bf16[256,256]{1,0:T(8,128)(2,1)S(1)}, bf16[256,256]{1,0:T(8,128)(2,1)}, u32[]{:S(2)}) copy-start(bf16[256,256]{1,0:T(8,128)(2,1)} %w_neigh.3) | copy-start | bytes 393220
  15.6 3.0 %copy-start.5 = (s32[6]{0:T(128)S(1)}, s32[6]{0:T(128)}, u32[]{:S(2)}) copy-start(s32[6]{0:T(128)} %hub_ids.3) | copy-start | bytes 76
  18.7 3.6 %copy-start.3 = (bf16[1,4,2,128,128]{4,3,2,1,0:T(8,128)(2,1)S(1)}, bf16[1,4,2,128,128]{4,3,2,1,0:T(8,128)(2,1)}, u32[]{:S(2)}) copy-start(bf16[1,4,2,128,128]{4,3,2,1,0:T(8,128)(2,1)} %param.20) | copy-start | bytes 786436
  26.9 14.7 %copy-start.7 = (s32[1,4,2]{1,2,0:T(2,128)S(1)}, s32[1,4,2]{1,2,0:T(2,128)}, u32[]{:S(2)}) copy-start(s32[1,4,2]{1,2,0:T(2,128)} %param.17) | copy-start | bytes 100
  26.9 4.8 %collective-permute-start.10 = (bf16[4,256,256]{2,1,0:T(8,128)(2,1)S(1)}, bf16[4,256,256]{2,1,0:T(8,128)(2,1)S(1)}, u32[]{:S(2)}, u32[]{:S(2)}) collective-permute-start(bf16[4,256,256]{2,1,0:T(8,128)(2,1)S(1)} %get-tuple-element.56), channel_id=1, source_target_pairs={{0,4},{4,0},{8,12},{12,8},{16,20},{20,16},{24,28},{28,24},{1,5},{5... | collective-permute-start | bytes 1572872 | tf_op jit(solution)/shard_map/ppermute | solution.py:281
  27.2 7.8 %collective-permute-start.7 = (bf16[2,128,256]{2,1,0:T(8,128)(2,1)S(1)}, bf16[2,128,256]{2,1,0:T(8,128)(2,1)S(1)}, u32[]{:S(2)}, u32[]{:S(2)}) collective-permute-start(bf16[2,128,256]{2,1,0:T(8,128)(2,1)S(1)} %get-tuple-element.48), channel_id=1, source_target_pairs={{0,1},{1,0},{2,3},{3,2},{4,5},{5,4},{6,7},{7,6},{8,9},{9,8},{10,11... | collective-permute-start | bytes 393224 | tf_op jit(solution)/shard_map/ppermute | solution.py:281
  28.1 13.5 %collective-permute-start.8 = (bf16[2,128,256]{2,1,0:T(8,128)(2,1)S(1)}, bf16[2,128,256]{2,1,0:T(8,128)(2,1)S(1)}, u32[]{:S(2)}, u32[]{:S(2)}) collective-permute-start(bf16[2,128,256]{2,1,0:T(8,128)(2,1)S(1)} %get-tuple-element.49), channel_id=1, source_target_pairs={{0,2},{1,3},{2,0},{3,1},{4,6},{5,7},{6,4},{7,5},{8,10},{9,11},{10,... | collective-permute-start | bytes 393224 | tf_op jit(solution)/shard_map/ppermute | solution.py:281
  31.6 10.0 %collective-permute-start.9 = (bf16[2,128,256]{2,1,0:T(8,128)(2,1)S(1)}, bf16[2,128,256]{2,1,0:T(8,128)(2,1)S(1)}, u32[]{:S(2)}, u32[]{:S(2)}) collective-permute-start(bf16[2,128,256]{2,1,0:T(8,128)(2,1)S(1)} %get-tuple-element.50), channel_id=1, source_target_pairs={{0,3},{1,2},{2,1},{3,0},{4,7},{5,6},{6,5},{7,4},{8,11},{9,10},{10,... | collective-permute-start | bytes 393224 | tf_op jit(solution)/shard_map/ppermute | solution.py:281
  31.8 11.4 %collective-permute-start.11 = (bf16[256,256]{1,0:T(8,128)(2,1)S(1)}, bf16[256,256]{1,0:T(8,128)(2,1)S(1)}, u32[]{:S(2)}, u32[]{:S(2)}) collective-permute-start(bf16[256,256]{1,0:T(8,128)(2,1)S(1)} %get-tuple-element.58), channel_id=1, source_target_pairs={{0,8},{4,12},{8,0},{12,4},{16,24},{20,28},{24,16},{28,20},{1,9},{5... | collective-permute-start | bytes 393224 | tf_op jit(solution)/shard_map/ppermute | solution.py:281
  33.5 9.7 %collective-permute-start.12 = (bf16[256,256]{1,0:T(8,128)(2,1)S(1)}, bf16[256,256]{1,0:T(8,128)(2,1)S(1)}, u32[]{:S(2)}, u32[]{:S(2)}) collective-permute-start(bf16[256,256]{1,0:T(8,128)(2,1)S(1)} %get-tuple-element.59), channel_id=1, source_target_pairs={{0,16},{4,20},{8,24},{12,28},{16,0},{20,4},{24,8},{28,12},{1,17},{... | collective-permute-start | bytes 393224 | tf_op jit(solution)/shard_map/ppermute | solution.py:281
  35.0 8.2 %collective-permute-start.13 = (bf16[256,256]{1,0:T(8,128)(2,1)S(1)}, bf16[256,256]{1,0:T(8,128)(2,1)S(1)}, u32[]{:S(2)}, u32[]{:S(2)}) collective-permute-start(bf16[256,256]{1,0:T(8,128)(2,1)S(1)} %get-tuple-element.60), channel_id=1, source_target_pairs={{0,24},{4,28},{8,16},{12,20},{16,8},{20,12},{24,0},{28,4},{1,25},{... | collective-permute-start | bytes 393224 | tf_op jit(solution)/shard_map/ppermute | solution.py:281

commit v6 on v5

--- a/solution.py
+++ b/solution.py
@@ -88,6 +88,8 @@
     order, hub_ids, adj, same, other, deg, own, cot, w_neigh, raw, *rest, tile, chunk, group
 ):
     results, blocks = rest[:-1], rest[-1]
+    if results:
+        results, blocks = results[:-1] + rest[-1:], results[-1]
     row = lax.axis_index("row")
     sections, nodes, hub_rows = adj.shape
     for s in range(sections):
@@ -108,7 +110,7 @@
         weights = jnp.concatenate([adj[s, at, :] for s in range(sections)], axis=1)
         raw[at, :] = jnp.dot(weights, blocks[...], preferred_element_type=F32)
     if results:
-        out, grad, turned = results
+        out, grad, acc, turned = results
         first = tiles - out.shape[0] // tile
         for start in range(first, tiles, group):
             here = pl.ds((start - first) * tile, group * tile)
@@ -119,6 +121,10 @@
             out[here, :] = o
             grad[here, :] = g
             turned[:, here] = a.T
+        acc[...] = jnp.zeros_like(acc)
+        for s in range(sections):
+            weights = jnp.concatenate([adj[s, rows_at(order[i], tile), :] for i in range(first, tiles)])
+            acc[hub_ids[s] ^ row] += jnp.dot(turned[...], weights, preferred_element_type=F32)
 
 
 def landed_kernel(count, dst, order, place, raw_in, deg_in, own, cot, adj, w_neigh, *rest, peers, slots, tile, group):
@@ -173,16 +179,15 @@
             back[d][k] = (part * jnp.where(alive, 1.0, 0.0).astype(F32)).astype(BF16)
 
 
-def hub_backward_kernel(order, hub_ids, adj, *rest, tile):
-    pieces, (even, odd, acc) = rest[:-3], rest[-3:]
+def hub_backward_kernel(order, hub_ids, adj, turned, *rest, tile):
+    before, (even, odd, acc) = rest[:-3], rest[-3:]
     row = lax.axis_index("row")
-    sections, nodes, _ = adj.shape
-    there = [rows_at(order[i], tile) for i in range(nodes // tile)]
-    acc[...] = jnp.zeros_like(acc)
+    sections = adj.shape[0]
+    there = [rows_at(order[i], tile) for i in range(turned.shape[1] // tile)]
+    acc[...] = before[0][...] if before else jnp.zeros_like(acc)
     for s in range(sections):
-        turned = jnp.concatenate([piece[...] for piece in pieces], axis=1)
         weights = jnp.concatenate([adj[s, at, :] for at in there])
-        acc[hub_ids[s] ^ row] += jnp.dot(turned, weights, preferred_element_type=F32)
+        acc[hub_ids[s] ^ row] += jnp.dot(turned[...], weights, preferred_element_type=F32)
     for e in range(even.shape[0]):
         even[e] = acc[2 * e].astype(BF16)
         odd[e] = acc[2 * e + 1].astype(BF16)
@@ -222,40 +227,41 @@
         out[...] = (even[e].astype(F32) + came[e].astype(F32)).astype(BF16)
 
 
-def tiles_kernel(send, self_grad, *rest, peers, slots, tile):
-    back, (_, out, head, total, done, sems) = rest[:peers], rest[peers:]
+def final_kernel(send, self_grad, *rest, peers, slots, tile):
+    back, hub, (_, out, total, done, sems) = rest[:peers], rest[peers:-5], rest[-5:]
     col = lax.axis_index("col")
+    head = pl.ds(0, hub[0].shape[1])
     targets = [send[k, col ^ d] for d in range(peers) for k in range(slots)]
     spots = [rows_at(target, tile) for target in targets]
-    top = pl.ds(0, head.shape[0])
-    total[top, :] = self_grad[top, :]
+    total[head, :] = self_grad[head, :]
     for at in spots:
         total[at, :] = self_grad[at, :]
     for i, at in enumerate(spots):
         total[at, :] += back[i // slots][i % slots].astype(F32)
-    copies = []
-    for i, at in enumerate(spots):
-        fresh = targets[i] * tile >= head.shape[0]
-        for other in targets[:i]:
-            fresh = fresh & (other != targets[i])
-        done[i] = total[at, :].astype(BF16)
-        copy = pltpu.make_async_copy(done.at[i], out.at[at], sems.at[i])
-        pl.when(fresh)(copy.start)
-        copies.append((fresh, copy))
-    head[...] = total[top, :]
-    for fresh, copy in copies:
-        pl.when(fresh)(copy.wait)
-
-
-def head_kernel(head, *rest):
-    hub, (_, out, done, sem) = rest[:-4], rest[-4:]
     come = hub[0][...].astype(F32)
     for h in hub[1:]:
         come = come + h[...].astype(F32)
-    done[...] = (head[...] + come.T).astype(BF16)
-    copy = pltpu.make_async_copy(done, out.at[pl.ds(0, done.shape[0])], sem)
-    copy.start()
-    copy.wait()
+    total[head, :] += come.T
+    done[head, :] = total[head, :].astype(BF16)
+    copies = [(None, pltpu.make_async_copy(done.at[head], out.at[head], sems.at[len(spots)]))]
+    copies[0][1].start()
+    for i, at in enumerate(spots):
+        fresh = targets[i] * tile >= hub[0].shape[1]
+        for other in targets[:i]:
+            fresh = fresh & (other != targets[i])
+        copy = pltpu.make_async_copy(done.at[at], out.at[at], sems.at[i])
+        copies.append((fresh, copy))
+
+        @pl.when(fresh)
+        def _(at=at, copy=copy):
+            done[at, :] = total[at, :].astype(BF16)
+            copy.start()
+
+    for fresh, copy in copies:
+        if fresh is None:
+            copy.wait()
+        else:
+            pl.when(fresh)(copy.wait)
 
 
 def shards(
@@ -330,12 +336,16 @@
         compiler_params=params,
         name="degree",
     )(adj)
+    early_shapes = results(tiles - first)[:2]
+    if early_shapes:
+        early_shapes.append(shape((n_row, width, hub_rows), F32))
     raw, *others = pl.pallas_call(
         functools.partial(forward_kernel, tile=tile, chunk=256, group=group),
         in_specs=[SMEM] * 2 + [VMEM] * 7,
-        out_specs=[VMEM] * (1 + len(results(tiles - first))),
-        scratch_shapes=[pltpu.VMEM((sections * hub_rows, width), BF16)],
-        out_shape=[shape((nodes, width), F32)] + results(tiles - first),
+        out_specs=[VMEM] * (1 + len(early_shapes)),
+        scratch_shapes=[pltpu.VMEM((sections * hub_rows, width), BF16)]
+        + [pltpu.VMEM(x.shape, x.dtype) for x in results(tiles - first)[2:]],
+        out_shape=[shape((nodes, width), F32)] + early_shapes,
         compiler_params=params,
         cost_estimate=cost(2 * sections * nodes * hub_rows * width),
         name="forward",
@@ -349,7 +359,7 @@
         compiler_params=params,
         name="landed",
     )(count, dst, tile_at, place, raw, deg, own, cotangent, weights, w_neigh, *incoming)
-    outs, grads, turned = zip(*([landed[:3]] + ([others] if others else [])))
+    outs, grads = zip(*([landed[:2]] + ([others[:2]] if others else [])))
     going = landed[3:]
     returned = [going[0]] + [None] * (peers - 1)
     for d in order:
@@ -358,14 +368,14 @@
     half = shape((n_row // 2, width, hub_rows), BF16)
     even, odd = pl.pallas_call(
         functools.partial(hub_backward_kernel, tile=tile),
-        in_specs=[SMEM] * 2 + [VMEM] * (1 + len(turned)),
+        in_specs=[SMEM] * 2 + [VMEM] * (2 + len(others[2:])),
         out_specs=[VMEM] * 2,
         scratch_shapes=[pltpu.VMEM((n_row, width, hub_rows), F32)],
         out_shape=[half, half],
         compiler_params=params,
         cost_estimate=cost(2 * sections * nodes * hub_rows * width),
         name="hub_backward",
-    )(tile_at, hub_ids, adj, *turned)
+    )(tile_at, hub_ids, adj, landed[2], *others[2:])
     came = across(odd, "row", n_row, 1)
     output, feature_grad, self_grad = pl.pallas_call(
         functools.partial(self_kernel, tile=tile),
@@ -385,31 +395,20 @@
     )(even, came)
     hubs = [sums[0]] + [across(sums[d // 2], "row", n_row, d) for d in range(2, n_row, 2)]
 
-    whole = shape((nodes, width), BF16)
-    feature_grad, head = pl.pallas_call(
-        functools.partial(tiles_kernel, **sizes),
-        in_specs=[SMEM] + [VMEM] * (1 + peers) + [HBM],
-        out_specs=[HBM, VMEM],
+    feature_grad = pl.pallas_call(
+        functools.partial(final_kernel, **sizes),
+        in_specs=[SMEM] + [VMEM] * (1 + peers + len(hubs)) + [HBM],
+        out_specs=HBM,
         scratch_shapes=[
             pltpu.VMEM((nodes, width), F32),
-            pltpu.VMEM((peers * slots, tile, width), BF16),
-            pltpu.SemaphoreType.DMA((peers * slots,)),
+            pltpu.VMEM((nodes, width), BF16),
+            pltpu.SemaphoreType.DMA((peers * slots + 1,)),
         ],
-        out_shape=[whole, shape((hub_rows, width), F32)],
-        input_output_aliases={2 + peers: 0},
-        compiler_params=params,
-        name="tiles_done",
-    )(send, self_grad, *returned, feature_grad)
-    feature_grad = pl.pallas_call(
-        head_kernel,
-        in_specs=[VMEM] * (1 + len(hubs)) + [HBM],
-        out_specs=HBM,
-        scratch_shapes=[pltpu.VMEM((hub_rows, width), BF16), pltpu.SemaphoreType.DMA],
-        out_shape=whole,
-        input_output_aliases={1 + len(hubs): 0},
-        compiler_params=params,
-        name="head",
-    )(head, *hubs, feature_grad)
+        out_shape=shape((nodes, width), BF16),
+        input_output_aliases={2 + peers + len(hubs): 0},
+        compiler_params=params,
+        name="final",
+    )(send, self_grad, *returned, *hubs, feature_grad)
     return (output, feature_grad)
 
 

time: 44.2 us -> 43.6 us (0.986)
  Pallas kernels: 16.6 us -> 16.1 us
    pallas_call x1, Pallas kernels: 3.31 us -> 4.22 us  [shards(): pl.pallas_call(functools.partial(forward_kernel, tile=tile, chunk=256, gr...]
    pallas_call x1, Pallas kernels: 2.61 us -> 1.78 us  [shards(): pl.pallas_call(functools.partial(hub_backward_kernel, tile=tile), in_spec...]
    pallas_call x2 -> x1, Pallas kernels: 2.36 us -> 1.67 us  [shards(): pl.pallas_call(functools.partial(final_kernel, **sizes), in_specs=[SMEM]...]
  transfers between devices with their start and end apart: 14 -> 14, of which waited for: 3 -> 2; matrix products, arithmetic and copies ran while one was open for 0% -> 0% of each run, Pallas kernels for 22% -> 21%
where the time goes in v6:
time: 43.6 us; the launch traced here: 43.4 us
  starting transfers between devices  20 us (46%)
  Pallas kernels  16.1 us (37%)
  local copies, waits for them, and re-layouts  4.06 us (9%)
  waiting for transfers between devices  2.36 us (5%)
  between operations  0.88 us (2%)
    ppermute x14, starting transfers between devices, across(): return lax.ppermute(x, axis, [(i, i ^ d) for i in range(size)])  20 us
    pallas_call x1, Pallas kernels, shards(): pl.pallas_call(functools.partial(forward_kernel, tile=tile, chunk=256, gr...  4.22 us
    unnamed x24, local copies, waits for them, and re-layouts  4.06 us
    pallas_call x1, Pallas kernels, shards(): pl.pallas_call(functools.partial(self_kernel, tile=tile), in_specs=[SMEM]...  2.39 us
    ppermute x14, waiting for transfers between devices, across(): return lax.ppermute(x, axis, [(i, i ^ d) for i in range(size)])  2.36 us
    pallas_call x1, Pallas kernels, shards(): pl.pallas_call(functools.partial(landed_kernel, group=group, **sizes), in...  2.04 us
    pallas_call x1, Pallas kernels, shards(): pl.pallas_call(functools.partial(hub_backward_kernel, tile=tile), in_spec...  1.78 us
    pallas_call x1, Pallas kernels, shards(): pl.pallas_call(functools.partial(final_kernel, **sizes), in_specs=[SMEM]...  1.67 us
  transfers between devices with their start and end apart: 14, of which 2 were waited for; matrix products, arithmetic and copies ran while one was open for 0% of the time, Pallas kernels for 21%

profile of v6, /device:TPU:0, one launch (start us, length us, event | category | flops | bytes accessed | tf_op | source)
XLA Modules:
  0.0 43.4 jit_solution(3024613774132859160)
XLA Ops:
  0.6 1.3 %pick.1 = (bf16[2048,256]{1,0:T(8,128)(2,1)S(1)}, bf16[256,256]{1,0:T(8,128)(2,1)S(1)}, bf16[2,128,256]{2,1,0:T(8,128)(2,1)S(1)}, bf16[2,128,256]{2,1,0:T(8,128)...) custom-call(s32[2,4]{1,0:T(2,128)} %bitcast.22, bf16[2048,256]{1,0:T(8,128)(2,1)} %feats_in.1), custom_call_target="tpu_custom_call" | custom-call | flops 1000000000 | tf_op jit(solution)/shard_map/pick/pallas_call | solution.py:291
  1.9 4.0 %collective-permute-start.2 = (bf16[256,256]{1,0:T(8,128)(2,1)S(1)}, bf16[256,256]{1,0:T(8,128)(2,1)S(1)}, u32[]{:S(2)}, u32[]{:S(2)}) collective-permute-start(bf16[256,256]{1,0:T(8,128)(2,1)S(1)} %get-tuple-element.32), channel_id=1, source_target_pairs={{0,24},{4,28},{8,16},{12,20},{16,8},{20,12},{24,0},{28,4},{1,25},{... | collective-permute-start | bytes 393224 | tf_op jit(solution)/shard_map/ppermute | solution.py:287
  5.9 0.5 %collective-permute-start.1 = (bf16[256,256]{1,0:T(8,128)(2,1)S(1)}, bf16[256,256]{1,0:T(8,128)(2,1)S(1)}, u32[]{:S(2)}, u32[]{:S(2)}) collective-permute-start(bf16[256,256]{1,0:T(8,128)(2,1)S(1)} %get-tuple-element.32), channel_id=1, source_target_pairs={{0,16},{4,20},{8,24},{12,28},{16,0},{20,4},{24,8},{28,12},{1,17},{... | collective-permute-start | bytes 393224 | tf_op jit(solution)/shard_map/ppermute | solution.py:287
  6.4 0.1 collective-permute-start
  6.6 2.0 %collective-permute-start.4 = (bf16[2,128,256]{2,1,0:T(8,128)(2,1)S(1)}, bf16[2,128,256]{2,1,0:T(8,128)(2,1)S(1)}, u32[]{:S(2)}, u32[]{:S(2)}) collective-permute-start(bf16[2,128,256]{2,1,0:T(8,128)(2,1)S(1)} %get-tuple-element.36), channel_id=1, source_target_pairs={{0,1},{1,0},{2,3},{3,2},{4,5},{5,4},{6,7},{7,6},{8,9},{9,8},{10,11... | collective-permute-start | bytes 393224 | tf_op jit(solution)/shard_map/ppermute | solution.py:287
  8.5 2.6 %collective-permute-start.5 = (bf16[2,128,256]{2,1,0:T(8,128)(2,1)S(1)}, bf16[2,128,256]{2,1,0:T(8,128)(2,1)S(1)}, u32[]{:S(2)}, u32[]{:S(2)}) collective-permute-start(bf16[2,128,256]{2,1,0:T(8,128)(2,1)S(1)} %get-tuple-element.37), channel_id=1, source_target_pairs={{0,2},{1,3},{2,0},{3,1},{4,6},{5,7},{6,4},{7,5},{8,10},{9,11},{10,... | collective-permute-start | bytes 393224 | tf_op jit(solution)/shard_map/ppermute | solution.py:287
  11.1 2.8 %copy-done = bf16[1,6,2048,256]{3,2,1,0:T(8,128)(2,1)S(1)} copy-done((bf16[1,6,2048,256]{3,2,1,0:T(8,128)(2,1)S(1)}, bf16[1,6,2048,256]{3,2,1,0:T(8,128)(2,1)}, u32[]{:S(2)}) %copy-start) | copy-done | bytes 6291480
  13.9 0.9 %degree.1.deg.deg_in = f32[2048,128]{1,0:T(8,128)S(1)} custom-call(bf16[6,2048,256]{2,1,0:T(8,128)(2,1)S(1)} %bitcast.13), custom_call_target="tpu_custom_call" | custom-call | tf_op jit(solution)/shard_map/degree/pallas_call | solution.py:331
  14.8 0.0 copy-done.4
  14.8 0.0 copy-start.8
  14.8 0.4 early.1.own
  15.3 0.0 collective-permute-done.2
  15.3 0.1 collective-permute-start.6
  15.4 0.0 collective-permute-done.1
  15.4 0.0 collective-permute-done
  15.4 0.1 pad_maximum_fusion.same
  15.5 0.1 collective-permute-start.3
  15.5 0.0 slice-start
  15.6 0.0 copy-start.1
  15.6 0.0 copy-start.2
  15.6 0.0 copy-start.5
  15.6 1.2 %tables.1 = (s32[16]{0:T(128)S(1)}, s32[16]{0:T(128)S(1)}) custom-call(s32[1,4]{1,0:T(1,128)S(1)} %copy-done.8, s32[2,4]{1,0:T(2,128)S(1)} %bitcast.20), custom_call_target="tpu_custom_call" | custom-call | flops 10000000000 | tf_op jit(solution)/shard_map/tables/pallas_call | solution.py:316
  16.8 0.6 %collective-permute-done.3.other = bf16[4,256,256]{2,1,0:T(8,128)(2,1)S(1)} collective-permute-done((bf16[4,256,256]{2,1,0:T(8,128)(2,1)S(1)}, bf16[4,256,256]{2,1,0:T(8,128)(2,1)S(1)}, u32[]{:S(2)}, u32[]{:S(2)}) %collective-permute-start.3) | collective-permute-done | bytes 524320 | tf_op jit(solution)/shard_map/ppermute | solution.py:287
  17.4 0.3 slice-done
  17.7 0.7 %slice-done.1 = s8[2097152]{0:T(1024)(128)(4,1)S(1)} async-done(((s8[6291456]{0:T(1024)(128)(4,1)}), s8[2097152]{0:T(1024)(128)(4,1)S(1)}, s32[]{:S(2)}) %slice-start.1) | async-done | bytes 2097176
  18.4 0.2 copy-done.1
  18.7 4.2 %forward.1 = (f32[2048,256]{1,0:T(8,128)S(1)}, bf16[1024,256]{1,0:T(8,128)(2,1)S(1)}, bf16[1024,256]{1,0:T(8,128)(2,1)S(1)}, f32[8,256,256]{2,1,0:T(8,128)S(1)}) custom-call(s32[16]{0:T(128)S(1)} %get-tuple-element.30.order, s32[6]{0:T(128)S(1)} %copy-done.5, bf16[6,2048,256]{2,1,0:T(8,128)(2,1)S(1)} %bitcast.16, ...), custom_call_target="tpu_custom_call" | custom-call | flops 1610612736 | bytes 4194304 | tf_op jit(solution)/shard_map/forward/pallas_call | solution.py:342
  22.9 0.0 collective-permute-done.4.rest_1_
  22.9 0.0 collective-permute-done.6.rest_3_
  22.9 2.0 %landed.1 = (bf16[1024,256]{1,0:T(8,128)(2,1)S(1)}, bf16[1024,256]{1,0:T(8,128)(2,1)S(1)}, bf16[256,1024]{1,0:T(8,128)(2,1)S(1)}, bf16[2,128,256]{2,1,0:T(8,128)...) custom-call(s32[1,4]{1,0:T(1,128)S(1)} %copy-done.8, ...), custom_call_target="tpu_custom_call" | custom-call | tf_op jit(solution)/shard_map/landed/pallas_call | solution.py:353
  25.0 1.8 %hub_backward.1 = (bf16[4,256,256]{2,1,0:T(8,128)(2,1)S(1)}, bf16[4,256,256]{2,1,0:T(8,128)(2,1)S(1)}) custom-call(s32[16]{0:T(128)S(1)} %get-tuple-element.30.order, s32[6]{0:T(128)S(1)} %copy-done.5, bf16[6,2048,256]{2,1,0:T(8,128)(2,1)S(1)} %bitcast.17, bf16[256,1024]{1,0:T(8,128)(2,1)S(1)} %get-tuple-element.49.turned, ...), custom_call_target="tpu_custom_call" | custom-call | flops 1610612736 | bytes 4194304 | tf_op jit(solution)/shard_map/hub_backward/pallas_call | solution.py:369
  26.8 0.0 copy-start.7
  26.8 0.6 %collective-permute-start.10 = (bf16[4,256,256]{2,1,0:T(8,128)(2,1)S(1)}, bf16[4,256,256]{2,1,0:T(8,128)(2,1)S(1)}, u32[]{:S(2)}, u32[]{:S(2)}) collective-permute-start(bf16[4,256,256]{2,1,0:T(8,128)(2,1)S(1)} %get-tuple-element.52), channel_id=1, source_target_pairs={{0,4},{4,0},{8,12},{12,8},{16,20},{20,16},{24,28},{28,24},{1,5},{5... | collective-permute-start | bytes 1572872 | tf_op jit(solution)/shard_map/ppermute | solution.py:287
  27.3 0.9 %collective-permute-start.7 = (bf16[2,128,256]{2,1,0:T(8,128)(2,1)S(1)}, bf16[2,128,256]{2,1,0:T(8,128)(2,1)S(1)}, u32[]{:S(2)}, u32[]{:S(2)}) collective-permute-start(bf16[2,128,256]{2,1,0:T(8,128)(2,1)S(1)} %get-tuple-element.46), channel_id=1, source_target_pairs={{0,1},{1,0},{2,3},{3,2},{4,5},{5,4},{6,7},{7,6},{8,9},{9,8},{10,11... | collective-permute-start | bytes 393224 | tf_op jit(solution)/shard_map/ppermute | solution.py:287
  28.2 3.5 %collective-permute-start.8 = (bf16[2,128,256]{2,1,0:T(8,128)(2,1)S(1)}, bf16[2,128,256]{2,1,0:T(8,128)(2,1)S(1)}, u32[]{:S(2)}, u32[]{:S(2)}) collective-permute-start(bf16[2,128,256]{2,1,0:T(8,128)(2,1)S(1)} %get-tuple-element.47), channel_id=1, source_target_pairs={{0,2},{1,3},{2,0},{3,1},{4,6},{5,7},{6,4},{7,5},{8,10},{9,11},{10,... | collective-permute-start | bytes 393224 | tf_op jit(solution)/shard_map/ppermute | solution.py:287
  31.7 0.0 collective-permute-start.9
  31.7 0.0 collective-permute-done.10.came
  31.7 0.1 pair_add.1
  31.9 1.7 %collective-permute-start.11 = (bf16[256,256]{1,0:T(8,128)(2,1)S(1)}, bf16[256,256]{1,0:T(8,128)(2,1)S(1)}, u32[]{:S(2)}, u32[]{:S(2)}) collective-permute-start(bf16[256,256]{1,0:T(8,128)(2,1)S(1)} %get-tuple-element.54), channel_id=1, source_target_pairs={{0,8},{4,12},{8,0},{12,4},{16,24},{20,28},{24,16},{28,20},{1,9},{5... | collective-permute-start | bytes 393224 | tf_op jit(solution)/shard_map/ppermute | solution.py:287
  33.6 1.5 %collective-permute-start.12 = (bf16[256,256]{1,0:T(8,128)(2,1)S(1)}, bf16[256,256]{1,0:T(8,128)(2,1)S(1)}, u32[]{:S(2)}, u32[]{:S(2)}) collective-permute-start(bf16[256,256]{1,0:T(8,128)(2,1)S(1)} %get-tuple-element.55), channel_id=1, source_target_pairs={{0,16},{4,20},{8,24},{12,28},{16,0},{20,4},{24,8},{28,12},{1,17},{... | collective-permute-start | bytes 393224 | tf_op jit(solution)/shard_map/ppermute | solution.py:287
  35.1 0.0 collective-permute-done.7.rest_1_
  35.1 2.4 %collective-permute-start.13 = (bf16[256,256]{1,0:T(8,128)(2,1)S(1)}, bf16[256,256]{1,0:T(8,128)(2,1)S(1)}, u32[]{:S(2)}, u32[]{:S(2)}) collective-permute-start(bf16[256,256]{1,0:T(8,128)(2,1)S(1)} %get-tuple-element.56), channel_id=1, source_target_pairs={{0,24},{4,28},{8,16},{12,20},{16,8},{20,12},{24,0},{28,4},{1,25},{... | collective-permute-start | bytes 393224 | tf_op jit(solution)/shard_map/ppermute | solution.py:287
  37.6 2.4 %self.1 = (bf16[2048,256]{1,0:T(8,128)(2,1)}, bf16[2048,256]{1,0:T(8,128)(2,1)}, f32[2048,256]{1,0:T(8,128)S(1)}) custom-call(s32[16]{0:T(128)S(1)} %get-tuple-element.30.order, bf16[256,256]{1,0:T(8,128)(2,1)S(1)} %copy-done.4, bf16[1024,256]{1,0:T(8,128)(2,1)S(1)} %get-tuple-element.39.rest_0_, bf16[1024,256]{1,0:T(8,128)(2,1)S(1)} %get-tuple-element.40.rest_1_, ...), custom_call_target="tpu_custom_call" | custom-call | tf_op jit(solution)/shard_map/self/pallas_call | solution.py:380
  40.0 1.7 %collective-permute-done.8.rest_2_ = bf16[2,128,256]{2,1,0:T(8,128)(2,1)S(1)} collective-permute-done((bf16[2,128,256]{2,1,0:T(8,128)(2,1)S(1)}, bf16[2,128,256]{2,1,0:T(8,128)(2,1)S(1)}, u32[]{:S(2)}, u32[]{:S(2)}) %collective-permute-start.8) | collective-permute-done | bytes 131104 | tf_op jit(solution)/shard_map/ppermute | solution.py:287
  41.7 0.0 collective-permute-done.11.rest_5_
  41.7 0.0 collective-permute-done.12.rest_6_
  41.7 0.0 collective-permute-done.13.rest_7_
  41.7 1.7 %final.1 = bf16[2048,256]{1,0:T(8,128)(2,1)} custom-call(s32[2,4]{1,0:T(2,128)S(1)} %bitcast.23, f32[2048,256]{1,0:T(8,128)S(1)} %get-tuple-element.44.self_grad, bf16[2,128,256]{2,1,0:T(8,128)(2,1)S(1)} %get-tuple-element.45.rest_0_, bf16[2,128,256]{2,1,0:T(8,128)(2,1)S(1)} %collective-permute-done.7.rest_1_, ...), custom_call_target="tpu_custom_call", output_to_operand_aliasing={{}: (10, {})} | custom-call | tf_op jit(solution)/shard_map/final/pallas_call | solution.py:398
  (16 shorter events, 0.0 us)
Async XLA Ops:
  1.9 13.3 %collective-permute-start.2 = (bf16[256,256]{1,0:T(8,128)(2,1)S(1)}, bf16[256,256]{1,0:T(8,128)(2,1)S(1)}, u32[]{:S(2)}, u32[]{:S(2)}) collective-permute-start(bf16[256,256]{1,0:T(8,128)(2,1)S(1)} %get-tuple-element.32), channel_id=1, source_target_pairs={{0,24},{4,28},{8,16},{12,20},{16,8},{20,12},{24,0},{28,4},{1,25},{... | collective-permute-start | bytes 393224 | tf_op jit(solution)/shard_map/ppermute | solution.py:287
  5.9 9.5 %collective-permute-start.1 = (bf16[256,256]{1,0:T(8,128)(2,1)S(1)}, bf16[256,256]{1,0:T(8,128)(2,1)S(1)}, u32[]{:S(2)}, u32[]{:S(2)}) collective-permute-start(bf16[256,256]{1,0:T(8,128)(2,1)S(1)} %get-tuple-element.32), channel_id=1, source_target_pairs={{0,16},{4,20},{8,24},{12,28},{16,0},{20,4},{24,8},{28,12},{1,17},{... | collective-permute-start | bytes 393224 | tf_op jit(solution)/shard_map/ppermute | solution.py:287
  6.4 9.0 %collective-permute-start = (bf16[256,256]{1,0:T(8,128)(2,1)S(1)}, bf16[256,256]{1,0:T(8,128)(2,1)S(1)}, u32[]{:S(2)}, u32[]{:S(2)}) collective-permute-start(bf16[256,256]{1,0:T(8,128)(2,1)S(1)} %get-tuple-element.32), channel_id=1, source_target_pairs={{0,8},{4,12},{8,0},{12,4},{16,24},{20,28},{24,16},{28,20},{1,9},{5... | collective-permute-start | bytes 393224 | tf_op jit(solution)/shard_map/ppermute | solution.py:287
  6.6 16.3 %collective-permute-start.4 = (bf16[2,128,256]{2,1,0:T(8,128)(2,1)S(1)}, bf16[2,128,256]{2,1,0:T(8,128)(2,1)S(1)}, u32[]{:S(2)}, u32[]{:S(2)}) collective-permute-start(bf16[2,128,256]{2,1,0:T(8,128)(2,1)S(1)} %get-tuple-element.36), channel_id=1, source_target_pairs={{0,1},{1,0},{2,3},{3,2},{4,5},{5,4},{6,7},{7,6},{8,9},{9,8},{10,11... | collective-permute-start | bytes 393224 | tf_op jit(solution)/shard_map/ppermute | solution.py:287
  8.5 14.4 %collective-permute-start.5 = (bf16[2,128,256]{2,1,0:T(8,128)(2,1)S(1)}, bf16[2,128,256]{2,1,0:T(8,128)(2,1)S(1)}, u32[]{:S(2)}, u32[]{:S(2)}) collective-permute-start(bf16[2,128,256]{2,1,0:T(8,128)(2,1)S(1)} %get-tuple-element.37), channel_id=1, source_target_pairs={{0,2},{1,3},{2,0},{3,1},{4,6},{5,7},{6,4},{7,5},{8,10},{9,11},{10,... | collective-permute-start | bytes 393224 | tf_op jit(solution)/shard_map/ppermute | solution.py:287
  11.1 2.8 %copy-start = (bf16[1,6,2048,256]{3,2,1,0:T(8,128)(2,1)S(1)}, bf16[1,6,2048,256]{3,2,1,0:T(8,128)(2,1)}, u32[]{:S(2)}) copy-start(bf16[1,6,2048,256]{3,2,1,0:T(8,128)(2,1)} %param.16) | copy-start | bytes 18874372
  13.9 0.9 %copy-start.4 = (bf16[256,256]{1,0:T(8,128)(2,1)S(1)}, bf16[256,256]{1,0:T(8,128)(2,1)}, u32[]{:S(2)}) copy-start(bf16[256,256]{1,0:T(8,128)(2,1)} %w_self.3) | copy-start | bytes 393220
  13.9 0.9 %copy-start.9 = (f32[256]{0:T(256)S(1)}, f32[256]{0:T(256)}, u32[]{:S(2)}) copy-start(f32[256]{0:T(256)} %param.14) | copy-start | bytes 3076
  14.8 0.7 %copy-start.6 = (s32[1,4,2]{1,2,0:T(2,128)S(1)}, s32[1,4,2]{1,2,0:T(2,128)}, u32[]{:S(2)}) copy-start(s32[1,4,2]{1,2,0:T(2,128)} %param.19) | copy-start | bytes 100
  14.8 0.7 %copy-start.8 = (s32[1,4]{1,0:T(1,128)S(1)}, s32[1,4]{1,0:T(1,128)}, u32[]{:S(2)}) copy-start(s32[1,4]{1,0:T(1,128)} %count.3) | copy-start | bytes 52
  15.3 7.6 %collective-permute-start.6 = (bf16[2,128,256]{2,1,0:T(8,128)(2,1)S(1)}, bf16[2,128,256]{2,1,0:T(8,128)(2,1)S(1)}, u32[]{:S(2)}, u32[]{:S(2)}) collective-permute-start(bf16[2,128,256]{2,1,0:T(8,128)(2,1)S(1)} %get-tuple-element.38), channel_id=1, source_target_pairs={{0,3},{1,2},{2,1},{3,0},{4,7},{5,6},{6,5},{7,4},{8,11},{9,10},{10,... | collective-permute-start | bytes 393224 | tf_op jit(solution)/shard_map/ppermute | solution.py:287
  15.5 2.0 %collective-permute-start.3 = (bf16[4,256,256]{2,1,0:T(8,128)(2,1)S(1)}, bf16[4,256,256]{2,1,0:T(8,128)(2,1)S(1)}, u32[]{:S(2)}, u32[]{:S(2)}) collective-permute-start(bf16[4,256,256]{2,1,0:T(8,128)(2,1)S(1)} %pad_maximum_fusion.same), channel_id=1, source_target_pairs={{0,4},{4,0},{8,12},{12,8},{16,20},{20,16},{24,28},{28,24},{1,5},{5... | collective-permute-start | bytes 1572872 | tf_op jit(solution)/shard_map/ppermute | solution.py:287
  15.5 2.2 %slice-start = ((s8[6291456]{0:T(1024)(128)(4,1)}), s8[4194304]{0:T(1024)(128)(4,1)S(1)}, s32[]{:S(2)}) async-start(s8[6291456]{0:T(1024)(128)(4,1)} %bitcast.14), calls=%async_computation | async-start | bytes 8388608
  15.6 2.8 %slice-start.1 = ((s8[6291456]{0:T(1024)(128)(4,1)}), s8[2097152]{0:T(1024)(128)(4,1)S(1)}, s32[]{:S(2)}) async-start(s8[6291456]{0:T(1024)(128)(4,1)} %bitcast.14), calls=%async_computation.1 | async-start | bytes 4194304
  15.6 3.1 %copy-start.1 = (bf16[2048,256]{1,0:T(8,128)(2,1)S(1)}, bf16[2048,256]{1,0:T(8,128)(2,1)}, u32[]{:S(2)}) copy-start(bf16[2048,256]{1,0:T(8,128)(2,1)} %cot.3) | copy-start | bytes 3145732
  15.6 3.1 %copy-start.2 = (bf16[256,256]{1,0:T(8,128)(2,1)S(1)}, bf16[256,256]{1,0:T(8,128)(2,1)}, u32[]{:S(2)}) copy-start(bf16[256,256]{1,0:T(8,128)(2,1)} %w_neigh.3) | copy-start | bytes 393220
  15.6 3.0 %copy-start.5 = (s32[6]{0:T(128)S(1)}, s32[6]{0:T(128)}, u32[]{:S(2)}) copy-start(s32[6]{0:T(128)} %hub_ids.3) | copy-start | bytes 76
  18.7 4.3 %copy-start.3 = (bf16[1,4,2,128,128]{4,3,2,1,0:T(8,128)(2,1)S(1)}, bf16[1,4,2,128,128]{4,3,2,1,0:T(8,128)(2,1)}, u32[]{:S(2)}) copy-start(bf16[1,4,2,128,128]{4,3,2,1,0:T(8,128)(2,1)} %param.20) | copy-start | bytes 786436
  26.8 14.9 %copy-start.7 = (s32[1,4,2]{1,2,0:T(2,128)S(1)}, s32[1,4,2]{1,2,0:T(2,128)}, u32[]{:S(2)}) copy-start(s32[1,4,2]{1,2,0:T(2,128)} %param.17) | copy-start | bytes 100
  26.8 4.9 %collective-permute-start.10 = (bf16[4,256,256]{2,1,0:T(8,128)(2,1)S(1)}, bf16[4,256,256]{2,1,0:T(8,128)(2,1)S(1)}, u32[]{:S(2)}, u32[]{:S(2)}) collective-permute-start(bf16[4,256,256]{2,1,0:T(8,128)(2,1)S(1)} %get-tuple-element.52), channel_id=1, source_target_pairs={{0,4},{4,0},{8,12},{12,8},{16,20},{20,16},{24,28},{28,24},{1,5},{5... | collective-permute-start | bytes 1572872 | tf_op jit(solution)/shard_map/ppermute | solution.py:287
  27.3 7.8 %collective-permute-start.7 = (bf16[2,128,256]{2,1,0:T(8,128)(2,1)S(1)}, bf16[2,128,256]{2,1,0:T(8,128)(2,1)S(1)}, u32[]{:S(2)}, u32[]{:S(2)}) collective-permute-start(bf16[2,128,256]{2,1,0:T(8,128)(2,1)S(1)} %get-tuple-element.46), channel_id=1, source_target_pairs={{0,1},{1,0},{2,3},{3,2},{4,5},{5,4},{6,7},{7,6},{8,9},{9,8},{10,11... | collective-permute-start | bytes 393224 | tf_op jit(solution)/shard_map/ppermute | solution.py:287
  28.2 13.5 %collective-permute-start.8 = (bf16[2,128,256]{2,1,0:T(8,128)(2,1)S(1)}, bf16[2,128,256]{2,1,0:T(8,128)(2,1)S(1)}, u32[]{:S(2)}, u32[]{:S(2)}) collective-permute-start(bf16[2,128,256]{2,1,0:T(8,128)(2,1)S(1)} %get-tuple-element.47), channel_id=1, source_target_pairs={{0,2},{1,3},{2,0},{3,1},{4,6},{5,7},{6,4},{7,5},{8,10},{9,11},{10,... | collective-permute-start | bytes 393224 | tf_op jit(solution)/shard_map/ppermute | solution.py:287
  31.7 10.0 %collective-permute-start.9 = (bf16[2,128,256]{2,1,0:T(8,128)(2,1)S(1)}, bf16[2,128,256]{2,1,0:T(8,128)(2,1)S(1)}, u32[]{:S(2)}, u32[]{:S(2)}) collective-permute-start(bf16[2,128,256]{2,1,0:T(8,128)(2,1)S(1)} %get-tuple-element.48), channel_id=1, source_target_pairs={{0,3},{1,2},{2,1},{3,0},{4,7},{5,6},{6,5},{7,4},{8,11},{9,10},{10,... | collective-permute-start | bytes 393224 | tf_op jit(solution)/shard_map/ppermute | solution.py:287
  31.9 9.9 %collective-permute-start.11 = (bf16[256,256]{1,0:T(8,128)(2,1)S(1)}, bf16[256,256]{1,0:T(8,128)(2,1)S(1)}, u32[]{:S(2)}, u32[]{:S(2)}) collective-permute-start(bf16[256,256]{1,0:T(8,128)(2,1)S(1)} %get-tuple-element.54), channel_id=1, source_target_pairs={{0,8},{4,12},{8,0},{12,4},{16,24},{20,28},{24,16},{28,20},{1,9},{5... | collective-permute-start | bytes 393224 | tf_op jit(solution)/shard_map/ppermute | solution.py:287
  33.6 8.1 %collective-permute-start.12 = (bf16[256,256]{1,0:T(8,128)(2,1)S(1)}, bf16[256,256]{1,0:T(8,128)(2,1)S(1)}, u32[]{:S(2)}, u32[]{:S(2)}) collective-permute-start(bf16[256,256]{1,0:T(8,128)(2,1)S(1)} %get-tuple-element.55), channel_id=1, source_target_pairs={{0,16},{4,20},{8,24},{12,28},{16,0},{20,4},{24,8},{28,12},{1,17},{... | collective-permute-start | bytes 393224 | tf_op jit(solution)/shard_map/ppermute | solution.py:287
  35.1 6.6 %collective-permute-start.13 = (bf16[256,256]{1,0:T(8,128)(2,1)S(1)}, bf16[256,256]{1,0:T(8,128)(2,1)S(1)}, u32[]{:S(2)}, u32[]{:S(2)}) collective-permute-start(bf16[256,256]{1,0:T(8,128)(2,1)S(1)} %get-tuple-element.56), channel_id=1, source_target_pairs={{0,24},{4,28},{8,16},{12,20},{16,8},{20,12},{24,0},{28,4},{1,25},{... | collective-permute-start | bytes 393224 | tf_op jit(solution)/shard_map/ppermute | solution.py:287
